TPU v7x, 32 devices: a whole 2x2x4 slice. The times are simulated.
32 devices in a mesh: grp: 2 (over y), tile: 4 (over x, core), tp: 4 (over z).
Axes of the slice: x: 2, y: 2, z: 4, core: 2. Of those that a mesh axis runs over, the one named last changes fastest.
Arguments:
- atmos_state: bfloat16 [4096, 1536], P(('grp', 'tile')), may hold values from -6 to 6
- atmos_gain: float32 [1536], replicated, may hold values from 0.25 to 1.75
- w_first: bfloat16 [1536, 3072], P(('grp', 'tile'), 'tp'), may hold values from -0.15625 to 0.15625
- w_second: bfloat16 [1536, 3072], P(('grp', 'tile'), 'tp'), may hold values from -0.109375 to 0.109375
- flux_proj: bfloat16 [1536, 256], replicated, may hold values from -0.15625 to 0.15625
- remap_index: int32 [64, 3], P(('grp', 'tile', 'tp')), may hold values from 0 to 3
- remap_weight: bfloat16 [64, 3, 128, 128], P(('grp', 'tile', 'tp')), may hold values from -0.3125 to 0.3125
- ocean_state: bfloat16 [64, 128, 256], P(('grp', 'tile'), 'tp'), may hold values from -6 to 6
- depth_levels: int32 [64, 128], P(('grp', 'tile'), 'tp'), may hold values from 0 to 16
- conv_kernel: float32 [3, 3, 256], replicated, may hold values from -2 to 2
- ocean_gain: float32 [256], replicated, may hold values from 0.25 to 1.75
- ocean_w_in: bfloat16 [256, 1024], replicated, may hold values from -0.375 to 0.375
- ocean_w_out: bfloat16 [1024, 256], replicated, may hold values from -0.1875 to 0.1875
- ocean_cotangent: bfloat16 [64, 128, 256], P(('grp', 'tile'), 'tp'), may hold values from -6 to 6
Outputs:
- atmos_out: bfloat16 [4096, 1536], P(('grp', 'tile', 'tp'))
- ocean_out: bfloat16 [64, 128, 256], P(('grp', 'tile'), 'tp')
- weight_grads: float32 [2048, 256], P(('grp', 'tile', 'tp'))
Inputs may be any that keep to these rules, and one draw needn't show every extreme that they name: `remap_index`: index the 128-token blocks among the 512 atmosphere tokens of the same grp and tile indices as the ocean tile of that block. `depth_levels`: 0 marks land.
All inputs are finite; a program needn't handle non-finite values.
Results may differ from a plain program's by a relative error of at most 0.018.
Values may be sent and summed in bfloat16 or wider, within the bound.
No kernel may reach another device: no remote copies, remote signals or barrier semaphores. Data moves between devices by JAX's collectives and lax.ppermute only.
A program may use at most 64 MiB of HBM per device.

v0:
```python
import functools

import jax
import jax.numpy as jnp
from jax import lax
from jax.experimental import pallas as pl
from jax.experimental.pallas import tpu as pltpu
from jax.sharding import PartitionSpec as P


LEV = 16
ALL = ("grp", "tile", "tp")

epsilon = 1e-06
bf16 = jnp.bfloat16
f32 = jnp.float32
NT = (((1,), (1,)), ((), ()))
TN = (((0,), (0,)), ((), ()))
VMEM = pl.BlockSpec(memory_space=pltpu.VMEM)
SMEM = pl.BlockSpec(memory_space=pltpu.SMEM)


def send(value, target):
    groups = lax.axis_size("grp") * lax.axis_size("tile")
    depth = lax.axis_size("tp")
    pairs = []
    for group in range(groups):
        for z in range(depth):
            to = target(group, z)
            if to is not None:
                pairs.append((group * depth + z, to[0] * depth + to[1]))
    return lax.ppermute(value, ALL, pairs)


def flip(mask):
    return lambda group, z: (group ^ mask, z)


def shift_z(step):
    depth = lax.axis_size("tp")
    return lambda group, z: (group, (z + step) % depth)


def next_group(step):
    groups = lax.axis_size("grp") * lax.axis_size("tile")
    return lambda group, z: (group + step, z) if 0 <= group + step < groups else None


def gather_rows(block, order):
    groups = lax.axis_size("grp") * lax.axis_size("tile")
    rows = block.shape[0]
    if groups != 8 or rows % 64 != 0:
        full = lax.all_gather(block, ("grp", "tile"), axis=0, tiled=True)
        return [(None, full)]
    masks = {"x": 2, "y": 4}
    held = {0: block}
    for axis in "yx":
        held[masks[axis]] = send(block, flip(masks[axis]))
    leg = masks[order[0]]
    held[6] = send(held[leg], flip(6 - leg))
    for mask in (0, 2, 4, 6):
        held[mask + 1] = send(held[mask], flip(1))
    return sorted(held.items())


def call(body, outs, args, specs=None, scratch=(), flops=0, moved=0, tanhs=0):
    return pl.pallas_call(
        body,
        out_shape=[jax.ShapeDtypeStruct(*o) for o in outs],
        in_specs=specs or [VMEM] * len(args),
        out_specs=[VMEM] * len(outs),
        scratch_shapes=list(scratch),
        cost_estimate=pl.CostEstimate(
            flops=int(flops), bytes_accessed=int(moved), transcendentals=int(tanhs)
        ),
        compiler_params=pltpu.CompilerParams(vmem_limit_bytes=56 * 2**20),
    )(*args)


def gelu(x):
    inner = 0.7978845608028654 * (x + 0.044715 * (x * x * x))
    return x * (0.5 * (1.0 + jnp.tanh(inner)))


def gelu_both(x):
    root = 0.7978845608028654
    square = x * x
    t = jnp.tanh(root * (x + 0.044715 * (square * x)))
    half = 0.5 * (1.0 + t)
    slope = half + 0.5 * x * (1.0 - t * t) * (root * (1.0 + 3.0 * 0.044715 * square))
    return x * half, slope


def norm_body(depth, id_ref, x_ref, gain_ref, proj_ref, out_ref, own_ref):
    wide = x_ref[...].astype(f32)
    scale = lax.rsqrt(jnp.mean(wide * wide, axis=-1, keepdims=True) + epsilon)
    out_ref[...] = (wide * scale * gain_ref[...]).astype(bf16)
    own = own_ref.shape[0]
    mine = pl.ds(pl.multiple_of((id_ref[0] % depth) * own, own), own)
    own_ref[...] = jnp.dot(x_ref[mine, :], proj_ref[...], preferred_element_type=f32)


def edge_columns(flat, tile_x, tile_y):
    grid = flat.reshape(tile_x, tile_y, flat.shape[-1])
    return grid[:, 0], grid[:, tile_y - 1]


def payload_rows(sources, rows, tile_x, halves):
    at_index = sources * rows
    at_state = at_index + -(-sources // 16) * 16
    at_depth = at_state + 2 * halves * tile_x
    return at_index, at_state, at_depth, at_depth + 2 * tile_x


def prep_body(tile_x, tile_y, index_ref, weight_ref, state_ref, depth_ref, out_ref):
    sources, rows, inner = weight_ref.shape
    per_block = index_ref.shape[1]
    channels = state_ref.shape[1]
    halves = channels // inner
    at_index, at_state, at_depth, _ = payload_rows(sources, rows, tile_x, halves)
    for n in range(sources):
        out_ref[n * rows : (n + 1) * rows, :] = weight_ref[n]
    row = lax.broadcasted_iota(jnp.int32, (at_state - at_index, inner), 0)
    table = jnp.zeros(row.shape, jnp.int32)
    for n in range(sources):
        table = jnp.where(row == n, index_ref[n // per_block, n % per_block], table)
    out_ref[at_index:at_state, :] = table.astype(f32).astype(bf16)
    first, last = edge_columns(state_ref[...].astype(f32), tile_x, tile_y)
    edges = [e[:, h * inner : (h + 1) * inner] for e in (last, first) for h in range(halves)]
    out_ref[at_state:at_depth, :] = jnp.concatenate(edges, axis=0).astype(bf16)
    deep = depth_ref[...].astype(f32)
    edges = [
        jnp.broadcast_to(deep[:, at : at + 1], (tile_x, inner)) for at in (tile_y - 1, 0)
    ]
    out_ref[at_depth:, :] = jnp.concatenate(edges, axis=0).astype(bf16)


def build_matrix(per_block, sources, rows, at_index, load_ref, out_ref):
    inner = load_ref.shape[1]
    count = out_ref.shape[1] // inner
    for b in range(sources // per_block):
        taken = range(b * per_block, (b + 1) * per_block)
        values = [load_ref[n * rows : (n + 1) * rows, :].astype(f32) for n in taken]
        picks = [load_ref[at_index + n : at_index + n + 1, :].astype(f32) for n in taken]
        for j in range(count):
            total = jnp.zeros((rows, inner), f32)
            for value, pick in zip(values, picks):
                total = total + jnp.where(pick == float(j), 1.0, 0.0) * value
            out_ref[b * rows : (b + 1) * rows, j * inner : (j + 1) * inner] = total.astype(bf16)


def place_rows(me, pieces, refs, rows, full_ref):
    for mask, ref in zip(pieces, refs):
        if mask is None:
            full_ref[...] = ref[...]
        else:
            full_ref[pl.ds(pl.multiple_of((me ^ mask) * rows, 64), rows), :] = ref[...]


def add_product(me, x_ref, pieces, rows, full_ref, at, step, total):
    if pieces[0] is None:
        part = jnp.dot(x_ref[...], full_ref[:, at : at + step], preferred_element_type=f32)
        return part if total is None else total + part
    for n, pair in enumerate(sorted({mask // 2 for mask in pieces})):
        start = pl.multiple_of(((me // 2) ^ pair) * (2 * rows), 128)
        part = jnp.dot(
            x_ref[:, pl.ds(start, 2 * rows)],
            full_ref[n * 2 * rows : (n + 1) * 2 * rows, at : at + step],
            preferred_element_type=f32,
        )
        total = part if total is None else total + part
    return total


def place_pairs(me, pieces, refs, rows, full_ref):
    if pieces[0] is None:
        full_ref[...] = refs[0][...]
        return
    pairs = sorted({mask // 2 for mask in pieces})
    for mask, ref in zip(pieces, refs):
        start = pairs.index(mask // 2) * 2 * rows + ((me % 2) ^ (mask % 2)) * rows
        full_ref[pl.ds(pl.multiple_of(start, 64), rows), :] = ref[...]


def early_body(pieces, rows, depth, id_ref, x_ref, *refs):
    blocks, out_ref, full = refs[:-2], refs[-2], refs[-1]
    me = id_ref[0] // depth
    place_pairs(me, pieces, blocks, rows, full)
    width = out_ref.shape[1]
    step = 256 if width % 256 == 0 else width
    for at in range(0, width, step):
        out_ref[:, at : at + step] = add_product(me, x_ref, pieces, rows, full, at, step, None)


def first_body(
    pieces, rows, depth, tile_x, tile_y, remap, early, id_ref, x_ref, own_ref, both_ref, *refs
):
    mats, refs = refs[:depth], refs[depth:]
    sums, refs = refs[: int(early)], refs[int(early) :]
    blocks, refs = refs[: len(pieces)], refs[len(pieces) :]
    hid_ref, moved, refs = refs[0], refs[1 : depth + 1], refs[depth + 1 :]
    full, flux, dense = refs[0], refs[1], refs[2:]
    me = id_ref[0] // depth
    z = id_ref[0] % depth
    place_pairs(me, pieces, blocks, rows, full)
    for k in range(depth):
        build_matrix(*remap, mats[k], dense[k])
    width = hid_ref.shape[1]
    step = 256 if width % 256 == 0 else width
    total = jnp.zeros(flux.shape, f32)
    for at in range(0, width, step):
        pre = sums[0][:, at : at + step] if early else None
        pre = add_product(me, x_ref, pieces, rows, full, at, step, pre)
        hidden = gelu(pre).astype(bf16)
        hid_ref[:, at : at + step] = hidden
        total = total + lax.dot_general(
            hidden, both_ref[:, at : at + step], NT, preferred_element_type=f32
        )
    flux[...] = total
    own = own_ref.shape[0]
    mine = pl.ds(pl.multiple_of(z * own, own), own)
    flux[mine, :] += own_ref[...]
    low = flux[...].astype(bf16)
    cells = tile_x * tile_y
    results = [jnp.dot(m[...], low, preferred_element_type=f32) for m in dense]
    edges = [edge_columns(r, tile_x, tile_y) for r in results]
    for k in range(depth):
        moved[k][:cells, :] = results[k].astype(bf16)
        sides = [edges[(k + 1) % depth][1], edges[(k - 1) % depth][0]]
        moved[k][cells:, :] = jnp.concatenate(sides, axis=0).astype(bf16)


def both_body(pieces, rows, depth, id_ref, proj_ref, *refs):
    blocks, out_ref, full = refs[:-2], refs[-2], refs[-1]
    place_rows(id_ref[0] // depth, pieces, blocks, rows, full)
    out_ref[...] = lax.dot_general(
        proj_ref[...], full[...], TN, preferred_element_type=f32
    ).astype(bf16)


def second_body(pieces, rows, depth, id_ref, hid_ref, *refs):
    blocks, refs = refs[: len(pieces)], refs[len(pieces) :]
    parts, full, sums = refs[:depth], refs[depth], refs[depth + 1]
    z = id_ref[0] % depth
    place_rows(id_ref[0] // depth, pieces, blocks, rows, full)
    tokens, width = sums.shape
    own = tokens // depth
    step = 256 if width % 256 == 0 else width
    for at in range(0, width, step):
        sums[:, at : at + step] = lax.dot_general(
            hid_ref[...], full[at : at + step, :], NT, preferred_element_type=f32
        ).astype(bf16)
    for k in range(depth):
        start = pl.multiple_of(((z - k + depth) % depth) * own, own)
        parts[k][...] = sums[pl.ds(start, own), :]


def field_body(depth, tile_x, tile_y, rows_at, id_ref, state_ref, wet_ref, west_ref, east_ref, *refs):
    parts, refs = refs[:depth], refs[depth:]
    field_ref, side_ref, first_ref, last_ref = refs
    z = id_ref[0] % depth
    cells = tile_x * tile_y
    channels = state_ref.shape[1]
    total = parts[0][...].astype(f32)
    for p in parts[1:]:
        total = total + p[...].astype(f32)
    total = total.astype(bf16).astype(f32)
    field = ((state_ref[...].astype(f32) + total[:cells]) * wet_ref[...].astype(f32)).astype(bf16)
    field_ref[...] = field
    _, at_state, at_depth, _ = rows_at
    inner = west_ref.shape[1]
    halves = channels // inner
    level = lax.broadcasted_iota(jnp.int32, (tile_x, channels), 1) // (channels // LEV)
    sides = []
    for which, ref, inside in ((0, west_ref, z > 0), (1, east_ref, z < depth - 1)):
        at = at_state + which * halves * tile_x
        state = jnp.concatenate(
            [ref[at + h * tile_x : at + (h + 1) * tile_x, :].astype(f32) for h in range(halves)],
            axis=1,
        )
        at = at_depth + which * tile_x
        deep = jnp.concatenate([ref[at : at + tile_x, :].astype(f32)] * halves, axis=1)
        deep = deep * jnp.where(inside, 1.0, 0.0).astype(f32)
        at = cells + which * tile_x
        sides.append(jnp.where(level.astype(f32) < deep, state + total[at : at + tile_x], 0.0))
    side_w, side_e = sides
    side_ref[...] = jnp.concatenate([side_w, side_e], axis=0).astype(bf16)
    spare = jnp.zeros((first_ref.shape[0] - tile_y - 2, channels), f32)
    wide = field.astype(f32)
    for ref, row in ((first_ref, 0), (last_ref, tile_x - 1)):
        ref[...] = jnp.concatenate(
            [
                wide[row * tile_y : (row + 1) * tile_y],
                side_w[row : row + 1],
                side_e[row : row + 1],
                spare,
            ],
            axis=0,
        ).astype(bf16)


def ocean_body(
    depth, tile_x, tile_y, split, id_ref, field_ref, side_ref, top_ref, low_ref, wet_ref, dout_ref,
    kern_ref, gain_ref, win_ref, wout_ref, *refs
):
    out_ref, refs = refs[0], refs[1:]
    pad = refs[-1]
    cells, channels = field_ref.shape
    core = (id_ref[0] // depth) % 2
    at = 8
    pad[1 : tile_x + 1, at : at + tile_y, :] = (
        field_ref[...].astype(f32).reshape(tile_x, tile_y, channels)
    )
    side = side_ref[...].astype(f32)
    pad[1 : tile_x + 1, at - 1, :] = side[:tile_x]
    pad[1 : tile_x + 1, at + tile_y, :] = side[tile_x:]
    for row, ref in ((0, top_ref), (tile_x + 1, low_ref)):
        line = ref[...].astype(f32)
        pad[row, at : at + tile_y, :] = line[:tile_y]
        pad[row, at - 1 : at, :] = line[tile_y : tile_y + 1]
        pad[row, at + tile_y : at + tile_y + 1, :] = line[tile_y + 1 : tile_y + 2]
    conv = jnp.zeros((tile_x, tile_y, channels), f32)
    for i in range(3):
        for j in range(3):
            tap = kern_ref[i, j].reshape(1, 1, channels)
            conv = conv + tap * pad[i : i + tile_x, at - 1 + j : at - 1 + j + tile_y, :]
    conv = conv.reshape(cells, channels)
    centred = conv - jnp.mean(conv, axis=-1, keepdims=True)
    variance = jnp.mean(centred * centred, axis=-1, keepdims=True)
    normed = (centred * lax.rsqrt(variance + epsilon) * gain_ref[...]).astype(bf16)
    wet = wet_ref[...].astype(f32)
    dout = dout_ref[...]
    hid = win_ref.shape[1]
    step = hid // 4
    total = jnp.zeros((cells, channels), f32)
    for c in range(4):
        span = slice(c * step, (c + 1) * step)
        pre = jnp.dot(normed, win_ref[:, span], preferred_element_type=f32)
        value, slope = gelu_both(pre)
        act = value.astype(bf16)
        total = total + jnp.dot(act, wout_ref[span, :], preferred_element_type=f32)
        dact = lax.dot_general(dout, wout_ref[span, :], NT, preferred_element_type=f32)
        dpre = (dact * slope).astype(bf16)
        grads = (
            lax.dot_general(dpre, normed, TN, preferred_element_type=f32),
            lax.dot_general(act, dout, TN, preferred_element_type=f32),
        )
        for which, grad in enumerate(grads):
            if not split:
                refs[0][which * hid + c * step : which * hid + (c + 1) * step, :] = grad
                continue
            spot = 2 * which + c // 2

            @pl.when(core == c % 2)
            def _():
                refs[0][spot] = grad

            @pl.when(core != c % 2)
            def _():
                refs[1][spot] = grad.astype(bf16)

    out_ref[...] = ((field_ref[...].astype(f32) + total) * wet).astype(bf16)


def step(
    atmos_state,
    atmos_gain,
    w_first,
    w_second,
    flux_proj,
    remap_index,
    remap_weight,
    ocean_state,
    depth_levels,
    conv_kernel,
    ocean_gain,
    ocean_w_in,
    ocean_w_out,
    ocean_cotangent,
):
    depth = lax.axis_size("tp")
    groups = lax.axis_size("grp") * lax.axis_size("tile")
    me = lax.axis_index(ALL).astype(jnp.int32).reshape(1)
    tokens, model = atmos_state.shape
    own = tokens // depth
    channels = flux_proj.shape[1]
    share = w_first.shape[1]
    tile_x, tile_y, _ = ocean_state.shape
    cells = tile_x * tile_y
    hid = ocean_w_in.shape[1]
    mb = 2**20

    second = gather_rows(w_second, "yx")
    first = gather_rows(w_first, "xy")
    own_rows = lax.dynamic_slice_in_dim(atmos_state, (me[0] % depth) * own, own, 0)

    levels = jnp.arange(channels, dtype=jnp.int32) // (channels // LEV)
    wet = (levels[None, :] < depth_levels.reshape(cells)[:, None]).astype(bf16)
    state = ocean_state.reshape(cells, channels)
    blocks, per_block, block_rows, inner = remap_weight.shape
    sources = blocks * per_block
    rows_at = payload_rows(sources, block_rows, tile_x, channels // inner)
    (payload,) = call(
        functools.partial(prep_body, tile_x, tile_y),
        [((rows_at[3], inner), bf16)],
        (remap_index, remap_weight.reshape(sources, block_rows, inner), state, depth_levels),
        specs=[SMEM, VMEM, VMEM, VMEM],
        moved=mb,
    )
    payloads = [payload] + [send(payload, shift_z(k)) for k in range(1, depth)]
    normed, own_flux = call(
        functools.partial(norm_body, depth),
        [((tokens, model), bf16), ((own, channels), f32)],
        (me, atmos_state, atmos_gain.reshape(1, model), flux_proj),
        specs=[SMEM] + [VMEM] * 3,
        moved=4 * mb,
    )

    rows = w_second.shape[0]
    second_at = [p[0] for p in second]
    second = [p[1] for p in second]
    (both,) = call(
        functools.partial(both_body, second_at, rows, depth),
        [((channels, share), bf16)],
        (me, flux_proj, *second),
        specs=[SMEM] + [VMEM] * (1 + len(second)),
        scratch=[pltpu.VMEM((model, share), bf16)],
        flops=2 * model * share * channels,
        moved=3 * mb,
    )

    rows = w_first.shape[0]
    early = first[0][0] is not None
    sums = []
    if early:
        soon = [p for p in first if p[0] < 6]
        first = [p for p in first if p[0] >= 6]
        sums = call(
            functools.partial(early_body, [p[0] for p in soon], rows, depth),
            [((tokens, share), f32)],
            (me, normed, *[p[1] for p in soon]),
            specs=[SMEM] + [VMEM] * (1 + len(soon)),
            scratch=[pltpu.VMEM((6 * rows, share), bf16)],
            flops=2 * tokens * share * 6 * rows,
            moved=5 * mb,
        )
    outs = call(
        functools.partial(
            first_body,
            [p[0] for p in first],
            rows,
            depth,
            tile_x,
            tile_y,
            (per_block, sources, block_rows, rows_at[0]),
            early,
        ),
        [((tokens, share), bf16)] + [((cells + 2 * tile_x, channels), bf16)] * depth,
        (me, normed, own_flux, both, *payloads, *sums, *[p[1] for p in first]),
        specs=[SMEM] + [VMEM] * (3 + depth + len(sums) + len(first)),
        scratch=[
            pltpu.VMEM((2 * rows if early else model, share), bf16),
            pltpu.VMEM((tokens, channels), f32),
        ]
        + [pltpu.VMEM((cells, tokens), bf16)] * depth,
        flops=2 * tokens * share * (2 * rows + channels),
        moved=5 * mb,
        tanhs=tokens * share,
    )
    hidden, moved = outs[0], outs[1:]
    moved = [moved[0]] + [send(moved[k], shift_z(-k)) for k in range(1, depth)]

    rows = w_second.shape[0]
    parts = call(
        functools.partial(second_body, second_at, rows, depth),
        [((own, model), bf16)] * depth,
        (me, hidden, *second),
        specs=[SMEM] + [VMEM] * (1 + len(second)),
        scratch=[pltpu.VMEM((model, share), bf16), pltpu.VMEM((tokens, model), bf16)],
        flops=2 * tokens * model * share,
        moved=6 * mb,
    )
    parts = [parts[0]] + [send(parts[k], shift_z(-k)) for k in range(1, depth)]

    dout = (ocean_cotangent.reshape(cells, channels).astype(f32) * wet.astype(f32)).astype(bf16)

    line = -(-(tile_y + 2) // 16) * 16
    field, side, row_first, row_last = call(
        functools.partial(field_body, depth, tile_x, tile_y, rows_at),
        [((cells, channels), bf16), ((2 * tile_x, channels), bf16)]
        + [((line, channels), bf16)] * 2,
        (me, state, wet, payloads[1], payloads[depth - 1], *moved),
        specs=[SMEM] + [VMEM] * (4 + depth),
        moved=mb,
    )
    top = send(row_last, next_group(1))
    low = send(row_first, next_group(-1))

    split = groups == 8
    grad_outs = [((2 * hid, channels), f32)]
    if split:
        grad_outs = [((4, hid // 4, channels), f32), ((4, hid // 4, channels), bf16)]
    outs = call(
        functools.partial(ocean_body, depth, tile_x, tile_y, split),
        [((cells, channels), bf16)] + grad_outs,
        (
            me,
            field,
            side,
            top,
            low,
            wet,
            dout,
            conv_kernel,
            ocean_gain.reshape(1, channels),
            ocean_w_in,
            ocean_w_out,
        ),
        specs=[SMEM] + [VMEM] * 10,
        scratch=[pltpu.VMEM((tile_x + 2, tile_y + 16, channels), f32)],
        flops=10 * cells * channels * hid,
        moved=5 * mb,
        tanhs=cells * hid,
    )
    ocean_out = outs[0].reshape(tile_x, tile_y, channels)
    if split:
        keep, give = outs[1:]
        place = me[0] // depth // 2

        def quarter(mask):
            return lax.dynamic_index_in_dim(terms, place ^ mask, 0, keepdims=False)

        terms = keep + send(give, flip(1)).astype(f32)
        arrived = [send(quarter(m).astype(bf16), flip(2 * m)) for m in (1, 2, 3)]
        total = quarter(0)
        for piece in arrived:
            total = total + piece.astype(f32)
        total = total.reshape(depth, -1, channels)
        z = me[0] % depth

        def slab(k):
            return lax.dynamic_index_in_dim(total, (z - k) % depth, 0, keepdims=False)

        arrived = [send(slab(k).astype(bf16), shift_z(-k)) for k in range(1, depth)]
        weight_grads = slab(0)
        for piece in arrived:
            weight_grads = weight_grads + piece.astype(f32)
    else:
        weight_grads = lax.psum_scatter(outs[1], ALL, scatter_dimension=0, tiled=True)

    total = own_rows.astype(f32)
    for part in parts:
        total = total + part.astype(f32)
    atmos_out = total.astype(bf16)
    return (atmos_out, ocean_out, weight_grads)


def solution(mesh):
    in_specs = (
        P(("grp", "tile"), None),
        P(),
        P(("grp", "tile"), "tp"),
        P(("grp", "tile"), "tp"),
        P(),
        P(ALL, None),
        P(ALL, None, None, None),
        P(("grp", "tile"), "tp", None),
        P(("grp", "tile"), "tp"),
        P(),
        P(),
        P(),
        P(),
        P(("grp", "tile"), "tp", None),
    )
    out_specs = (
        P(ALL, None),
        P(("grp", "tile"), "tp", None),
        P(ALL, None),
    )
    return jax.shard_map(step, mesh=mesh, in_specs=in_specs, out_specs=out_specs, check_vma=False)
```

profile of v0, /device:TPU:0, one launch (start us, length us, event | category | flops | bytes accessed | tf_op | source)
XLA Modules:
  0.0 148.4 jit_solution(6713431175187341385)
XLA Ops:
  0.6 3.0 %collective-permute-start.11 = (bf16[192,768]{1,0:T(8,128)(2,1)}, bf16[192,768]{1,0:T(8,128)(2,1)S(1)}, u32[]{:S(2)}, u32[]{:S(2)}) collective-permute-start(bf16[192,768]{1,0:T(8,128)(2,1)} %refs_0_.4), channel_id=1, source_target_pairs={{0,8},{1,9},{2,10},{3,11},{4,12},{5,13},{6,14},{7,15},{8,0},{9,1},... | collective-permute-start | bytes 884744 | tf_op jit(solution)/shard_map/ppermute | solution.py:32
  3.7 1.5 %collective-permute-start.13 = (bf16[192,768]{1,0:T(8,128)(2,1)}, bf16[192,768]{1,0:T(8,128)(2,1)S(1)}, u32[]{:S(2)}, u32[]{:S(2)}) collective-permute-start(bf16[192,768]{1,0:T(8,128)(2,1)} %refs_0_.4), channel_id=1, source_target_pairs={{0,16},{1,17},{2,18},{3,19},{4,20},{5,21},{6,22},{7,23},{8,24},{9,... | collective-permute-start | bytes 884744 | tf_op jit(solution)/shard_map/ppermute | solution.py:32
  5.8 6.0 %collective-permute-done.11.refs_2_ = bf16[192,768]{1,0:T(8,128)(2,1)S(1)} collective-permute-done((bf16[192,768]{1,0:T(8,128)(2,1)}, bf16[192,768]{1,0:T(8,128)(2,1)S(1)}, u32[]{:S(2)}, u32[]{:S(2)}) %collective-permute-start.11) | collective-permute-done | bytes 294944 | tf_op jit(solution)/shard_map/ppermute | solution.py:32
  11.7 2.0 %collective-permute-done.13.refs_4_ = bf16[192,768]{1,0:T(8,128)(2,1)S(1)} collective-permute-done((bf16[192,768]{1,0:T(8,128)(2,1)}, bf16[192,768]{1,0:T(8,128)(2,1)S(1)}, u32[]{:S(2)}, u32[]{:S(2)}) %collective-permute-start.13) | collective-permute-done | bytes 294944 | tf_op jit(solution)/shard_map/ppermute | solution.py:32
  13.8 4.9 %collective-permute-done.3.refs_4_ = bf16[192,768]{1,0:T(8,128)(2,1)S(1)} collective-permute-done((bf16[192,768]{1,0:T(8,128)(2,1)}, bf16[192,768]{1,0:T(8,128)(2,1)S(1)}, u32[]{:S(2)}, u32[]{:S(2)}) %collective-permute-start.3) | collective-permute-done | bytes 294944 | tf_op jit(solution)/shard_map/ppermute | solution.py:32
  19.1 1.7 %collective-permute-start.15 = (bf16[192,768]{1,0:T(8,128)(2,1)S(1)}, bf16[192,768]{1,0:T(8,128)(2,1)}, u32[]{:S(2)}, u32[]{:S(2)}) collective-permute-start(bf16[192,768]{1,0:T(8,128)(2,1)S(1)} %collective-permute-done.11.refs_2_), channel_id=1, source_target_pairs={{0,16},{1,17},{2,18},{3,19},{4,20},{5,21},{6,22},{7,23},{8,24},{9,... | collective-permute-start | bytes 884744 | tf_op jit(solution)/shard_map/ppermute | solution.py:32
  21.3 4.9 %collective-permute-done.5.refs_6_ = bf16[192,768]{1,0:T(8,128)(2,1)S(1)} collective-permute-done((bf16[192,768]{1,0:T(8,128)(2,1)S(1)}, bf16[192,768]{1,0:T(8,128)(2,1)S(1)}, u32[]{:S(2)}, u32[]{:S(2)}) %collective-permute-start.5) | collective-permute-done | bytes 294944 | tf_op jit(solution)/shard_map/ppermute | solution.py:32
  28.9 1.7 %shard_map.159.refs_0_ = bf16[832,128]{1,0:T(8,128)(2,1)} custom-call(s32[2,3]{1,0:T(2,128)} %index_ref.1, bf16[6,128,128]{2,1,0:T(8,128)(2,1)} %bitcast.37, bf16[256,256]{1,0:T(8,128)(2,1)} %bitcast.35, s32[8,32]{1,0:T(8,128)} %depth_ref.1), custom_call_target="tpu_custom_call" | custom-call | bytes 1048576 | tf_op jit(solution)/shard_map/pallas_call | solution.py:67
  30.6 3.6 %shard_map.157 = (bf16[512,1536]{1,0:T(8,128)(2,1)}, f32[128,256]{1,0:T(8,128)}) custom-call(s32[1]{0:T(128)} %bitcast.id_ref, bf16[512,1536]{1,0:T(8,128)(2,1)} %x_ref.1, f32[1,1536]{1,0:T(1,128)} %reshape.51.gain_ref, bf16[1536,256]{1,0:T(8,128)(2,1)} %proj_ref.3), custom_call_target="tpu_custom_call" | custom-call | bytes 4194304 | tf_op jit(solution)/shard_map/pallas_call | solution.py:67
  34.2 1.6 %collective-permute-start.7 = (bf16[832,128]{1,0:T(8,128)(2,1)S(1)}, bf16[832,128]{1,0:T(8,128)(2,1)S(1)}, u32[]{:S(2)}, u32[]{:S(2)}) collective-permute-start(bf16[832,128]{1,0:T(8,128)(2,1)S(1)} %copy-done), channel_id=1, source_target_pairs={{0,1},{1,2},{2,3},{3,0},{4,5},{5,6},{6,7},{7,4},{8,9},{9,10},{10,1... | collective-permute-start | bytes 638984 | tf_op jit(solution)/shard_map/ppermute | solution.py:32
  35.8 2.2 %collective-permute-start.9 = (bf16[832,128]{1,0:T(8,128)(2,1)S(1)}, bf16[832,128]{1,0:T(8,128)(2,1)S(1)}, u32[]{:S(2)}, u32[]{:S(2)}) collective-permute-start(bf16[832,128]{1,0:T(8,128)(2,1)S(1)} %copy-done), channel_id=1, source_target_pairs={{0,3},{1,0},{2,1},{3,2},{4,7},{5,4},{6,5},{7,6},{8,11},{9,8},{10,9... | collective-permute-start | bytes 638984 | tf_op jit(solution)/shard_map/ppermute | solution.py:32
  38.9 4.6 %shard_map.160.refs_4_ = f32[512,768]{1,0:T(8,128)} custom-call(s32[1]{0:T(128)} %bitcast.id_ref, bf16[512,1536]{1,0:T(8,128)(2,1)} %get-tuple-element.21.x_ref, bf16[192,768]{1,0:T(8,128)(2,1)} %refs_0_.4, bf16[192,768]{1,0:T(8,128)(2,1)} %copy-done.5, bf16[192,768]{1,0:T(8,128)(2,1)} %copy-done.3, bf16[192,768]{1,0:T(8,128)(2,1)} %copy-done.6, ...), custom_call_target="tpu_custom_call" | custom-call | flops 905969664 | bytes 5242880 | tf_op jit(solution)/shard_map/pallas_call | solution.py:67
  43.5 3.5 %shard_map.158.both_ref = bf16[256,768]{1,0:T(8,128)(2,1)} custom-call(s32[1]{0:T(128)} %bitcast.id_ref, bf16[1536,256]{1,0:T(8,128)(2,1)} %proj_ref.3, bf16[192,768]{1,0:T(8,128)(2,1)} %refs_0_.5, bf16[192,768]{1,0:T(8,128)(2,1)} %copy-done.10, bf16[192,768]{1,0:T(8,128)(2,1)} %copy-done.9, bf16[192,768]{1,0:T(8,128)(2,1)} %copy-done.13, ...), custom_call_target="tpu_custom_call" | custom-call | flops 603979776 | bytes 3145728 | tf_op jit(solution)/shard_map/pallas_call | solution.py:67
  47.6 9.7 %collective-permute-done.8.refs_2_ = bf16[832,128]{1,0:T(8,128)(2,1)S(1)} collective-permute-done((bf16[832,128]{1,0:T(8,128)(2,1)S(1)}, bf16[832,128]{1,0:T(8,128)(2,1)S(1)}, u32[]{:S(2)}, u32[]{:S(2)}) %collective-permute-start.8) | collective-permute-done | bytes 213024 | tf_op jit(solution)/shard_map/ppermute | solution.py:32
  58.1 5.3 %shard_map.161 = (bf16[512,768]{1,0:T(8,128)(2,1)}, bf16[272,256]{1,0:T(8,128)(2,1)}, bf16[272,256]{1,0:T(8,128)(2,1)}, bf16[272,256]{1,0:T(8,128)(2,1)}, bf16[272,256]{1,0:T(8,128)(2,1)}) custom-call(s32[1]{0:T(128)} %bitcast.id_ref, bf16[512,1536]{1,0:T(8,128)(2,1)} %get-tuple-element.21.x_ref, f32[128,256]{1,0:T(8,128)} %get-tuple-element.22.own_ref, ...), custom_call_target="tpu_custom_call" | custom-call | flops 503316480 | bytes 5242880 | tf_op jit(solution)/shard_map/pallas_call | solution.py:67
  63.3 1.6 %collective-permute-start.20 = (bf16[272,256]{1,0:T(8,128)(2,1)}, bf16[272,256]{1,0:T(8,128)(2,1)S(1)}, u32[]{:S(2)}, u32[]{:S(2)}) collective-permute-start(bf16[272,256]{1,0:T(8,128)(2,1)} %get-tuple-element.29), channel_id=1, source_target_pairs={{0,3},{1,0},{2,1},{3,2},{4,7},{5,4},{6,5},{7,6},{8,11},{9,8},{10,9... | collective-permute-start | bytes 417800 | tf_op jit(solution)/shard_map/ppermute | solution.py:32
  66.2 3.6 %collective-permute-done.20.refs_1_ = bf16[272,256]{1,0:T(8,128)(2,1)S(1)} collective-permute-done((bf16[272,256]{1,0:T(8,128)(2,1)}, bf16[272,256]{1,0:T(8,128)(2,1)S(1)}, u32[]{:S(2)}, u32[]{:S(2)}) %collective-permute-start.20) | collective-permute-done | bytes 139296 | tf_op jit(solution)/shard_map/ppermute | solution.py:32
  69.9 6.9 %collective-permute-done.21.refs_2_ = bf16[272,256]{1,0:T(8,128)(2,1)S(1)} collective-permute-done((bf16[272,256]{1,0:T(8,128)(2,1)}, bf16[272,256]{1,0:T(8,128)(2,1)S(1)}, u32[]{:S(2)}, u32[]{:S(2)}) %collective-permute-start.21) | collective-permute-done | bytes 139296 | tf_op jit(solution)/shard_map/ppermute | solution.py:32
  77.5 2.2 %shard_map.163 = (bf16[256,256]{1,0:T(8,128)(2,1)}, bf16[16,256]{1,0:T(8,128)(2,1)}, bf16[48,256]{1,0:T(8,128)(2,1)}, bf16[48,256]{1,0:T(8,128)(2,1)}) custom-call(s32[1]{0:T(128)} %bitcast.id_ref, bf16[256,256]{1,0:T(8,128)(2,1)} %bitcast.36, bf16[256,256]{1,0:T(8,128)(2,1)} %compare_convert_fusion.wet_ref, bf16[832,128]{1,0:T(8,128)(2,1)} %copy-done.1, ...), custom_call_target="tpu_custom_call" | custom-call | bytes 1048576 | tf_op jit(solution)/shard_map/pallas_call | solution.py:67
  83.0 3.1 %collective-permute-done.24.low_ref = bf16[48,256]{1,0:T(8,128)(2,1)S(1)} collective-permute-done((bf16[48,256]{1,0:T(8,128)(2,1)}, bf16[48,256]{1,0:T(8,128)(2,1)S(1)}, u32[]{:S(2)}, u32[]{:S(2)}) %collective-permute-start.24) | collective-permute-done | bytes 24608 | tf_op jit(solution)/shard_map/ppermute | solution.py:32
  86.7 5.5 %shard_map.164 = (bf16[256,256]{1,0:T(8,128)(2,1)}, f32[4,256,256]{2,1,0:T(8,128)}, bf16[4,256,256]{2,1,0:T(8,128)(2,1)}) custom-call(s32[1]{0:T(128)} %bitcast.id_ref, bf16[256,256]{1,0:T(8,128)(2,1)} %get-tuple-element.32.field_ref, bf16[16,256]{1,0:T(8,128)(2,1)} %get-tuple-element.33.side_ref, bf16[48,256]{1,0:T(8,128)(2,1)} %copy-done.19, ...), custom_call_target="tpu_custom_call" | custom-call | flops 671088640 | bytes 5242880 | tf_op jit(solution)/shard_map/pallas_call | solution.py:67
  92.1 2.6 %collective-permute-start.25 = (bf16[4,256,256]{2,1,0:T(8,128)(2,1)}, bf16[4,256,256]{2,1,0:T(8,128)(2,1)S(1)}, u32[]{:S(2)}, u32[]{:S(2)}) collective-permute-start(bf16[4,256,256]{2,1,0:T(8,128)(2,1)} %get-tuple-element.38), channel_id=1, source_target_pairs={{0,4},{1,5},{2,6},{3,7},{4,0},{5,1},{6,2},{7,3},{8,12},{9,13},{10,... | collective-permute-start | bytes 1572872 | tf_op jit(solution)/shard_map/ppermute | solution.py:32
  94.7 1.7 %collective-permute-done.25 = bf16[4,256,256]{2,1,0:T(8,128)(2,1)S(1)} collective-permute-done((bf16[4,256,256]{2,1,0:T(8,128)(2,1)}, bf16[4,256,256]{2,1,0:T(8,128)(2,1)S(1)}, u32[]{:S(2)}, u32[]{:S(2)}) %collective-permute-start.25) | collective-permute-done | bytes 524320 | tf_op jit(solution)/shard_map/ppermute | solution.py:32
  97.9 2.3 %collective-permute-start.26 = (bf16[256,256]{1,0:T(8,128)(2,1)S(1)}, bf16[256,256]{1,0:T(8,128)(2,1)S(1)}, u32[]{:S(2)}, u32[]{:S(2)}) collective-permute-start(bf16[256,256]{1,0:T(8,128)(2,1)S(1)} %get-tuple-element.39), channel_id=1, source_target_pairs={{0,8},{1,9},{2,10},{3,11},{4,12},{5,13},{6,14},{7,15},{8,0},{9,1},... | collective-permute-start | bytes 393224 | tf_op jit(solution)/shard_map/ppermute | solution.py:32
  100.2 1.5 %collective-permute-start.28 = (bf16[256,256]{1,0:T(8,128)(2,1)S(1)}, bf16[256,256]{1,0:T(8,128)(2,1)S(1)}, u32[]{:S(2)}, u32[]{:S(2)}) collective-permute-start(bf16[256,256]{1,0:T(8,128)(2,1)S(1)} %get-tuple-element.40), channel_id=1, source_target_pairs={{0,24},{1,25},{2,26},{3,27},{4,28},{5,29},{6,30},{7,31},{8,16},{9,... | collective-permute-start | bytes 393224 | tf_op jit(solution)/shard_map/ppermute | solution.py:32
  101.7 4.6 %shard_map.162 = (bf16[128,1536]{1,0:T(8,128)(2,1)}, bf16[128,1536]{1,0:T(8,128)(2,1)}, bf16[128,1536]{1,0:T(8,128)(2,1)}, bf16[128,1536]{1,0:T(8,128)(2,1)}) custom-call(s32[1]{0:T(128)} %bitcast.id_ref, bf16[512,768]{1,0:T(8,128)(2,1)} %get-tuple-element.23.hid_ref, bf16[192,768]{1,0:T(8,128)(2,1)} %refs_0_.5, bf16[192,768]{1,0:T(8,128)(2,1)} %copy-done.10, ...), custom_call_target="tpu_custom_call" | custom-call | flops 1207959552 | bytes 6291456 | tf_op jit(solution)/shard_map/pallas_call | solution.py:67
  109.0 2.0 %collective-permute-start.19 = (bf16[128,1536]{1,0:T(8,128)(2,1)}, bf16[128,1536]{1,0:T(8,128)(2,1)S(1)}, u32[]{:S(2)}, u32[]{:S(2)}) collective-permute-start(bf16[128,1536]{1,0:T(8,128)(2,1)} %get-tuple-element.27), channel_id=1, source_target_pairs={{0,1},{1,2},{2,3},{3,0},{4,5},{5,6},{6,7},{7,4},{8,9},{9,10},{10,1... | collective-permute-start | bytes 1179656 | tf_op jit(solution)/shard_map/ppermute | solution.py:32
  111.1 1.9 %collective-permute-start.29 = (bf16[64,256]{1,0:T(8,128)(2,1)S(1)}, bf16[64,256]{1,0:T(8,128)(2,1)S(1)}, u32[]{:S(2)}, u32[]{:S(2)}) collective-permute-start(bf16[64,256]{1,0:T(8,128)(2,1)S(1)} %get-tuple-element.42), channel_id=1, source_target_pairs={{0,3},{1,0},{2,1},{3,2},{4,7},{5,4},{6,5},{7,6},{8,11},{9,8},{10,9... | collective-permute-start | bytes 98312 | tf_op jit(solution)/shard_map/ppermute | solution.py:32
  113.0 5.0 %collective-permute-done.17 = bf16[128,1536]{1,0:T(8,128)(2,1)S(1)} collective-permute-done((bf16[128,1536]{1,0:T(8,128)(2,1)}, bf16[128,1536]{1,0:T(8,128)(2,1)S(1)}, u32[]{:S(2)}, u32[]{:S(2)}) %collective-permute-start.17) | collective-permute-done | bytes 393248 | tf_op jit(solution)/shard_map/ppermute | solution.py:32
  118.0 2.6 %collective-permute-start.31 = (bf16[64,256]{1,0:T(8,128)(2,1)S(1)}, bf16[64,256]{1,0:T(8,128)(2,1)S(1)}, u32[]{:S(2)}, u32[]{:S(2)}) collective-permute-start(bf16[64,256]{1,0:T(8,128)(2,1)S(1)} %get-tuple-element.43), channel_id=1, source_target_pairs={{0,1},{1,2},{2,3},{3,0},{4,5},{5,6},{6,7},{7,4},{8,9},{9,10},{10,1... | collective-permute-start | bytes 98312 | tf_op jit(solution)/shard_map/ppermute | solution.py:32
  120.6 25.1 %collective-permute-done.18 = bf16[128,1536]{1,0:T(8,128)(2,1)S(1)} collective-permute-done((bf16[128,1536]{1,0:T(8,128)(2,1)}, bf16[128,1536]{1,0:T(8,128)(2,1)S(1)}, u32[]{:S(2)}, u32[]{:S(2)}) %collective-permute-start.18) | collective-permute-done | bytes 393248 | tf_op jit(solution)/shard_map/ppermute | solution.py:32
  145.7 2.1 %add_convert_fusion = bf16[128,1536]{1,0:T(8,128)(2,1)} fusion(bf16[128,1536]{1,0:T(8,128)(2,1)S(1)} %collective-permute-done.19, bf16[128,1536]{1,0:T(8,128)(2,1)S(1)} %collective-permute-done.18, bf16[128,1536]{1,0:T(8,128)(2,1)S(1)} %collective-permute-done.17, bf16[128,1536]{1,0:T(8,128)(2,1)} %get-tuple-element.24, bf16[512,1536]{1,0:T(8,128)(2,1)} %x_ref.1, ...), kind=kLoop, calls=%fused_computation.1 | loop fusion | flops 1966080 | bytes 2359300 | tf_op jit(solution)/shard_map/convert_element_type | solution.py:554
  (93 shorter events, 17.1 us)
Async XLA Ops:
  0.6 11.1 %collective-permute-start.11 = (bf16[192,768]{1,0:T(8,128)(2,1)}, bf16[192,768]{1,0:T(8,128)(2,1)S(1)}, u32[]{:S(2)}, u32[]{:S(2)}) collective-permute-start(bf16[192,768]{1,0:T(8,128)(2,1)} %refs_0_.4), channel_id=1, source_target_pairs={{0,8},{1,9},{2,10},{3,11},{4,12},{5,13},{6,14},{7,15},{8,0},{9,1},... | collective-permute-start | bytes 884744 | tf_op jit(solution)/shard_map/ppermute | solution.py:32
  3.7 10.1 %collective-permute-start.13 = (bf16[192,768]{1,0:T(8,128)(2,1)}, bf16[192,768]{1,0:T(8,128)(2,1)S(1)}, u32[]{:S(2)}, u32[]{:S(2)}) collective-permute-start(bf16[192,768]{1,0:T(8,128)(2,1)} %refs_0_.4), channel_id=1, source_target_pairs={{0,16},{1,17},{2,18},{3,19},{4,20},{5,21},{6,22},{7,23},{8,24},{9,... | collective-permute-start | bytes 884744 | tf_op jit(solution)/shard_map/ppermute | solution.py:32
  5.2 13.5 %collective-permute-start.3 = (bf16[192,768]{1,0:T(8,128)(2,1)}, bf16[192,768]{1,0:T(8,128)(2,1)S(1)}, u32[]{:S(2)}, u32[]{:S(2)}) collective-permute-start(bf16[192,768]{1,0:T(8,128)(2,1)} %refs_0_.5), channel_id=1, source_target_pairs={{0,16},{1,17},{2,18},{3,19},{4,20},{5,21},{6,22},{7,23},{8,24},{9,... | collective-permute-start | bytes 884744 | tf_op jit(solution)/shard_map/ppermute | solution.py:32
  5.7 13.4 %collective-permute-start.10 = (bf16[192,768]{1,0:T(8,128)(2,1)}, bf16[192,768]{1,0:T(8,128)(2,1)S(1)}, u32[]{:S(2)}, u32[]{:S(2)}) collective-permute-start(bf16[192,768]{1,0:T(8,128)(2,1)} %refs_0_.4), channel_id=1, source_target_pairs={{0,4},{1,5},{2,6},{3,7},{4,0},{5,1},{6,2},{7,3},{8,12},{9,13},{10,... | collective-permute-start | bytes 884744 | tf_op jit(solution)/shard_map/ppermute | solution.py:32
  5.7 15.0 %collective-permute-start.1 = (bf16[192,768]{1,0:T(8,128)(2,1)}, bf16[192,768]{1,0:T(8,128)(2,1)S(1)}, u32[]{:S(2)}, u32[]{:S(2)}) collective-permute-start(bf16[192,768]{1,0:T(8,128)(2,1)} %refs_0_.5), channel_id=1, source_target_pairs={{0,8},{1,9},{2,10},{3,11},{4,12},{5,13},{6,14},{7,15},{8,0},{9,1},... | collective-permute-start | bytes 884744 | tf_op jit(solution)/shard_map/ppermute | solution.py:32
  11.7 9.0 %collective-permute-start = (bf16[192,768]{1,0:T(8,128)(2,1)}, bf16[192,768]{1,0:T(8,128)(2,1)S(1)}, u32[]{:S(2)}, u32[]{:S(2)}) collective-permute-start(bf16[192,768]{1,0:T(8,128)(2,1)} %refs_0_.5), channel_id=1, source_target_pairs={{0,4},{1,5},{2,6},{3,7},{4,0},{5,1},{6,2},{7,3},{8,12},{9,13},{10,... | collective-permute-start | bytes 884744 | tf_op jit(solution)/shard_map/ppermute | solution.py:32
  13.8 7.5 %collective-permute-start.12 = (bf16[192,768]{1,0:T(8,128)(2,1)S(1)}, bf16[192,768]{1,0:T(8,128)(2,1)S(1)}, u32[]{:S(2)}, u32[]{:S(2)}) collective-permute-start(bf16[192,768]{1,0:T(8,128)(2,1)S(1)} %collective-permute-done.11.refs_2_), channel_id=1, source_target_pairs={{0,4},{1,5},{2,6},{3,7},{4,0},{5,1},{6,2},{7,3},{8,12},{9,13},{10,... | collective-permute-start | bytes 884744 | tf_op jit(solution)/shard_map/ppermute | solution.py:32
  18.7 7.6 %collective-permute-start.5 = (bf16[192,768]{1,0:T(8,128)(2,1)S(1)}, bf16[192,768]{1,0:T(8,128)(2,1)S(1)}, u32[]{:S(2)}, u32[]{:S(2)}) collective-permute-start(bf16[192,768]{1,0:T(8,128)(2,1)S(1)} %collective-permute-done.3.refs_4_), channel_id=1, source_target_pairs={{0,8},{1,9},{2,10},{3,11},{4,12},{5,13},{6,14},{7,15},{8,0},{9,1},... | collective-permute-start | bytes 884744 | tf_op jit(solution)/shard_map/ppermute | solution.py:32
  19.1 7.7 %collective-permute-start.15 = (bf16[192,768]{1,0:T(8,128)(2,1)S(1)}, bf16[192,768]{1,0:T(8,128)(2,1)}, u32[]{:S(2)}, u32[]{:S(2)}) collective-permute-start(bf16[192,768]{1,0:T(8,128)(2,1)S(1)} %collective-permute-done.11.refs_2_), channel_id=1, source_target_pairs={{0,16},{1,17},{2,18},{3,19},{4,20},{5,21},{6,22},{7,23},{8,24},{9,... | collective-permute-start | bytes 884744 | tf_op jit(solution)/shard_map/ppermute | solution.py:32
  20.7 13.4 %collective-permute-start.14 = (bf16[192,768]{1,0:T(8,128)(2,1)S(1)}, bf16[192,768]{1,0:T(8,128)(2,1)S(1)}, u32[]{:S(2)}, u32[]{:S(2)}) collective-permute-start(bf16[192,768]{1,0:T(8,128)(2,1)S(1)} %collective-permute-done.13.refs_4_), channel_id=1, source_target_pairs={{0,4},{1,5},{2,6},{3,7},{4,0},{5,1},{6,2},{7,3},{8,12},{9,13},{10,... | collective-permute-start | bytes 884744 | tf_op jit(solution)/shard_map/ppermute | solution.py:32
  20.8 15.0 %collective-permute-start.4 = (bf16[192,768]{1,0:T(8,128)(2,1)S(1)}, bf16[192,768]{1,0:T(8,128)(2,1)S(1)}, u32[]{:S(2)}, u32[]{:S(2)}) collective-permute-start(bf16[192,768]{1,0:T(8,128)(2,1)S(1)} %collective-permute-done.3.refs_4_), channel_id=1, source_target_pairs={{0,4},{1,5},{2,6},{3,7},{4,0},{5,1},{6,2},{7,3},{8,12},{9,13},{10,... | collective-permute-start | bytes 884744 | tf_op jit(solution)/shard_map/ppermute | solution.py:32
  21.3 16.8 %collective-permute-start.2 = (bf16[192,768]{1,0:T(8,128)(2,1)S(1)}, bf16[192,768]{1,0:T(8,128)(2,1)S(1)}, u32[]{:S(2)}, u32[]{:S(2)}) collective-permute-start(bf16[192,768]{1,0:T(8,128)(2,1)S(1)} %collective-permute-done.1.refs_2_), channel_id=1, source_target_pairs={{0,4},{1,5},{2,6},{3,7},{4,0},{5,1},{6,2},{7,3},{8,12},{9,13},{10,... | collective-permute-start | bytes 884744 | tf_op jit(solution)/shard_map/ppermute | solution.py:32
  26.3 17.2 %collective-permute-start.6 = (bf16[192,768]{1,0:T(8,128)(2,1)S(1)}, bf16[192,768]{1,0:T(8,128)(2,1)}, u32[]{:S(2)}, u32[]{:S(2)}) collective-permute-start(bf16[192,768]{1,0:T(8,128)(2,1)S(1)} %collective-permute-done.5.refs_6_), channel_id=1, source_target_pairs={{0,4},{1,5},{2,6},{3,7},{4,0},{5,1},{6,2},{7,3},{8,12},{9,13},{10,... | collective-permute-start | bytes 884744 | tf_op jit(solution)/shard_map/ppermute | solution.py:32
  26.8 30.6 %collective-permute-start.16 = (bf16[192,768]{1,0:T(8,128)(2,1)}, bf16[192,768]{1,0:T(8,128)(2,1)}, u32[]{:S(2)}, u32[]{:S(2)}) collective-permute-start(bf16[192,768]{1,0:T(8,128)(2,1)} %collective-permute-done.15.refs_5_), channel_id=1, source_target_pairs={{0,4},{1,5},{2,6},{3,7},{4,0},{5,1},{6,2},{7,3},{8,12},{9,13},{10,... | collective-permute-start | bytes 884744 | tf_op jit(solution)/shard_map/ppermute | solution.py:32
  34.2 12.8 %collective-permute-start.7 = (bf16[832,128]{1,0:T(8,128)(2,1)S(1)}, bf16[832,128]{1,0:T(8,128)(2,1)S(1)}, u32[]{:S(2)}, u32[]{:S(2)}) collective-permute-start(bf16[832,128]{1,0:T(8,128)(2,1)S(1)} %copy-done), channel_id=1, source_target_pairs={{0,1},{1,2},{2,3},{3,0},{4,5},{5,6},{6,7},{7,4},{8,9},{9,10},{10,1... | collective-permute-start | bytes 638984 | tf_op jit(solution)/shard_map/ppermute | solution.py:32
  35.8 11.8 %collective-permute-start.9 = (bf16[832,128]{1,0:T(8,128)(2,1)S(1)}, bf16[832,128]{1,0:T(8,128)(2,1)S(1)}, u32[]{:S(2)}, u32[]{:S(2)}) collective-permute-start(bf16[832,128]{1,0:T(8,128)(2,1)S(1)} %copy-done), channel_id=1, source_target_pairs={{0,3},{1,0},{2,1},{3,2},{4,7},{5,4},{6,5},{7,6},{8,11},{9,8},{10,9... | collective-permute-start | bytes 638984 | tf_op jit(solution)/shard_map/ppermute | solution.py:32
  38.1 19.3 %collective-permute-start.8 = (bf16[832,128]{1,0:T(8,128)(2,1)S(1)}, bf16[832,128]{1,0:T(8,128)(2,1)S(1)}, u32[]{:S(2)}, u32[]{:S(2)}) collective-permute-start(bf16[832,128]{1,0:T(8,128)(2,1)S(1)} %copy-done), channel_id=1, source_target_pairs={{0,2},{1,3},{2,0},{3,1},{4,6},{5,7},{6,4},{7,5},{8,10},{9,11},{10,... | collective-permute-start | bytes 638984 | tf_op jit(solution)/shard_map/ppermute | solution.py:32
  63.3 6.5 %collective-permute-start.20 = (bf16[272,256]{1,0:T(8,128)(2,1)}, bf16[272,256]{1,0:T(8,128)(2,1)S(1)}, u32[]{:S(2)}, u32[]{:S(2)}) collective-permute-start(bf16[272,256]{1,0:T(8,128)(2,1)} %get-tuple-element.29), channel_id=1, source_target_pairs={{0,3},{1,0},{2,1},{3,2},{4,7},{5,4},{6,5},{7,6},{8,11},{9,8},{10,9... | collective-permute-start | bytes 417800 | tf_op jit(solution)/shard_map/ppermute | solution.py:32
  64.9 11.9 %collective-permute-start.21 = (bf16[272,256]{1,0:T(8,128)(2,1)}, bf16[272,256]{1,0:T(8,128)(2,1)S(1)}, u32[]{:S(2)}, u32[]{:S(2)}) collective-permute-start(bf16[272,256]{1,0:T(8,128)(2,1)} %get-tuple-element.30), channel_id=1, source_target_pairs={{0,2},{1,3},{2,0},{3,1},{4,6},{5,7},{6,4},{7,5},{8,10},{9,11},{10,... | collective-permute-start | bytes 417800 | tf_op jit(solution)/shard_map/ppermute | solution.py:32
  64.9 11.9 %collective-permute-start.22 = (bf16[272,256]{1,0:T(8,128)(2,1)}, bf16[272,256]{1,0:T(8,128)(2,1)S(1)}, u32[]{:S(2)}, u32[]{:S(2)}) collective-permute-start(bf16[272,256]{1,0:T(8,128)(2,1)} %get-tuple-element.31), channel_id=1, source_target_pairs={{0,1},{1,2},{2,3},{3,0},{4,5},{5,6},{6,7},{7,4},{8,9},{9,10},{10,1... | collective-permute-start | bytes 417800 | tf_op jit(solution)/shard_map/ppermute | solution.py:32
  79.6 3.4 %collective-permute-start.23 = (bf16[48,256]{1,0:T(8,128)(2,1)}, bf16[48,256]{1,0:T(8,128)(2,1)S(1)}, u32[]{:S(2)}, u32[]{:S(2)}) collective-permute-start(bf16[48,256]{1,0:T(8,128)(2,1)} %get-tuple-element.34), channel_id=1, source_target_pairs={{0,4},{1,5},{2,6},{3,7},{4,8},{5,9},{6,10},{7,11},{8,12},{9,13},{1... | collective-permute-start | bytes 73736 | tf_op jit(solution)/shard_map/ppermute | solution.py:32
  80.9 5.2 %collective-permute-start.24 = (bf16[48,256]{1,0:T(8,128)(2,1)}, bf16[48,256]{1,0:T(8,128)(2,1)S(1)}, u32[]{:S(2)}, u32[]{:S(2)}) collective-permute-start(bf16[48,256]{1,0:T(8,128)(2,1)} %get-tuple-element.35), channel_id=1, source_target_pairs={{4,0},{5,1},{6,2},{7,3},{8,4},{9,5},{10,6},{11,7},{12,8},{13,9},{1... | collective-permute-start | bytes 73736 | tf_op jit(solution)/shard_map/ppermute | solution.py:32
  92.1 4.3 %collective-permute-start.25 = (bf16[4,256,256]{2,1,0:T(8,128)(2,1)}, bf16[4,256,256]{2,1,0:T(8,128)(2,1)S(1)}, u32[]{:S(2)}, u32[]{:S(2)}) collective-permute-start(bf16[4,256,256]{2,1,0:T(8,128)(2,1)} %get-tuple-element.38), channel_id=1, source_target_pairs={{0,4},{1,5},{2,6},{3,7},{4,0},{5,1},{6,2},{7,3},{8,12},{9,13},{10,... | collective-permute-start | bytes 1572872 | tf_op jit(solution)/shard_map/ppermute | solution.py:32
  97.9 11.1 %collective-permute-start.26 = (bf16[256,256]{1,0:T(8,128)(2,1)S(1)}, bf16[256,256]{1,0:T(8,128)(2,1)S(1)}, u32[]{:S(2)}, u32[]{:S(2)}) collective-permute-start(bf16[256,256]{1,0:T(8,128)(2,1)S(1)} %get-tuple-element.39), channel_id=1, source_target_pairs={{0,8},{1,9},{2,10},{3,11},{4,12},{5,13},{6,14},{7,15},{8,0},{9,1},... | collective-permute-start | bytes 393224 | tf_op jit(solution)/shard_map/ppermute | solution.py:32
  100.2 10.8 %collective-permute-start.27 = (bf16[256,256]{1,0:T(8,128)(2,1)S(1)}, bf16[256,256]{1,0:T(8,128)(2,1)S(1)}, u32[]{:S(2)}, u32[]{:S(2)}) collective-permute-start(bf16[256,256]{1,0:T(8,128)(2,1)S(1)} %get-tuple-element.41), channel_id=1, source_target_pairs={{0,16},{1,17},{2,18},{3,19},{4,20},{5,21},{6,22},{7,23},{8,24},{9,... | collective-permute-start | bytes 393224 | tf_op jit(solution)/shard_map/ppermute | solution.py:32
  100.2 10.8 %collective-permute-start.28 = (bf16[256,256]{1,0:T(8,128)(2,1)S(1)}, bf16[256,256]{1,0:T(8,128)(2,1)S(1)}, u32[]{:S(2)}, u32[]{:S(2)}) collective-permute-start(bf16[256,256]{1,0:T(8,128)(2,1)S(1)} %get-tuple-element.40), channel_id=1, source_target_pairs={{0,24},{1,25},{2,26},{3,27},{4,28},{5,29},{6,30},{7,31},{8,16},{9,... | collective-permute-start | bytes 393224 | tf_op jit(solution)/shard_map/ppermute | solution.py:32
  106.3 11.7 %collective-permute-start.17 = (bf16[128,1536]{1,0:T(8,128)(2,1)}, bf16[128,1536]{1,0:T(8,128)(2,1)S(1)}, u32[]{:S(2)}, u32[]{:S(2)}) collective-permute-start(bf16[128,1536]{1,0:T(8,128)(2,1)} %get-tuple-element.25), channel_id=1, source_target_pairs={{0,3},{1,0},{2,1},{3,2},{4,7},{5,4},{6,5},{7,6},{8,11},{9,8},{10,9... | collective-permute-start | bytes 1179656 | tf_op jit(solution)/shard_map/ppermute | solution.py:32
  107.6 38.1 %collective-permute-start.18 = (bf16[128,1536]{1,0:T(8,128)(2,1)}, bf16[128,1536]{1,0:T(8,128)(2,1)S(1)}, u32[]{:S(2)}, u32[]{:S(2)}) collective-permute-start(bf16[128,1536]{1,0:T(8,128)(2,1)} %get-tuple-element.26), channel_id=1, source_target_pairs={{0,2},{1,3},{2,0},{3,1},{4,6},{5,7},{6,4},{7,5},{8,10},{9,11},{10,... | collective-permute-start | bytes 1179656 | tf_op jit(solution)/shard_map/ppermute | solution.py:32
  109.0 36.7 %collective-permute-start.19 = (bf16[128,1536]{1,0:T(8,128)(2,1)}, bf16[128,1536]{1,0:T(8,128)(2,1)S(1)}, u32[]{:S(2)}, u32[]{:S(2)}) collective-permute-start(bf16[128,1536]{1,0:T(8,128)(2,1)} %get-tuple-element.27), channel_id=1, source_target_pairs={{0,1},{1,2},{2,3},{3,0},{4,5},{5,6},{6,7},{7,4},{8,9},{9,10},{10,1... | collective-permute-start | bytes 1179656 | tf_op jit(solution)/shard_map/ppermute | solution.py:32
  111.1 36.7 %collective-permute-start.29 = (bf16[64,256]{1,0:T(8,128)(2,1)S(1)}, bf16[64,256]{1,0:T(8,128)(2,1)S(1)}, u32[]{:S(2)}, u32[]{:S(2)}) collective-permute-start(bf16[64,256]{1,0:T(8,128)(2,1)S(1)} %get-tuple-element.42), channel_id=1, source_target_pairs={{0,3},{1,0},{2,1},{3,2},{4,7},{5,4},{6,5},{7,6},{8,11},{9,8},{10,9... | collective-permute-start | bytes 98312 | tf_op jit(solution)/shard_map/ppermute | solution.py:32
  113.0 34.8 %collective-permute-start.30 = (bf16[64,256]{1,0:T(8,128)(2,1)S(1)}, bf16[64,256]{1,0:T(8,128)(2,1)S(1)}, u32[]{:S(2)}, u32[]{:S(2)}) collective-permute-start(bf16[64,256]{1,0:T(8,128)(2,1)S(1)} %get-tuple-element.44), channel_id=1, source_target_pairs={{0,2},{1,3},{2,0},{3,1},{4,6},{5,7},{6,4},{7,5},{8,10},{9,11},{10,... | collective-permute-start | bytes 98312 | tf_op jit(solution)/shard_map/ppermute | solution.py:32
  118.0 29.8 %collective-permute-start.31 = (bf16[64,256]{1,0:T(8,128)(2,1)S(1)}, bf16[64,256]{1,0:T(8,128)(2,1)S(1)}, u32[]{:S(2)}, u32[]{:S(2)}) collective-permute-start(bf16[64,256]{1,0:T(8,128)(2,1)S(1)} %get-tuple-element.43), channel_id=1, source_target_pairs={{0,1},{1,2},{2,3},{3,0},{4,5},{5,6},{6,7},{7,4},{8,9},{9,10},{10,1... | collective-permute-start | bytes 98312 | tf_op jit(solution)/shard_map/ppermute | solution.py:32
  (21 other events, 255.3 us)
where the time goes:
time: 149 us; the launch traced here: 148 us
  waiting for transfers between devices  74.1 us (50%)
  starting transfers between devices  32.8 us (22%)
  Pallas kernels  30.8 us (21%)
  other arithmetic  5.67 us (4%)
  local copies, waits for them, and re-layouts  4.17 us (3%)
    ppermute x32, waiting for transfers between devices, send(): return lax.ppermute(value, ALL, pairs)  74.1 us
    ppermute x32, starting transfers between devices, send(): return lax.ppermute(value, ALL, pairs)  32.8 us
    pallas_call x8, Pallas kernels, call(): pl.pallas_call(body, out_shape=[jax.ShapeDtypeStruct(*o) for o in outs],...  30.8 us
  transfers between devices with their start and end apart: 32, of which 13 were waited for; matrix products, arithmetic and copies ran while one was open for 4% of the time, Pallas kernels for 12%

commit v1 on v0

--- a/solution.py
+++ b/solution.py
@@ -73,7 +73,7 @@
         cost_estimate=pl.CostEstimate(
             flops=int(flops), bytes_accessed=int(moved), transcendentals=int(tanhs)
         ),
-        compiler_params=pltpu.CompilerParams(vmem_limit_bytes=56 * 2**20),
+        compiler_params=pltpu.CompilerParams(vmem_limit_bytes=20 * 2**20),
     )(*args)
 
 
@@ -94,7 +94,7 @@
 def norm_body(depth, id_ref, x_ref, gain_ref, proj_ref, out_ref, own_ref):
     wide = x_ref[...].astype(f32)
     scale = lax.rsqrt(jnp.mean(wide * wide, axis=-1, keepdims=True) + epsilon)
-    out_ref[...] = (wide * scale * gain_ref[...]).astype(bf16)
+    out_ref[...] = (wide * scale * gain_ref[...].reshape(1, -1)).astype(bf16)
     own = own_ref.shape[0]
     mine = pl.ds(pl.multiple_of((id_ref[0] % depth) * own, own), own)
     own_ref[...] = jnp.dot(x_ref[mine, :], proj_ref[...], preferred_element_type=f32)
@@ -149,12 +149,16 @@
             out_ref[b * rows : (b + 1) * rows, j * inner : (j + 1) * inner] = total.astype(bf16)
 
 
-def place_rows(me, pieces, refs, rows, full_ref):
+def place_blocks(me, pieces, refs, rows, full_ref, paired):
+    pairs = sorted({mask // 2 for mask in pieces if mask is not None})
     for mask, ref in zip(pieces, refs):
         if mask is None:
             full_ref[...] = ref[...]
-        else:
-            full_ref[pl.ds(pl.multiple_of((me ^ mask) * rows, 64), rows), :] = ref[...]
+            continue
+        start = (me ^ mask) * rows
+        if paired:
+            start = pairs.index(mask // 2) * 2 * rows + ((me % 2) ^ (mask % 2)) * rows
+        full_ref[pl.ds(pl.multiple_of(start, 64), rows), :] = ref[...]
 
 
 def add_product(me, x_ref, pieces, rows, full_ref, at, step, total):
@@ -172,20 +176,10 @@
     return total
 
 
-def place_pairs(me, pieces, refs, rows, full_ref):
-    if pieces[0] is None:
-        full_ref[...] = refs[0][...]
-        return
-    pairs = sorted({mask // 2 for mask in pieces})
-    for mask, ref in zip(pieces, refs):
-        start = pairs.index(mask // 2) * 2 * rows + ((me % 2) ^ (mask % 2)) * rows
-        full_ref[pl.ds(pl.multiple_of(start, 64), rows), :] = ref[...]
-
-
 def early_body(pieces, rows, depth, id_ref, x_ref, *refs):
-    blocks, out_ref, full = refs[:-2], refs[-2], refs[-1]
+    blocks, (out_ref, full) = refs[:-2], refs[-2:]
     me = id_ref[0] // depth
-    place_pairs(me, pieces, blocks, rows, full)
+    place_blocks(me, pieces, blocks, rows, full, True)
     width = out_ref.shape[1]
     step = 256 if width % 256 == 0 else width
     for at in range(0, width, step):
@@ -202,7 +196,7 @@
     full, flux, dense = refs[0], refs[1], refs[2:]
     me = id_ref[0] // depth
     z = id_ref[0] % depth
-    place_pairs(me, pieces, blocks, rows, full)
+    place_blocks(me, pieces, blocks, rows, full, True)
     for k in range(depth):
         build_matrix(*remap, mats[k], dense[k])
     width = hid_ref.shape[1]
@@ -231,18 +225,18 @@
 
 
 def both_body(pieces, rows, depth, id_ref, proj_ref, *refs):
-    blocks, out_ref, full = refs[:-2], refs[-2], refs[-1]
-    place_rows(id_ref[0] // depth, pieces, blocks, rows, full)
+    blocks, (out_ref, full) = refs[:-2], refs[-2:]
+    place_blocks(id_ref[0] // depth, pieces, blocks, rows, full, False)
     out_ref[...] = lax.dot_general(
         proj_ref[...], full[...], TN, preferred_element_type=f32
     ).astype(bf16)
 
 
-def second_body(pieces, rows, depth, id_ref, hid_ref, *refs):
+def second_body(pieces, rows, depth, shards, id_ref, hid_ref, *refs):
     blocks, refs = refs[: len(pieces)], refs[len(pieces) :]
-    parts, full, sums = refs[:depth], refs[depth], refs[depth + 1]
+    parts, (full, sums) = refs[:-2], refs[-2:]
     z = id_ref[0] % depth
-    place_rows(id_ref[0] // depth, pieces, blocks, rows, full)
+    place_blocks(id_ref[0] // depth, pieces, blocks, rows, full, False)
     tokens, width = sums.shape
     own = tokens // depth
     step = 256 if width % 256 == 0 else width
@@ -250,9 +244,10 @@
         sums[:, at : at + step] = lax.dot_general(
             hid_ref[...], full[at : at + step, :], NT, preferred_element_type=f32
         ).astype(bf16)
-    for k in range(depth):
-        start = pl.multiple_of(((z - k + depth) % depth) * own, own)
-        parts[k][...] = sums[pl.ds(start, own), :]
+    for ref, rule in zip(parts, shards):
+        for n, of in enumerate(rule):
+            start = pl.multiple_of(of(z) * own, own)
+            ref[n * own : (n + 1) * own, :] = sums[pl.ds(start, own), :]
 
 
 def field_body(depth, tile_x, tile_y, rows_at, id_ref, state_ref, wet_ref, west_ref, east_ref, *refs):
@@ -327,7 +322,7 @@
     conv = conv.reshape(cells, channels)
     centred = conv - jnp.mean(conv, axis=-1, keepdims=True)
     variance = jnp.mean(centred * centred, axis=-1, keepdims=True)
-    normed = (centred * lax.rsqrt(variance + epsilon) * gain_ref[...]).astype(bf16)
+    normed = (centred * lax.rsqrt(variance + epsilon) * gain_ref[...].reshape(1, -1)).astype(bf16)
     wet = wet_ref[...].astype(f32)
     dout = dout_ref[...]
     hid = win_ref.shape[1]
@@ -411,7 +406,7 @@
     normed, own_flux = call(
         functools.partial(norm_body, depth),
         [((tokens, model), bf16), ((own, channels), f32)],
-        (me, atmos_state, atmos_gain.reshape(1, model), flux_proj),
+        (me, atmos_state, atmos_gain, flux_proj),
         specs=[SMEM] + [VMEM] * 3,
         moved=4 * mb,
     )
@@ -423,7 +418,7 @@
         functools.partial(both_body, second_at, rows, depth),
         [((channels, share), bf16)],
         (me, flux_proj, *second),
-        specs=[SMEM] + [VMEM] * (1 + len(second)),
+        specs=[SMEM, VMEM] + [VMEM] * len(second),
         scratch=[pltpu.VMEM((model, share), bf16)],
         flops=2 * model * share * channels,
         moved=3 * mb,
@@ -439,7 +434,7 @@
             functools.partial(early_body, [p[0] for p in soon], rows, depth),
             [((tokens, share), f32)],
             (me, normed, *[p[1] for p in soon]),
-            specs=[SMEM] + [VMEM] * (1 + len(soon)),
+            specs=[SMEM, VMEM] + [VMEM] * len(soon),
             scratch=[pltpu.VMEM((6 * rows, share), bf16)],
             flops=2 * tokens * share * 6 * rows,
             moved=5 * mb,
@@ -457,7 +452,7 @@
         ),
         [((tokens, share), bf16)] + [((cells + 2 * tile_x, channels), bf16)] * depth,
         (me, normed, own_flux, both, *payloads, *sums, *[p[1] for p in first]),
-        specs=[SMEM] + [VMEM] * (3 + depth + len(sums) + len(first)),
+        specs=[SMEM] + [VMEM] * (3 + depth + len(sums)) + [VMEM] * len(first),
         scratch=[
             pltpu.VMEM((2 * rows if early else model, share), bf16),
             pltpu.VMEM((tokens, channels), f32),
@@ -471,16 +466,34 @@
     moved = [moved[0]] + [send(moved[k], shift_z(-k)) for k in range(1, depth)]
 
     rows = w_second.shape[0]
+    pairwise = depth == 4
+    if pairwise:
+        shards = [
+            [lambda z: z],
+            [lambda z: z ^ 2],
+            [lambda z: z ^ 1, lambda z: z ^ 3],
+        ]
+    else:
+        shards = [[lambda z, k=k: (z - k + depth) % depth] for k in range(depth)]
     parts = call(
-        functools.partial(second_body, second_at, rows, depth),
-        [((own, model), bf16)] * depth,
+        functools.partial(second_body, second_at, rows, depth, shards),
+        [((own * len(rule), model), bf16) for rule in shards],
         (me, hidden, *second),
-        specs=[SMEM] + [VMEM] * (1 + len(second)),
-        scratch=[pltpu.VMEM((model, share), bf16), pltpu.VMEM((tokens, model), bf16)],
+        specs=[SMEM, VMEM] + [VMEM] * len(second),
+        scratch=[
+            pltpu.VMEM((model, share), bf16),
+            pltpu.VMEM((tokens, model), bf16),
+        ],
         flops=2 * tokens * model * share,
         moved=6 * mb,
     )
-    parts = [parts[0]] + [send(parts[k], shift_z(-k)) for k in range(1, depth)]
+    if pairwise:
+        mine, far, give = parts
+        got = send(give, lambda group, z: (group, z ^ 1))
+        far = (far.astype(f32) + got[own:].astype(f32)).astype(bf16)
+        parts = [mine, got[:own], send(far, lambda group, z: (group, z ^ 2))]
+    else:
+        parts = [parts[0]] + [send(parts[k], shift_z(-k)) for k in range(1, depth)]
 
     dout = (ocean_cotangent.reshape(cells, channels).astype(f32) * wet.astype(f32)).astype(bf16)
 
@@ -512,7 +525,7 @@
             wet,
             dout,
             conv_kernel,
-            ocean_gain.reshape(1, channels),
+            ocean_gain,
             ocean_w_in,
             ocean_w_out,
         ),

time: 149 us -> 136 us (0.913)
  Pallas kernels: 30.8 us -> 15.1 us
  waiting for transfers between devices: 74.1 us -> 78.8 us
  local copies, waits for them, and re-layouts: 4.17 us -> 7.32 us
  starting transfers between devices: 32.8 us -> 29.7 us
  other arithmetic: 5.67 us -> 4.1 us
    pallas_call x8, Pallas kernels: 30.8 us -> 15.1 us  [call(): pl.pallas_call(body, out_shape=[jax.ShapeDtypeStruct(*o) for o in outs],...]
    ppermute x32 -> x31, waiting for transfers between devices: 74.1 us -> 78.8 us  [send(): return lax.ppermute(value, ALL, pairs)]
    unnamed x42 -> x36, local copies, waits for them, and re-layouts: 2.04 us -> 6.49 us
    ppermute x32 -> x31, starting transfers between devices: 32.8 us -> 29.7 us  [send(): return lax.ppermute(value, ALL, pairs)]
  transfers between devices with their start and end apart: 32 -> 31, of which waited for: 13 -> 14; matrix products, arithmetic and copies ran while one was open for 4% -> 2% of each run, Pallas kernels for 12% -> 6%
where the time goes in v1:
time: 136 us
  waiting for transfers between devices  78.8 us (58%)
  starting transfers between devices  29.7 us (22%)
  Pallas kernels  15.1 us (11%)
  local copies, waits for them, and re-layouts  7.32 us (5%)
  other arithmetic  4.1 us (3%)
    ppermute x31, waiting for transfers between devices, send(): return lax.ppermute(value, ALL, pairs)  78.8 us
    ppermute x31, starting transfers between devices, send(): return lax.ppermute(value, ALL, pairs)  29.7 us
    pallas_call x8, Pallas kernels, call(): pl.pallas_call(body, out_shape=[jax.ShapeDtypeStruct(*o) for o in outs],...  15.1 us
    unnamed x36, local copies, waits for them, and re-layouts  6.49 us
  transfers between devices with their start and end apart: 31, of which 14 were waited for; matrix products, arithmetic and copies ran while one was open for 2% of the time, Pallas kernels for 6%

profile of v1, /device:TPU:0, one launch (start us, length us, event | category | flops | bytes accessed | tf_op | source)
XLA Modules:
  0.0 135.9 jit_solution(13944851235614334396)
XLA Ops:
  0.6 3.0 %collective-permute-start.11 = (bf16[192,768]{1,0:T(8,128)(2,1)}, bf16[192,768]{1,0:T(8,128)(2,1)S(1)}, u32[]{:S(2)}, u32[]{:S(2)}) collective-permute-start(bf16[192,768]{1,0:T(8,128)(2,1)} %refs_0_.4), channel_id=1, source_target_pairs={{0,8},{1,9},{2,10},{3,11},{4,12},{5,13},{6,14},{7,15},{8,0},{9,1},... | collective-permute-start | bytes 884744 | tf_op jit(solution)/shard_map/ppermute | solution.py:32
  3.7 1.5 %collective-permute-start.13 = (bf16[192,768]{1,0:T(8,128)(2,1)}, bf16[192,768]{1,0:T(8,128)(2,1)S(1)}, u32[]{:S(2)}, u32[]{:S(2)}) collective-permute-start(bf16[192,768]{1,0:T(8,128)(2,1)} %refs_0_.4), channel_id=1, source_target_pairs={{0,16},{1,17},{2,18},{3,19},{4,20},{5,21},{6,22},{7,23},{8,24},{9,... | collective-permute-start | bytes 884744 | tf_op jit(solution)/shard_map/ppermute | solution.py:32
  5.8 6.0 %collective-permute-done.11.refs_2_ = bf16[192,768]{1,0:T(8,128)(2,1)S(1)} collective-permute-done((bf16[192,768]{1,0:T(8,128)(2,1)}, bf16[192,768]{1,0:T(8,128)(2,1)S(1)}, u32[]{:S(2)}, u32[]{:S(2)}) %collective-permute-start.11) | collective-permute-done | bytes 294944 | tf_op jit(solution)/shard_map/ppermute | solution.py:32
  11.7 2.0 %collective-permute-done.13.refs_4_ = bf16[192,768]{1,0:T(8,128)(2,1)S(1)} collective-permute-done((bf16[192,768]{1,0:T(8,128)(2,1)}, bf16[192,768]{1,0:T(8,128)(2,1)S(1)}, u32[]{:S(2)}, u32[]{:S(2)}) %collective-permute-start.13) | collective-permute-done | bytes 294944 | tf_op jit(solution)/shard_map/ppermute | solution.py:32
  13.8 4.9 %collective-permute-done.3.refs_4_ = bf16[192,768]{1,0:T(8,128)(2,1)S(1)} collective-permute-done((bf16[192,768]{1,0:T(8,128)(2,1)}, bf16[192,768]{1,0:T(8,128)(2,1)S(1)}, u32[]{:S(2)}, u32[]{:S(2)}) %collective-permute-start.3) | collective-permute-done | bytes 294944 | tf_op jit(solution)/shard_map/ppermute | solution.py:32
  19.0 1.7 %collective-permute-start.15 = (bf16[192,768]{1,0:T(8,128)(2,1)S(1)}, bf16[192,768]{1,0:T(8,128)(2,1)}, u32[]{:S(2)}, u32[]{:S(2)}) collective-permute-start(bf16[192,768]{1,0:T(8,128)(2,1)S(1)} %collective-permute-done.11.refs_2_), channel_id=1, source_target_pairs={{0,16},{1,17},{2,18},{3,19},{4,20},{5,21},{6,22},{7,23},{8,24},{9,... | collective-permute-start | bytes 884744 | tf_op jit(solution)/shard_map/ppermute | solution.py:32
  21.3 5.0 %collective-permute-done.5.refs_6_ = bf16[192,768]{1,0:T(8,128)(2,1)S(1)} collective-permute-done((bf16[192,768]{1,0:T(8,128)(2,1)S(1)}, bf16[192,768]{1,0:T(8,128)(2,1)S(1)}, u32[]{:S(2)}, u32[]{:S(2)}) %collective-permute-start.5) | collective-permute-done | bytes 294944 | tf_op jit(solution)/shard_map/ppermute | solution.py:32
  32.5 1.4 %copy-done.2 = bf16[512,1536]{1,0:T(8,128)(2,1)S(1)} copy-done((bf16[512,1536]{1,0:T(8,128)(2,1)S(1)}, bf16[512,1536]{1,0:T(8,128)(2,1)}, u32[]{:S(2)}) %copy-start.2) | copy-done | bytes 1572888
  35.4 1.6 %collective-permute-start.7 = (bf16[832,128]{1,0:T(8,128)(2,1)S(1)}, bf16[832,128]{1,0:T(8,128)(2,1)S(1)}, u32[]{:S(2)}, u32[]{:S(2)}) collective-permute-start(bf16[832,128]{1,0:T(8,128)(2,1)S(1)} %shard_map.159.refs_0_), channel_id=1, source_target_pairs={{0,1},{1,2},{2,3},{3,0},{4,5},{5,6},{6,7},{7,4},{8,9},{9,10},{10,1... | collective-permute-start | bytes 638984 | tf_op jit(solution)/shard_map/ppermute | solution.py:32
  37.0 2.2 %collective-permute-start.9 = (bf16[832,128]{1,0:T(8,128)(2,1)S(1)}, bf16[832,128]{1,0:T(8,128)(2,1)S(1)}, u32[]{:S(2)}, u32[]{:S(2)}) collective-permute-start(bf16[832,128]{1,0:T(8,128)(2,1)S(1)} %shard_map.159.refs_0_), channel_id=1, source_target_pairs={{0,3},{1,0},{2,1},{3,2},{4,7},{5,4},{6,5},{7,6},{8,11},{9,8},{10,9... | collective-permute-start | bytes 638984 | tf_op jit(solution)/shard_map/ppermute | solution.py:32
  40.1 1.5 %shard_map.160.refs_4_ = f32[512,768]{1,0:T(8,128)S(1)} custom-call(s32[1]{0:T(128)} %bitcast.id_ref, bf16[512,1536]{1,0:T(8,128)(2,1)S(1)} %get-tuple-element.20.x_ref, bf16[192,768]{1,0:T(8,128)(2,1)S(1)} %copy-done.5, bf16[192,768]{1,0:T(8,128)(2,1)S(1)} %collective-permute-done.10.refs_1_, bf16[192,768]{1,0:T(8,128)(2,1)S(1)} %collective-permute-done.11.refs_2_, ...), custom_call_target="tpu_custom_call" | custom-call | flops 905969664 | bytes 5242880 | tf_op jit(solution)/shard_map/pallas_call | solution.py:67
  41.6 1.9 %shard_map.158.both_ref = bf16[256,768]{1,0:T(8,128)(2,1)S(1)} custom-call(s32[1]{0:T(128)} %bitcast.id_ref, bf16[1536,256]{1,0:T(8,128)(2,1)S(1)} %copy-done.1, bf16[192,768]{1,0:T(8,128)(2,1)S(1)} %copy-done.6, bf16[192,768]{1,0:T(8,128)(2,1)S(1)} %collective-permute-done.refs_1_, bf16[192,768]{1,0:T(8,128)(2,1)S(1)} %collective-permute-done.1.refs_2_, ...), custom_call_target="tpu_custom_call" | custom-call | flops 603979776 | bytes 3145728 | tf_op jit(solution)/shard_map/pallas_call | solution.py:67
  43.6 1.8 %collective-permute-done.7.refs_1_.west_ref = bf16[832,128]{1,0:T(8,128)(2,1)S(1)} collective-permute-done((bf16[832,128]{1,0:T(8,128)(2,1)S(1)}, bf16[832,128]{1,0:T(8,128)(2,1)S(1)}, u32[]{:S(2)}, u32[]{:S(2)}) %collective-permute-start.7) | collective-permute-done | bytes 213024 | tf_op jit(solution)/shard_map/ppermute | solution.py:32
  45.4 3.4 %collective-permute-done.9.refs_3_.east_ref = bf16[832,128]{1,0:T(8,128)(2,1)S(1)} collective-permute-done((bf16[832,128]{1,0:T(8,128)(2,1)S(1)}, bf16[832,128]{1,0:T(8,128)(2,1)S(1)}, u32[]{:S(2)}, u32[]{:S(2)}) %collective-permute-start.9) | collective-permute-done | bytes 213024 | tf_op jit(solution)/shard_map/ppermute | solution.py:32
  48.8 9.8 %collective-permute-done.8.refs_2_ = bf16[832,128]{1,0:T(8,128)(2,1)S(1)} collective-permute-done((bf16[832,128]{1,0:T(8,128)(2,1)S(1)}, bf16[832,128]{1,0:T(8,128)(2,1)S(1)}, u32[]{:S(2)}, u32[]{:S(2)}) %collective-permute-start.8) | collective-permute-done | bytes 213024 | tf_op jit(solution)/shard_map/ppermute | solution.py:32
  58.6 3.0 %shard_map.161 = (bf16[512,768]{1,0:T(8,128)(2,1)S(1)}, bf16[272,256]{1,0:T(8,128)(2,1)S(1)}, bf16[272,256]{1,0:T(8,128)(2,1)S(1)}, bf16[272,256]{1,0:T(8,128)(2,1)S(1)}, bf16[272,256]{1,0:T(8,128)(2,1)S(1)}) custom-call(s32[1]{0:T(128)} %bitcast.id_ref, bf16[512,1536]{1,0:T(8,128)(2,1)S(1)} %get-tuple-element.20.x_ref, ...), custom_call_target="tpu_custom_call" | custom-call | flops 503316480 | bytes 5242880 | tf_op jit(solution)/shard_map/pallas_call | solution.py:67
  61.6 1.6 %collective-permute-start.19 = (bf16[272,256]{1,0:T(8,128)(2,1)S(1)}, bf16[272,256]{1,0:T(8,128)(2,1)S(1)}, u32[]{:S(2)}, u32[]{:S(2)}) collective-permute-start(bf16[272,256]{1,0:T(8,128)(2,1)S(1)} %get-tuple-element.27), channel_id=1, source_target_pairs={{0,3},{1,0},{2,1},{3,2},{4,7},{5,4},{6,5},{7,6},{8,11},{9,8},{10,9... | collective-permute-start | bytes 417800 | tf_op jit(solution)/shard_map/ppermute | solution.py:32
  64.0 4.0 %collective-permute-done.19.refs_1_ = bf16[272,256]{1,0:T(8,128)(2,1)S(1)} collective-permute-done((bf16[272,256]{1,0:T(8,128)(2,1)S(1)}, bf16[272,256]{1,0:T(8,128)(2,1)S(1)}, u32[]{:S(2)}, u32[]{:S(2)}) %collective-permute-start.19) | collective-permute-done | bytes 139296 | tf_op jit(solution)/shard_map/ppermute | solution.py:32
  68.0 6.9 %collective-permute-done.20.refs_2_ = bf16[272,256]{1,0:T(8,128)(2,1)S(1)} collective-permute-done((bf16[272,256]{1,0:T(8,128)(2,1)S(1)}, bf16[272,256]{1,0:T(8,128)(2,1)S(1)}, u32[]{:S(2)}, u32[]{:S(2)}) %collective-permute-start.20) | collective-permute-done | bytes 139296 | tf_op jit(solution)/shard_map/ppermute | solution.py:32
  75.0 1.4 %collective-permute-start.22 = (bf16[48,256]{1,0:T(8,128)(2,1)S(1)}, bf16[48,256]{1,0:T(8,128)(2,1)S(1)}, u32[]{:S(2)}, u32[]{:S(2)}) collective-permute-start(bf16[48,256]{1,0:T(8,128)(2,1)S(1)} %get-tuple-element.32), channel_id=1, source_target_pairs={{0,4},{1,5},{2,6},{3,7},{4,8},{5,9},{6,10},{7,11},{8,12},{9,13},{1... | collective-permute-start | bytes 73736 | tf_op jit(solution)/shard_map/ppermute | solution.py:32
  77.9 3.5 %collective-permute-done.23.low_ref = bf16[48,256]{1,0:T(8,128)(2,1)S(1)} collective-permute-done((bf16[48,256]{1,0:T(8,128)(2,1)S(1)}, bf16[48,256]{1,0:T(8,128)(2,1)S(1)}, u32[]{:S(2)}, u32[]{:S(2)}) %collective-permute-start.23) | collective-permute-done | bytes 24608 | tf_op jit(solution)/shard_map/ppermute | solution.py:32
  81.5 3.7 %shard_map.164 = (bf16[256,256]{1,0:T(8,128)(2,1)}, f32[4,256,256]{2,1,0:T(8,128)S(1)}, bf16[4,256,256]{2,1,0:T(8,128)(2,1)}) custom-call(s32[1]{0:T(128)} %bitcast.id_ref, bf16[256,256]{1,0:T(8,128)(2,1)S(1)} %get-tuple-element.30.field_ref, bf16[16,256]{1,0:T(8,128)(2,1)S(1)} %get-tuple-element.31.side_ref, ...), custom_call_target="tpu_custom_call" | custom-call | flops 671088640 | bytes 5242880 | tf_op jit(solution)/shard_map/pallas_call | solution.py:67
  85.1 2.5 %collective-permute-start.24 = (bf16[4,256,256]{2,1,0:T(8,128)(2,1)}, bf16[4,256,256]{2,1,0:T(8,128)(2,1)}, u32[]{:S(2)}, u32[]{:S(2)}) collective-permute-start(bf16[4,256,256]{2,1,0:T(8,128)(2,1)} %get-tuple-element.36), channel_id=1, source_target_pairs={{0,4},{1,5},{2,6},{3,7},{4,0},{5,1},{6,2},{7,3},{8,12},{9,13},{10,... | collective-permute-start | bytes 1572872 | tf_op jit(solution)/shard_map/ppermute | solution.py:32
  87.7 3.5 %shard_map.162 = (bf16[128,1536]{1,0:T(8,128)(2,1)S(1)}, bf16[128,1536]{1,0:T(8,128)(2,1)S(1)}, bf16[256,1536]{1,0:T(8,128)(2,1)}) custom-call(s32[1]{0:T(128)} %bitcast.id_ref, bf16[512,768]{1,0:T(8,128)(2,1)S(1)} %get-tuple-element.22.hid_ref, bf16[192,768]{1,0:T(8,128)(2,1)S(1)} %copy-done.6, bf16[192,768]{1,0:T(8,128)(2,1)S(1)} %collective-permute-done.refs_1_, ...), custom_call_target="tpu_custom_call" | custom-call | flops 1207959552 | bytes 6291456 | tf_op jit(solution)/shard_map/pallas_call | solution.py:67
  93.1 2.4 %collective-permute-start.25 = (bf16[256,256]{1,0:T(8,128)(2,1)S(1)}, bf16[256,256]{1,0:T(8,128)(2,1)S(1)}, u32[]{:S(2)}, u32[]{:S(2)}) collective-permute-start(bf16[256,256]{1,0:T(8,128)(2,1)S(1)} %get-tuple-element.37), channel_id=1, source_target_pairs={{0,8},{1,9},{2,10},{3,11},{4,12},{5,13},{6,14},{7,15},{8,0},{9,1},... | collective-permute-start | bytes 393224 | tf_op jit(solution)/shard_map/ppermute | solution.py:32
  95.6 1.5 %collective-permute-start.27 = (bf16[256,256]{1,0:T(8,128)(2,1)S(1)}, bf16[256,256]{1,0:T(8,128)(2,1)S(1)}, u32[]{:S(2)}, u32[]{:S(2)}) collective-permute-start(bf16[256,256]{1,0:T(8,128)(2,1)S(1)} %get-tuple-element.38), channel_id=1, source_target_pairs={{0,24},{1,25},{2,26},{3,27},{4,28},{5,29},{6,30},{7,31},{8,16},{9,... | collective-permute-start | bytes 393224 | tf_op jit(solution)/shard_map/ppermute | solution.py:32
  97.1 13.8 %collective-permute-done.17 = bf16[256,1536]{1,0:T(8,128)(2,1)S(1)} collective-permute-done((bf16[256,1536]{1,0:T(8,128)(2,1)}, bf16[256,1536]{1,0:T(8,128)(2,1)S(1)}, u32[]{:S(2)}, u32[]{:S(2)}) %collective-permute-start.17) | collective-permute-done | bytes 786464 | tf_op jit(solution)/shard_map/ppermute | solution.py:32
  111.0 2.7 %collective-permute-start.18 = (bf16[128,1536]{1,0:T(8,128)(2,1)S(1)}, bf16[128,1536]{1,0:T(8,128)(2,1)S(1)}, u32[]{:S(2)}, u32[]{:S(2)}) collective-permute-start(bf16[128,1536]{1,0:T(8,128)(2,1)S(1)} %add_convert_fusion.1), channel_id=1, source_target_pairs={{0,2},{1,3},{2,0},{3,1},{4,6},{5,7},{6,4},{7,5},{8,10},{9,11},{10,... | collective-permute-start | bytes 1179656 | tf_op jit(solution)/shard_map/ppermute | solution.py:32
  114.2 1.3 collective-permute-start.29
  116.2 6.6 %collective-permute-done.28 = bf16[64,256]{1,0:T(8,128)(2,1)S(1)} collective-permute-done((bf16[64,256]{1,0:T(8,128)(2,1)S(1)}, bf16[64,256]{1,0:T(8,128)(2,1)S(1)}, u32[]{:S(2)}, u32[]{:S(2)}) %collective-permute-start.28) | collective-permute-done | bytes 32800 | tf_op jit(solution)/shard_map/ppermute | solution.py:32
  122.8 10.6 %collective-permute-done.29 = bf16[64,256]{1,0:T(8,128)(2,1)S(1)} collective-permute-done((bf16[64,256]{1,0:T(8,128)(2,1)S(1)}, bf16[64,256]{1,0:T(8,128)(2,1)S(1)}, u32[]{:S(2)}, u32[]{:S(2)}) %collective-permute-start.29) | collective-permute-done | bytes 32800 | tf_op jit(solution)/shard_map/ppermute | solution.py:32
  134.0 1.9 %add_convert_fusion = bf16[128,1536]{1,0:T(8,128)(2,1)} fusion(bf16[128,1536]{1,0:T(8,128)(2,1)S(1)} %collective-permute-done.18, bf16[128,1536]{1,0:T(8,128)(2,1)S(1)} %get-tuple-element.23, bf16[256,1536]{1,0:T(8,128)(2,1)S(1)} %collective-permute-done.17, bf16[512,1536]{1,0:T(8,128)(2,1)} %x_ref.1, s32[]{:T(128)S(6)} %select_n.71), kind=kLoop, calls=%fused_computation.1 | loop fusion | flops 1572864 | bytes 1966084 | tf_op jit(solution)/shard_map/convert_element_type | solution.py:567
  (85 shorter events, 16.2 us)
Async XLA Ops:
  0.6 11.1 %collective-permute-start.11 = (bf16[192,768]{1,0:T(8,128)(2,1)}, bf16[192,768]{1,0:T(8,128)(2,1)S(1)}, u32[]{:S(2)}, u32[]{:S(2)}) collective-permute-start(bf16[192,768]{1,0:T(8,128)(2,1)} %refs_0_.4), channel_id=1, source_target_pairs={{0,8},{1,9},{2,10},{3,11},{4,12},{5,13},{6,14},{7,15},{8,0},{9,1},... | collective-permute-start | bytes 884744 | tf_op jit(solution)/shard_map/ppermute | solution.py:32
  3.7 10.1 %collective-permute-start.13 = (bf16[192,768]{1,0:T(8,128)(2,1)}, bf16[192,768]{1,0:T(8,128)(2,1)S(1)}, u32[]{:S(2)}, u32[]{:S(2)}) collective-permute-start(bf16[192,768]{1,0:T(8,128)(2,1)} %refs_0_.4), channel_id=1, source_target_pairs={{0,16},{1,17},{2,18},{3,19},{4,20},{5,21},{6,22},{7,23},{8,24},{9,... | collective-permute-start | bytes 884744 | tf_op jit(solution)/shard_map/ppermute | solution.py:32
  5.2 13.5 %collective-permute-start.3 = (bf16[192,768]{1,0:T(8,128)(2,1)}, bf16[192,768]{1,0:T(8,128)(2,1)S(1)}, u32[]{:S(2)}, u32[]{:S(2)}) collective-permute-start(bf16[192,768]{1,0:T(8,128)(2,1)} %refs_0_.5), channel_id=1, source_target_pairs={{0,16},{1,17},{2,18},{3,19},{4,20},{5,21},{6,22},{7,23},{8,24},{9,... | collective-permute-start | bytes 884744 | tf_op jit(solution)/shard_map/ppermute | solution.py:32
  5.7 13.4 %collective-permute-start.10 = (bf16[192,768]{1,0:T(8,128)(2,1)}, bf16[192,768]{1,0:T(8,128)(2,1)S(1)}, u32[]{:S(2)}, u32[]{:S(2)}) collective-permute-start(bf16[192,768]{1,0:T(8,128)(2,1)} %refs_0_.4), channel_id=1, source_target_pairs={{0,4},{1,5},{2,6},{3,7},{4,0},{5,1},{6,2},{7,3},{8,12},{9,13},{10,... | collective-permute-start | bytes 884744 | tf_op jit(solution)/shard_map/ppermute | solution.py:32
  5.7 15.0 %collective-permute-start.1 = (bf16[192,768]{1,0:T(8,128)(2,1)}, bf16[192,768]{1,0:T(8,128)(2,1)S(1)}, u32[]{:S(2)}, u32[]{:S(2)}) collective-permute-start(bf16[192,768]{1,0:T(8,128)(2,1)} %refs_0_.5), channel_id=1, source_target_pairs={{0,8},{1,9},{2,10},{3,11},{4,12},{5,13},{6,14},{7,15},{8,0},{9,1},... | collective-permute-start | bytes 884744 | tf_op jit(solution)/shard_map/ppermute | solution.py:32
  11.7 9.0 %collective-permute-start = (bf16[192,768]{1,0:T(8,128)(2,1)}, bf16[192,768]{1,0:T(8,128)(2,1)S(1)}, u32[]{:S(2)}, u32[]{:S(2)}) collective-permute-start(bf16[192,768]{1,0:T(8,128)(2,1)} %refs_0_.5), channel_id=1, source_target_pairs={{0,4},{1,5},{2,6},{3,7},{4,0},{5,1},{6,2},{7,3},{8,12},{9,13},{10,... | collective-permute-start | bytes 884744 | tf_op jit(solution)/shard_map/ppermute | solution.py:32
  13.8 7.5 %collective-permute-start.12 = (bf16[192,768]{1,0:T(8,128)(2,1)S(1)}, bf16[192,768]{1,0:T(8,128)(2,1)S(1)}, u32[]{:S(2)}, u32[]{:S(2)}) collective-permute-start(bf16[192,768]{1,0:T(8,128)(2,1)S(1)} %collective-permute-done.11.refs_2_), channel_id=1, source_target_pairs={{0,4},{1,5},{2,6},{3,7},{4,0},{5,1},{6,2},{7,3},{8,12},{9,13},{10,... | collective-permute-start | bytes 884744 | tf_op jit(solution)/shard_map/ppermute | solution.py:32
  18.7 7.6 %collective-permute-start.5 = (bf16[192,768]{1,0:T(8,128)(2,1)S(1)}, bf16[192,768]{1,0:T(8,128)(2,1)S(1)}, u32[]{:S(2)}, u32[]{:S(2)}) collective-permute-start(bf16[192,768]{1,0:T(8,128)(2,1)S(1)} %collective-permute-done.3.refs_4_), channel_id=1, source_target_pairs={{0,8},{1,9},{2,10},{3,11},{4,12},{5,13},{6,14},{7,15},{8,0},{9,1},... | collective-permute-start | bytes 884744 | tf_op jit(solution)/shard_map/ppermute | solution.py:32
  19.0 7.7 %collective-permute-start.15 = (bf16[192,768]{1,0:T(8,128)(2,1)S(1)}, bf16[192,768]{1,0:T(8,128)(2,1)}, u32[]{:S(2)}, u32[]{:S(2)}) collective-permute-start(bf16[192,768]{1,0:T(8,128)(2,1)S(1)} %collective-permute-done.11.refs_2_), channel_id=1, source_target_pairs={{0,16},{1,17},{2,18},{3,19},{4,20},{5,21},{6,22},{7,23},{8,24},{9,... | collective-permute-start | bytes 884744 | tf_op jit(solution)/shard_map/ppermute | solution.py:32
  20.7 14.6 %collective-permute-start.14 = (bf16[192,768]{1,0:T(8,128)(2,1)S(1)}, bf16[192,768]{1,0:T(8,128)(2,1)S(1)}, u32[]{:S(2)}, u32[]{:S(2)}) collective-permute-start(bf16[192,768]{1,0:T(8,128)(2,1)S(1)} %collective-permute-done.13.refs_4_), channel_id=1, source_target_pairs={{0,4},{1,5},{2,6},{3,7},{4,0},{5,1},{6,2},{7,3},{8,12},{9,13},{10,... | collective-permute-start | bytes 884744 | tf_op jit(solution)/shard_map/ppermute | solution.py:32
  20.7 16.3 %collective-permute-start.4 = (bf16[192,768]{1,0:T(8,128)(2,1)S(1)}, bf16[192,768]{1,0:T(8,128)(2,1)S(1)}, u32[]{:S(2)}, u32[]{:S(2)}) collective-permute-start(bf16[192,768]{1,0:T(8,128)(2,1)S(1)} %collective-permute-done.3.refs_4_), channel_id=1, source_target_pairs={{0,4},{1,5},{2,6},{3,7},{4,0},{5,1},{6,2},{7,3},{8,12},{9,13},{10,... | collective-permute-start | bytes 884744 | tf_op jit(solution)/shard_map/ppermute | solution.py:32
  21.2 18.0 %collective-permute-start.2 = (bf16[192,768]{1,0:T(8,128)(2,1)S(1)}, bf16[192,768]{1,0:T(8,128)(2,1)S(1)}, u32[]{:S(2)}, u32[]{:S(2)}) collective-permute-start(bf16[192,768]{1,0:T(8,128)(2,1)S(1)} %collective-permute-done.1.refs_2_), channel_id=1, source_target_pairs={{0,4},{1,5},{2,6},{3,7},{4,0},{5,1},{6,2},{7,3},{8,12},{9,13},{10,... | collective-permute-start | bytes 884744 | tf_op jit(solution)/shard_map/ppermute | solution.py:32
  26.3 15.3 %collective-permute-start.6 = (bf16[192,768]{1,0:T(8,128)(2,1)S(1)}, bf16[192,768]{1,0:T(8,128)(2,1)}, u32[]{:S(2)}, u32[]{:S(2)}) collective-permute-start(bf16[192,768]{1,0:T(8,128)(2,1)S(1)} %collective-permute-done.5.refs_6_), channel_id=1, source_target_pairs={{0,4},{1,5},{2,6},{3,7},{4,0},{5,1},{6,2},{7,3},{8,12},{9,13},{10,... | collective-permute-start | bytes 884744 | tf_op jit(solution)/shard_map/ppermute | solution.py:32
  26.8 31.8 %collective-permute-start.16 = (bf16[192,768]{1,0:T(8,128)(2,1)}, bf16[192,768]{1,0:T(8,128)(2,1)}, u32[]{:S(2)}, u32[]{:S(2)}) collective-permute-start(bf16[192,768]{1,0:T(8,128)(2,1)} %collective-permute-done.15.refs_5_), channel_id=1, source_target_pairs={{0,4},{1,5},{2,6},{3,7},{4,0},{5,1},{6,2},{7,3},{8,12},{9,13},{10,... | collective-permute-start | bytes 884744 | tf_op jit(solution)/shard_map/ppermute | solution.py:32
  35.4 10.0 %collective-permute-start.7 = (bf16[832,128]{1,0:T(8,128)(2,1)S(1)}, bf16[832,128]{1,0:T(8,128)(2,1)S(1)}, u32[]{:S(2)}, u32[]{:S(2)}) collective-permute-start(bf16[832,128]{1,0:T(8,128)(2,1)S(1)} %shard_map.159.refs_0_), channel_id=1, source_target_pairs={{0,1},{1,2},{2,3},{3,0},{4,5},{5,6},{6,7},{7,4},{8,9},{9,10},{10,1... | collective-permute-start | bytes 638984 | tf_op jit(solution)/shard_map/ppermute | solution.py:32
  37.0 11.8 %collective-permute-start.9 = (bf16[832,128]{1,0:T(8,128)(2,1)S(1)}, bf16[832,128]{1,0:T(8,128)(2,1)S(1)}, u32[]{:S(2)}, u32[]{:S(2)}) collective-permute-start(bf16[832,128]{1,0:T(8,128)(2,1)S(1)} %shard_map.159.refs_0_), channel_id=1, source_target_pairs={{0,3},{1,0},{2,1},{3,2},{4,7},{5,4},{6,5},{7,6},{8,11},{9,8},{10,9... | collective-permute-start | bytes 638984 | tf_op jit(solution)/shard_map/ppermute | solution.py:32
  39.2 19.3 %collective-permute-start.8 = (bf16[832,128]{1,0:T(8,128)(2,1)S(1)}, bf16[832,128]{1,0:T(8,128)(2,1)S(1)}, u32[]{:S(2)}, u32[]{:S(2)}) collective-permute-start(bf16[832,128]{1,0:T(8,128)(2,1)S(1)} %shard_map.159.refs_0_), channel_id=1, source_target_pairs={{0,2},{1,3},{2,0},{3,1},{4,6},{5,7},{6,4},{7,5},{8,10},{9,11},{10,... | collective-permute-start | bytes 638984 | tf_op jit(solution)/shard_map/ppermute | solution.py:32
  61.6 19.9 %copy-start.13 = (bf16[256,1024]{1,0:T(8,128)(2,1)S(1)}, bf16[256,1024]{1,0:T(8,128)(2,1)}, u32[]{:S(2)}) copy-start(bf16[256,1024]{1,0:T(8,128)(2,1)} %win_ref.1) | copy-start | bytes 1572868
  61.6 6.4 %collective-permute-start.19 = (bf16[272,256]{1,0:T(8,128)(2,1)S(1)}, bf16[272,256]{1,0:T(8,128)(2,1)S(1)}, u32[]{:S(2)}, u32[]{:S(2)}) collective-permute-start(bf16[272,256]{1,0:T(8,128)(2,1)S(1)} %get-tuple-element.27), channel_id=1, source_target_pairs={{0,3},{1,0},{2,1},{3,2},{4,7},{5,4},{6,5},{7,6},{8,11},{9,8},{10,9... | collective-permute-start | bytes 417800 | tf_op jit(solution)/shard_map/ppermute | solution.py:32
  63.2 11.7 %collective-permute-start.20 = (bf16[272,256]{1,0:T(8,128)(2,1)S(1)}, bf16[272,256]{1,0:T(8,128)(2,1)S(1)}, u32[]{:S(2)}, u32[]{:S(2)}) collective-permute-start(bf16[272,256]{1,0:T(8,128)(2,1)S(1)} %get-tuple-element.28), channel_id=1, source_target_pairs={{0,2},{1,3},{2,0},{3,1},{4,6},{5,7},{6,4},{7,5},{8,10},{9,11},{10,... | collective-permute-start | bytes 417800 | tf_op jit(solution)/shard_map/ppermute | solution.py:32
  63.2 11.7 %collective-permute-start.21 = (bf16[272,256]{1,0:T(8,128)(2,1)S(1)}, bf16[272,256]{1,0:T(8,128)(2,1)S(1)}, u32[]{:S(2)}, u32[]{:S(2)}) collective-permute-start(bf16[272,256]{1,0:T(8,128)(2,1)S(1)} %get-tuple-element.29), channel_id=1, source_target_pairs={{0,1},{1,2},{2,3},{3,0},{4,5},{5,6},{6,7},{7,4},{8,9},{9,10},{10,1... | collective-permute-start | bytes 417800 | tf_op jit(solution)/shard_map/ppermute | solution.py:32
  75.0 2.9 %collective-permute-start.22 = (bf16[48,256]{1,0:T(8,128)(2,1)S(1)}, bf16[48,256]{1,0:T(8,128)(2,1)S(1)}, u32[]{:S(2)}, u32[]{:S(2)}) collective-permute-start(bf16[48,256]{1,0:T(8,128)(2,1)S(1)} %get-tuple-element.32), channel_id=1, source_target_pairs={{0,4},{1,5},{2,6},{3,7},{4,8},{5,9},{6,10},{7,11},{8,12},{9,13},{1... | collective-permute-start | bytes 73736 | tf_op jit(solution)/shard_map/ppermute | solution.py:32
  76.5 4.9 %collective-permute-start.23 = (bf16[48,256]{1,0:T(8,128)(2,1)S(1)}, bf16[48,256]{1,0:T(8,128)(2,1)S(1)}, u32[]{:S(2)}, u32[]{:S(2)}) collective-permute-start(bf16[48,256]{1,0:T(8,128)(2,1)S(1)} %get-tuple-element.33), channel_id=1, source_target_pairs={{4,0},{5,1},{6,2},{7,3},{8,4},{9,5},{10,6},{11,7},{12,8},{13,9},{1... | collective-permute-start | bytes 73736 | tf_op jit(solution)/shard_map/ppermute | solution.py:32
  85.1 6.8 %collective-permute-start.24 = (bf16[4,256,256]{2,1,0:T(8,128)(2,1)}, bf16[4,256,256]{2,1,0:T(8,128)(2,1)}, u32[]{:S(2)}, u32[]{:S(2)}) collective-permute-start(bf16[4,256,256]{2,1,0:T(8,128)(2,1)} %get-tuple-element.36), channel_id=1, source_target_pairs={{0,4},{1,5},{2,6},{3,7},{4,0},{5,1},{6,2},{7,3},{8,12},{9,13},{10,... | collective-permute-start | bytes 1572872 | tf_op jit(solution)/shard_map/ppermute | solution.py:32
  91.2 19.7 %collective-permute-start.17 = (bf16[256,1536]{1,0:T(8,128)(2,1)}, bf16[256,1536]{1,0:T(8,128)(2,1)S(1)}, u32[]{:S(2)}, u32[]{:S(2)}) collective-permute-start(bf16[256,1536]{1,0:T(8,128)(2,1)} %get-tuple-element.24), channel_id=1, source_target_pairs={{0,1},{1,0},{2,3},{3,2},{4,5},{5,4},{6,7},{7,6},{8,9},{9,8},{10,11... | collective-permute-start | bytes 2359304 | tf_op jit(solution)/shard_map/ppermute | solution.py:32
  93.1 20.5 %collective-permute-start.25 = (bf16[256,256]{1,0:T(8,128)(2,1)S(1)}, bf16[256,256]{1,0:T(8,128)(2,1)S(1)}, u32[]{:S(2)}, u32[]{:S(2)}) collective-permute-start(bf16[256,256]{1,0:T(8,128)(2,1)S(1)} %get-tuple-element.37), channel_id=1, source_target_pairs={{0,8},{1,9},{2,10},{3,11},{4,12},{5,13},{6,14},{7,15},{8,0},{9,1},... | collective-permute-start | bytes 393224 | tf_op jit(solution)/shard_map/ppermute | solution.py:32
  95.5 18.1 %collective-permute-start.26 = (bf16[256,256]{1,0:T(8,128)(2,1)S(1)}, bf16[256,256]{1,0:T(8,128)(2,1)S(1)}, u32[]{:S(2)}, u32[]{:S(2)}) collective-permute-start(bf16[256,256]{1,0:T(8,128)(2,1)S(1)} %get-tuple-element.39), channel_id=1, source_target_pairs={{0,16},{1,17},{2,18},{3,19},{4,20},{5,21},{6,22},{7,23},{8,24},{9,... | collective-permute-start | bytes 393224 | tf_op jit(solution)/shard_map/ppermute | solution.py:32
  95.6 18.1 %collective-permute-start.27 = (bf16[256,256]{1,0:T(8,128)(2,1)S(1)}, bf16[256,256]{1,0:T(8,128)(2,1)S(1)}, u32[]{:S(2)}, u32[]{:S(2)}) collective-permute-start(bf16[256,256]{1,0:T(8,128)(2,1)S(1)} %get-tuple-element.38), channel_id=1, source_target_pairs={{0,24},{1,25},{2,26},{3,27},{4,28},{5,29},{6,30},{7,31},{8,16},{9,... | collective-permute-start | bytes 393224 | tf_op jit(solution)/shard_map/ppermute | solution.py:32
  111.0 23.0 %collective-permute-start.18 = (bf16[128,1536]{1,0:T(8,128)(2,1)S(1)}, bf16[128,1536]{1,0:T(8,128)(2,1)S(1)}, u32[]{:S(2)}, u32[]{:S(2)}) collective-permute-start(bf16[128,1536]{1,0:T(8,128)(2,1)S(1)} %add_convert_fusion.1), channel_id=1, source_target_pairs={{0,2},{1,3},{2,0},{3,1},{4,6},{5,7},{6,4},{7,5},{8,10},{9,11},{10,... | collective-permute-start | bytes 1179656 | tf_op jit(solution)/shard_map/ppermute | solution.py:32
  113.7 9.0 %collective-permute-start.28 = (bf16[64,256]{1,0:T(8,128)(2,1)S(1)}, bf16[64,256]{1,0:T(8,128)(2,1)S(1)}, u32[]{:S(2)}, u32[]{:S(2)}) collective-permute-start(bf16[64,256]{1,0:T(8,128)(2,1)S(1)} %get-tuple-element.40), channel_id=1, source_target_pairs={{0,3},{1,0},{2,1},{3,2},{4,7},{5,4},{6,5},{7,6},{8,11},{9,8},{10,9... | collective-permute-start | bytes 98312 | tf_op jit(solution)/shard_map/ppermute | solution.py:32
  114.2 19.1 %collective-permute-start.29 = (bf16[64,256]{1,0:T(8,128)(2,1)S(1)}, bf16[64,256]{1,0:T(8,128)(2,1)S(1)}, u32[]{:S(2)}, u32[]{:S(2)}) collective-permute-start(bf16[64,256]{1,0:T(8,128)(2,1)S(1)} %get-tuple-element.42), channel_id=1, source_target_pairs={{0,2},{1,3},{2,0},{3,1},{4,6},{5,7},{6,4},{7,5},{8,10},{9,11},{10,... | collective-permute-start | bytes 98312 | tf_op jit(solution)/shard_map/ppermute | solution.py:32
  115.5 17.8 %collective-permute-start.30 = (bf16[64,256]{1,0:T(8,128)(2,1)S(1)}, bf16[64,256]{1,0:T(8,128)(2,1)S(1)}, u32[]{:S(2)}, u32[]{:S(2)}) collective-permute-start(bf16[64,256]{1,0:T(8,128)(2,1)S(1)} %get-tuple-element.41), channel_id=1, source_target_pairs={{0,1},{1,2},{2,3},{3,0},{4,5},{5,6},{6,7},{7,4},{8,9},{9,10},{10,1... | collective-permute-start | bytes 98312 | tf_op jit(solution)/shard_map/ppermute | solution.py:32
  (17 other events, 129.0 us)

commit v2 on v1

--- a/solution.py
+++ b/solution.py
@@ -63,7 +63,7 @@
     return sorted(held.items())
 
 
-def call(body, outs, args, specs=None, scratch=(), flops=0, moved=0, tanhs=0):
+def call(body, outs, args, specs=None, scratch=(), flops=0, moved=0, tanhs=0, grant=20):
     return pl.pallas_call(
         body,
         out_shape=[jax.ShapeDtypeStruct(*o) for o in outs],
@@ -73,7 +73,7 @@
         cost_estimate=pl.CostEstimate(
             flops=int(flops), bytes_accessed=int(moved), transcendentals=int(tanhs)
         ),
-        compiler_params=pltpu.CompilerParams(vmem_limit_bytes=20 * 2**20),
+        compiler_params=pltpu.CompilerParams(vmem_limit_bytes=grant * 2**20),
     )(*args)
 
 
@@ -91,13 +91,12 @@
     return x * half, slope
 
 
-def norm_body(depth, id_ref, x_ref, gain_ref, proj_ref, out_ref, own_ref):
+def norm_body(depth, id_ref, x_ref, gain_ref, out_ref, own_ref):
     wide = x_ref[...].astype(f32)
     scale = lax.rsqrt(jnp.mean(wide * wide, axis=-1, keepdims=True) + epsilon)
     out_ref[...] = (wide * scale * gain_ref[...].reshape(1, -1)).astype(bf16)
     own = own_ref.shape[0]
-    mine = pl.ds(pl.multiple_of((id_ref[0] % depth) * own, own), own)
-    own_ref[...] = jnp.dot(x_ref[mine, :], proj_ref[...], preferred_element_type=f32)
+    own_ref[...] = x_ref[pl.ds(pl.multiple_of((id_ref[0] % depth) * own, own), own), :]
 
 
 def edge_columns(flat, tile_x, tile_y):
@@ -105,26 +104,25 @@
     return grid[:, 0], grid[:, tile_y - 1]
 
 
-def payload_rows(sources, rows, tile_x, halves):
-    at_index = sources * rows
-    at_state = at_index + -(-sources // 16) * 16
+def edge_rows(sources, tile_x, halves):
+    at_state = -(-sources // 16) * 16
     at_depth = at_state + 2 * halves * tile_x
-    return at_index, at_state, at_depth, at_depth + 2 * tile_x
-
-
-def prep_body(tile_x, tile_y, index_ref, weight_ref, state_ref, depth_ref, out_ref):
-    sources, rows, inner = weight_ref.shape
-    per_block = index_ref.shape[1]
+    return at_state, at_depth, at_depth + 2 * tile_x
+
+
+def prep_body(index_ref, state_ref, depth_ref, out_ref, wet_ref):
+    tile_x, tile_y = depth_ref.shape
+    blocks, per_block = index_ref.shape
+    inner = out_ref.shape[1]
     channels = state_ref.shape[1]
     halves = channels // inner
-    at_index, at_state, at_depth, _ = payload_rows(sources, rows, tile_x, halves)
-    for n in range(sources):
-        out_ref[n * rows : (n + 1) * rows, :] = weight_ref[n]
-    row = lax.broadcasted_iota(jnp.int32, (at_state - at_index, inner), 0)
+    at_state, at_depth, _ = edge_rows(blocks * per_block, tile_x, halves)
+    row = lax.broadcasted_iota(jnp.int32, (at_state, inner), 0)
     table = jnp.zeros(row.shape, jnp.int32)
-    for n in range(sources):
-        table = jnp.where(row == n, index_ref[n // per_block, n % per_block], table)
-    out_ref[at_index:at_state, :] = table.astype(f32).astype(bf16)
+    for b in range(blocks):
+        for k in range(per_block):
+            table = jnp.where(row == b * per_block + k, index_ref[b, k], table)
+    out_ref[:at_state, :] = table.astype(f32).astype(bf16)
     first, last = edge_columns(state_ref[...].astype(f32), tile_x, tile_y)
     edges = [e[:, h * inner : (h + 1) * inner] for e in (last, first) for h in range(halves)]
     out_ref[at_state:at_depth, :] = jnp.concatenate(edges, axis=0).astype(bf16)
@@ -133,15 +131,21 @@
         jnp.broadcast_to(deep[:, at : at + 1], (tile_x, inner)) for at in (tile_y - 1, 0)
     ]
     out_ref[at_depth:, :] = jnp.concatenate(edges, axis=0).astype(bf16)
-
-
-def build_matrix(per_block, sources, rows, at_index, load_ref, out_ref):
-    inner = load_ref.shape[1]
+    level = lax.broadcasted_iota(jnp.int32, (tile_y, channels), 1) // (channels // LEV)
+    down = deep.T
+    for x in range(tile_x):
+        wet = jnp.where(level.astype(f32) < down[:, x : x + 1], 1.0, 0.0)
+        wet_ref[x * tile_y : (x + 1) * tile_y, :] = wet.astype(bf16)
+
+
+def build_matrix(blocks, weight_ref, edge_ref, out_ref):
+    sources, rows, inner = weight_ref.shape
+    per_block = sources // blocks
     count = out_ref.shape[1] // inner
-    for b in range(sources // per_block):
+    for b in range(blocks):
         taken = range(b * per_block, (b + 1) * per_block)
-        values = [load_ref[n * rows : (n + 1) * rows, :].astype(f32) for n in taken]
-        picks = [load_ref[at_index + n : at_index + n + 1, :].astype(f32) for n in taken]
+        values = [weight_ref[n].astype(f32) for n in taken]
+        picks = [edge_ref[n : n + 1, :].astype(f32) for n in taken]
         for j in range(count):
             total = jnp.zeros((rows, inner), f32)
             for value, pick in zip(values, picks):
@@ -189,7 +193,7 @@
 def first_body(
     pieces, rows, depth, tile_x, tile_y, remap, early, id_ref, x_ref, own_ref, both_ref, *refs
 ):
-    mats, refs = refs[:depth], refs[depth:]
+    mats, tables, refs = refs[:depth], refs[depth : 2 * depth], refs[2 * depth :]
     sums, refs = refs[: int(early)], refs[int(early) :]
     blocks, refs = refs[: len(pieces)], refs[len(pieces) :]
     hid_ref, moved, refs = refs[0], refs[1 : depth + 1], refs[depth + 1 :]
@@ -198,7 +202,7 @@
     z = id_ref[0] % depth
     place_blocks(me, pieces, blocks, rows, full, True)
     for k in range(depth):
-        build_matrix(*remap, mats[k], dense[k])
+        build_matrix(remap, mats[k], tables[k], dense[k])
     width = hid_ref.shape[1]
     step = 256 if width % 256 == 0 else width
     total = jnp.zeros(flux.shape, f32)
@@ -224,12 +228,23 @@
         moved[k][cells:, :] = jnp.concatenate(sides, axis=0).astype(bf16)
 
 
-def both_body(pieces, rows, depth, id_ref, proj_ref, *refs):
-    blocks, (out_ref, full) = refs[:-2], refs[-2:]
+def both_body(pieces, rows, depth, id_ref, proj_ref, own_ref, *refs):
+    blocks, (out_ref, flux_ref, full) = refs[:-3], refs[-3:]
     place_blocks(id_ref[0] // depth, pieces, blocks, rows, full, False)
     out_ref[...] = lax.dot_general(
         proj_ref[...], full[...], TN, preferred_element_type=f32
     ).astype(bf16)
+    flux_ref[...] = jnp.dot(own_ref[...], proj_ref[...], preferred_element_type=f32)
+
+
+def back_body(wet_ref, cot_ref, wout_ref, dout_ref, dact_ref):
+    dout = (cot_ref[...].astype(f32) * wet_ref[...].astype(f32)).astype(bf16)
+    dout_ref[...] = dout
+    step = dact_ref.shape[1] // 4
+    for at in range(0, dact_ref.shape[1], step):
+        dact_ref[:, at : at + step] = lax.dot_general(
+            dout, wout_ref[at : at + step, :], NT, preferred_element_type=f32
+        )
 
 
 def second_body(pieces, rows, depth, shards, id_ref, hid_ref, *refs):
@@ -262,7 +277,7 @@
     total = total.astype(bf16).astype(f32)
     field = ((state_ref[...].astype(f32) + total[:cells]) * wet_ref[...].astype(f32)).astype(bf16)
     field_ref[...] = field
-    _, at_state, at_depth, _ = rows_at
+    at_state, at_depth, _ = rows_at
     inner = west_ref.shape[1]
     halves = channels // inner
     level = lax.broadcasted_iota(jnp.int32, (tile_x, channels), 1) // (channels // LEV)
@@ -295,7 +310,7 @@
 
 
 def ocean_body(
-    depth, tile_x, tile_y, split, id_ref, field_ref, side_ref, top_ref, low_ref, wet_ref, dout_ref,
+    depth, tile_x, tile_y, split, id_ref, field_ref, side_ref, top_ref, low_ref, wet_ref, dout_ref, dact_ref,
     kern_ref, gain_ref, win_ref, wout_ref, *refs
 ):
     out_ref, refs = refs[0], refs[1:]
@@ -334,8 +349,7 @@
         value, slope = gelu_both(pre)
         act = value.astype(bf16)
         total = total + jnp.dot(act, wout_ref[span, :], preferred_element_type=f32)
-        dact = lax.dot_general(dout, wout_ref[span, :], NT, preferred_element_type=f32)
-        dpre = (dact * slope).astype(bf16)
+        dpre = (dact_ref[:, span] * slope).astype(bf16)
         grads = (
             lax.dot_general(dpre, normed, TN, preferred_element_type=f32),
             lax.dot_general(act, dout, TN, preferred_element_type=f32),
@@ -355,6 +369,32 @@
                 refs[1][spot] = grad.astype(bf16)
 
     out_ref[...] = ((field_ref[...].astype(f32) + total) * wet).astype(bf16)
+
+
+def plane_body(depth, id_ref, keep_ref, got_ref, own_ref, *outs):
+    place = id_ref[0] // depth // 2
+    for mask, ref in enumerate((own_ref,) + outs):
+        spot = place ^ mask
+        ref[...] = (keep_ref[spot] + got_ref[spot].astype(f32)).astype(ref.dtype)
+
+
+def line_body(depth, id_ref, own_ref, a_ref, b_ref, c_ref, *refs):
+    outs, total = refs[:-1], refs[-1]
+    z = id_ref[0] % depth
+    arrived = a_ref[...].astype(f32) + b_ref[...].astype(f32) + c_ref[...].astype(f32)
+    total[...] = own_ref[...] + arrived
+    rows = total.shape[0] // depth
+    for k, ref in enumerate(outs):
+        start = pl.multiple_of(((z - k + depth) % depth) * rows, rows)
+        ref[...] = total[pl.ds(start, rows), :].astype(ref.dtype)
+
+
+def sum_body(*refs):
+    out_ref = refs[-1]
+    total = refs[0][...].astype(f32)
+    for ref in refs[1:-1]:
+        total = total + ref[...].astype(f32)
+    out_ref[...] = total.astype(out_ref.dtype)
 
 
 def step(
@@ -387,38 +427,36 @@
 
     second = gather_rows(w_second, "yx")
     first = gather_rows(w_first, "xy")
-    own_rows = lax.dynamic_slice_in_dim(atmos_state, (me[0] % depth) * own, own, 0)
-
-    levels = jnp.arange(channels, dtype=jnp.int32) // (channels // LEV)
-    wet = (levels[None, :] < depth_levels.reshape(cells)[:, None]).astype(bf16)
     state = ocean_state.reshape(cells, channels)
     blocks, per_block, block_rows, inner = remap_weight.shape
-    sources = blocks * per_block
-    rows_at = payload_rows(sources, block_rows, tile_x, channels // inner)
-    (payload,) = call(
-        functools.partial(prep_body, tile_x, tile_y),
-        [((rows_at[3], inner), bf16)],
-        (remap_index, remap_weight.reshape(sources, block_rows, inner), state, depth_levels),
-        specs=[SMEM, VMEM, VMEM, VMEM],
+    rows_at = edge_rows(blocks * per_block, tile_x, channels // inner)
+    weights = remap_weight.reshape(blocks * per_block, block_rows, inner)
+    steps = range(1, depth)
+    mats = [weights] + [send(weights, shift_z(k)) for k in steps]
+    edge, wet = call(
+        prep_body,
+        [((rows_at[2], inner), bf16), ((cells, channels), bf16)],
+        (remap_index, state, depth_levels),
+        specs=[SMEM, VMEM, VMEM],
         moved=mb,
     )
-    payloads = [payload] + [send(payload, shift_z(k)) for k in range(1, depth)]
-    normed, own_flux = call(
+    edges = [edge] + [send(edge, shift_z(k)) for k in steps]
+    normed, own_rows = call(
         functools.partial(norm_body, depth),
-        [((tokens, model), bf16), ((own, channels), f32)],
-        (me, atmos_state, atmos_gain, flux_proj),
-        specs=[SMEM] + [VMEM] * 3,
+        [((tokens, model), bf16), ((own, model), bf16)],
+        (me, atmos_state, atmos_gain),
+        specs=[SMEM, VMEM, VMEM],
         moved=4 * mb,
     )
 
     rows = w_second.shape[0]
     second_at = [p[0] for p in second]
     second = [p[1] for p in second]
-    (both,) = call(
+    both, own_flux = call(
         functools.partial(both_body, second_at, rows, depth),
-        [((channels, share), bf16)],
-        (me, flux_proj, *second),
-        specs=[SMEM, VMEM] + [VMEM] * len(second),
+        [((channels, share), bf16), ((own, channels), f32)],
+        (me, flux_proj, own_rows, *second),
+        specs=[SMEM, VMEM, VMEM] + [VMEM] * len(second),
         scratch=[pltpu.VMEM((model, share), bf16)],
         flops=2 * model * share * channels,
         moved=3 * mb,
@@ -447,12 +485,12 @@
             depth,
             tile_x,
             tile_y,
-            (per_block, sources, block_rows, rows_at[0]),
+            blocks,
             early,
         ),
         [((tokens, share), bf16)] + [((cells + 2 * tile_x, channels), bf16)] * depth,
-        (me, normed, own_flux, both, *payloads, *sums, *[p[1] for p in first]),
-        specs=[SMEM] + [VMEM] * (3 + depth + len(sums)) + [VMEM] * len(first),
+        (me, normed, own_flux, both, *mats, *edges, *sums, *[p[1] for p in first]),
+        specs=[SMEM] + [VMEM] * (3 + 2 * depth + len(sums)) + [VMEM] * len(first),
         scratch=[
             pltpu.VMEM((2 * rows if early else model, share), bf16),
             pltpu.VMEM((tokens, channels), f32),
@@ -471,7 +509,8 @@
         shards = [
             [lambda z: z],
             [lambda z: z ^ 2],
-            [lambda z: z ^ 1, lambda z: z ^ 3],
+            [lambda z: z ^ 3],
+            [lambda z: z ^ 1],
         ]
     else:
         shards = [[lambda z, k=k: (z - k + depth) % depth] for k in range(depth)]
@@ -488,21 +527,29 @@
         moved=6 * mb,
     )
     if pairwise:
-        mine, far, give = parts
-        got = send(give, lambda group, z: (group, z ^ 1))
-        far = (far.astype(f32) + got[own:].astype(f32)).astype(bf16)
-        parts = [mine, got[:own], send(far, lambda group, z: (group, z ^ 2))]
+        mine, far, give_far, give_near = parts
+        near_z = lambda group, z: (group, z ^ 1)
+        got_far = send(give_far, near_z)
+        got_near = send(give_near, near_z)
+        (far,) = call(sum_body, [((own, model), bf16)], (far, got_far), moved=mb)
+        parts = [mine, got_near, send(far, lambda group, z: (group, z ^ 2))]
     else:
         parts = [parts[0]] + [send(parts[k], shift_z(-k)) for k in range(1, depth)]
 
-    dout = (ocean_cotangent.reshape(cells, channels).astype(f32) * wet.astype(f32)).astype(bf16)
+    dout, dact = call(
+        back_body,
+        [((cells, channels), bf16), ((cells, hid), f32)],
+        (wet, ocean_cotangent.reshape(cells, channels), ocean_w_out),
+        flops=2 * cells * channels * hid,
+        moved=2 * mb,
+    )
 
     line = -(-(tile_y + 2) // 16) * 16
     field, side, row_first, row_last = call(
         functools.partial(field_body, depth, tile_x, tile_y, rows_at),
         [((cells, channels), bf16), ((2 * tile_x, channels), bf16)]
         + [((line, channels), bf16)] * 2,
-        (me, state, wet, payloads[1], payloads[depth - 1], *moved),
+        (me, state, wet, edges[1], edges[depth - 1], *moved),
         specs=[SMEM] + [VMEM] * (4 + depth),
         moved=mb,
     )
@@ -524,47 +571,48 @@
             low,
             wet,
             dout,
+            dact,
             conv_kernel,
             ocean_gain,
             ocean_w_in,
             ocean_w_out,
         ),
-        specs=[SMEM] + [VMEM] * 10,
+        specs=[SMEM] + [VMEM] * 11,
         scratch=[pltpu.VMEM((tile_x + 2, tile_y + 16, channels), f32)],
-        flops=10 * cells * channels * hid,
+        flops=8 * cells * channels * hid,
         moved=5 * mb,
         tanhs=cells * hid,
     )
     ocean_out = outs[0].reshape(tile_x, tile_y, channels)
     if split:
         keep, give = outs[1:]
-        place = me[0] // depth // 2
-
-        def quarter(mask):
-            return lax.dynamic_index_in_dim(terms, place ^ mask, 0, keepdims=False)
-
-        terms = keep + send(give, flip(1)).astype(f32)
-        arrived = [send(quarter(m).astype(bf16), flip(2 * m)) for m in (1, 2, 3)]
-        total = quarter(0)
-        for piece in arrived:
-            total = total + piece.astype(f32)
-        total = total.reshape(depth, -1, channels)
-        z = me[0] % depth
-
-        def slab(k):
-            return lax.dynamic_index_in_dim(total, (z - k) % depth, 0, keepdims=False)
-
-        arrived = [send(slab(k).astype(bf16), shift_z(-k)) for k in range(1, depth)]
-        weight_grads = slab(0)
-        for piece in arrived:
-            weight_grads = weight_grads + piece.astype(f32)
+        got = send(give, flip(1))
+        rows = hid // 4
+        plane = call(
+            functools.partial(plane_body, depth),
+            [((rows, channels), f32)] + [((rows, channels), bf16)] * 3,
+            (me, keep, got),
+            specs=[SMEM, VMEM, VMEM],
+            moved=2 * mb,
+        )
+        arrived = [send(plane[m], flip(2 * m)) for m in (1, 2, 3)]
+        rows = rows // depth
+        slabs = call(
+            functools.partial(line_body, depth),
+            [((rows, channels), f32)] + [((rows, channels), bf16)] * (depth - 1),
+            (me, plane[0], *arrived),
+            specs=[SMEM] + [VMEM] * 4,
+            scratch=[pltpu.VMEM((rows * depth, channels), f32)],
+            moved=mb,
+        )
+        arrived = [send(slabs[k], shift_z(-k)) for k in range(1, depth)]
+        (weight_grads,) = call(
+            sum_body, [((rows, channels), f32)], (slabs[0], *arrived), moved=mb // 4
+        )
     else:
         weight_grads = lax.psum_scatter(outs[1], ALL, scatter_dimension=0, tiled=True)
 
-    total = own_rows.astype(f32)
-    for part in parts:
-        total = total + part.astype(f32)
-    atmos_out = total.astype(bf16)
+    (atmos_out,) = call(sum_body, [((own, model), bf16)], (own_rows, *parts), moved=2 * mb)
     return (atmos_out, ocean_out, weight_grads)
 
 

time: 136 us -> 109 us (0.80)
  waiting for transfers between devices: 78.8 us -> 49.6 us
  starting transfers between devices: 29.7 us -> 36.7 us
  other arithmetic: 4.1 us -> 0 us
  local copies, waits for them, and re-layouts: 7.32 us -> 4.75 us
  Pallas kernels: 15.1 us -> 16.9 us
    ppermute x31 -> x35, waiting for transfers between devices: 78.8 us -> 49.6 us  [send(): return lax.ppermute(value, ALL, pairs)]
    ppermute x31 -> x35, starting transfers between devices: 29.7 us -> 36.7 us  [send(): return lax.ppermute(value, ALL, pairs)]
    convert_element_type x4 -> x0, other arithmetic: 2.23 us -> none  [the longest x1 1.93 us: step(): atmos_out = total.astype(bf16)]
    add x3 -> x0, other arithmetic: 1.87 us -> none  [the longest x1 1.15 us: step(): terms = keep + send(give, flip(1)).astype(f32)]
    pallas_call x8 -> x14, Pallas kernels: 15.1 us -> 16.9 us  [call(): pl.pallas_call(body, out_shape=[jax.ShapeDtypeStruct(*o) for o in outs],...]
    unnamed x36 -> x30, local copies, waits for them, and re-layouts: 6.49 us -> 4.75 us
  transfers between devices with their start and end apart: 31 -> 35, of which waited for: 14 -> 12; matrix products, arithmetic and copies ran while one was open for 2% -> 0% of each run, Pallas kernels for 6% -> 12%
where the time goes in v2:
time: 109 us
  waiting for transfers between devices  49.6 us (46%)
  starting transfers between devices  36.7 us (34%)
  Pallas kernels  16.9 us (16%)
  local copies, waits for them, and re-layouts  4.75 us (4%)
    ppermute x35, waiting for transfers between devices, send(): return lax.ppermute(value, ALL, pairs)  49.6 us
    ppermute x35, starting transfers between devices, send(): return lax.ppermute(value, ALL, pairs)  36.7 us
    pallas_call x14, Pallas kernels, call(): pl.pallas_call(body, out_shape=[jax.ShapeDtypeStruct(*o) for o in outs],...  16.9 us
    unnamed x30, local copies, waits for them, and re-layouts  4.75 us
  transfers between devices with their start and end apart: 35, of which 12 were waited for; matrix products, arithmetic and copies ran while one was open for 0% of the time, Pallas kernels for 12%

profile of v2, /device:TPU:0, one launch (start us, length us, event | category | flops | bytes accessed | tf_op | source)
XLA Modules:
  0.0 108.8 jit_solution(779896867872018654)
XLA Ops:
  0.6 3.1 %collective-permute-start.3 = (bf16[192,768]{1,0:T(8,128)(2,1)}, bf16[192,768]{1,0:T(8,128)(2,1)S(1)}, u32[]{:S(2)}, u32[]{:S(2)}) collective-permute-start(bf16[192,768]{1,0:T(8,128)(2,1)} %refs_0_.5), channel_id=1, source_target_pairs={{0,16},{1,17},{2,18},{3,19},{4,20},{5,21},{6,22},{7,23},{8,24},{9,... | collective-permute-start | bytes 884744 | tf_op jit(solution)/shard_map/ppermute | solution.py:32
  3.7 1.5 %collective-permute-start.1 = (bf16[192,768]{1,0:T(8,128)(2,1)}, bf16[192,768]{1,0:T(8,128)(2,1)S(1)}, u32[]{:S(2)}, u32[]{:S(2)}) collective-permute-start(bf16[192,768]{1,0:T(8,128)(2,1)} %refs_0_.5), channel_id=1, source_target_pairs={{0,8},{1,9},{2,10},{3,11},{4,12},{5,13},{6,14},{7,15},{8,0},{9,1},... | collective-permute-start | bytes 884744 | tf_op jit(solution)/shard_map/ppermute | solution.py:32
  8.7 1.6 %collective-permute-start.10 = (bf16[64,128]{1,0:T(8,128)(2,1)S(1)}, bf16[64,128]{1,0:T(8,128)(2,1)S(1)}, u32[]{:S(2)}, u32[]{:S(2)}) collective-permute-start(bf16[64,128]{1,0:T(8,128)(2,1)S(1)} %get-tuple-element.39.refs_4_), channel_id=1, source_target_pairs={{0,1},{1,2},{2,3},{3,0},{4,5},{5,6},{6,7},{7,4},{8,9},{9,10},{10,1... | collective-permute-start | bytes 49160 | tf_op jit(solution)/shard_map/ppermute | solution.py:32
  10.4 4.0 %collective-permute-done.10.refs_5_.west_ref = bf16[64,128]{1,0:T(8,128)(2,1)S(1)} collective-permute-done((bf16[64,128]{1,0:T(8,128)(2,1)S(1)}, bf16[64,128]{1,0:T(8,128)(2,1)S(1)}, u32[]{:S(2)}, u32[]{:S(2)}) %collective-permute-start.10) | collective-permute-done | bytes 16416 | tf_op jit(solution)/shard_map/ppermute | solution.py:32
  14.3 1.8 %collective-permute-start.12 = (bf16[64,128]{1,0:T(8,128)(2,1)S(1)}, bf16[64,128]{1,0:T(8,128)(2,1)S(1)}, u32[]{:S(2)}, u32[]{:S(2)}) collective-permute-start(bf16[64,128]{1,0:T(8,128)(2,1)S(1)} %get-tuple-element.39.refs_4_), channel_id=1, source_target_pairs={{0,3},{1,0},{2,1},{3,2},{4,7},{5,4},{6,5},{7,6},{8,11},{9,8},{10,9... | collective-permute-start | bytes 49160 | tf_op jit(solution)/shard_map/ppermute | solution.py:32
  16.1 1.9 %collective-permute-done.12.refs_7_.east_ref = bf16[64,128]{1,0:T(8,128)(2,1)S(1)} collective-permute-done((bf16[64,128]{1,0:T(8,128)(2,1)S(1)}, bf16[64,128]{1,0:T(8,128)(2,1)S(1)}, u32[]{:S(2)}, u32[]{:S(2)}) %collective-permute-start.12) | collective-permute-done | bytes 16416 | tf_op jit(solution)/shard_map/ppermute | solution.py:32
  18.4 1.8 %collective-permute-start.5 = (bf16[192,768]{1,0:T(8,128)(2,1)S(1)}, bf16[192,768]{1,0:T(8,128)(2,1)S(1)}, u32[]{:S(2)}, u32[]{:S(2)}) collective-permute-start(bf16[192,768]{1,0:T(8,128)(2,1)S(1)} %collective-permute-done.3.refs_4_), channel_id=1, source_target_pairs={{0,8},{1,9},{2,10},{3,11},{4,12},{5,13},{6,14},{7,15},{8,0},{9,1},... | collective-permute-start | bytes 884744 | tf_op jit(solution)/shard_map/ppermute | solution.py:32
  20.3 1.5 %collective-permute-start.18 = (bf16[192,768]{1,0:T(8,128)(2,1)S(1)}, bf16[192,768]{1,0:T(8,128)(2,1)}, u32[]{:S(2)}, u32[]{:S(2)}) collective-permute-start(bf16[192,768]{1,0:T(8,128)(2,1)S(1)} %collective-permute-done.14.refs_2_), channel_id=1, source_target_pairs={{0,16},{1,17},{2,18},{3,19},{4,20},{5,21},{6,22},{7,23},{8,24},{9,... | collective-permute-start | bytes 884744 | tf_op jit(solution)/shard_map/ppermute | solution.py:32
  21.8 5.9 %collective-permute-done.16.refs_4_ = bf16[192,768]{1,0:T(8,128)(2,1)S(1)} collective-permute-done((bf16[192,768]{1,0:T(8,128)(2,1)}, bf16[192,768]{1,0:T(8,128)(2,1)S(1)}, u32[]{:S(2)}, u32[]{:S(2)}) %collective-permute-start.16) | collective-permute-done | bytes 294944 | tf_op jit(solution)/shard_map/ppermute | solution.py:32
  28.7 3.2 %collective-permute-done.18.refs_9_ = bf16[192,768]{1,0:T(8,128)(2,1)} collective-permute-done((bf16[192,768]{1,0:T(8,128)(2,1)S(1)}, bf16[192,768]{1,0:T(8,128)(2,1)}, u32[]{:S(2)}, u32[]{:S(2)}) %collective-permute-start.18) | collective-permute-done | bytes 294944 | tf_op jit(solution)/shard_map/ppermute | solution.py:32
  31.9 4.1 %collective-permute-start.8 = (bf16[6,128,128]{2,1,0:T(8,128)(2,1)}, bf16[6,128,128]{2,1,0:T(8,128)(2,1)}, u32[]{:S(2)}, u32[]{:S(2)}) collective-permute-start(bf16[6,128,128]{2,1,0:T(8,128)(2,1)} %bitcast.8), channel_id=1, source_target_pairs={{0,2},{1,3},{2,0},{3,1},{4,6},{5,7},{6,4},{7,5},{8,10},{9,11},{10,... | collective-permute-start | bytes 589832 | tf_op jit(solution)/shard_map/ppermute | solution.py:32
  36.0 1.4 %copy-done.1 = bf16[512,1536]{1,0:T(8,128)(2,1)S(1)} copy-done((bf16[512,1536]{1,0:T(8,128)(2,1)S(1)}, bf16[512,1536]{1,0:T(8,128)(2,1)}, u32[]{:S(2)}) %copy-start.1) | copy-done | bytes 1572888
  39.1 1.5 %shard_map.160.refs_8_ = f32[512,768]{1,0:T(8,128)S(1)} custom-call(s32[1]{0:T(128)} %bitcast.id_ref, bf16[512,1536]{1,0:T(8,128)(2,1)S(1)} %get-tuple-element.36.x_ref, bf16[192,768]{1,0:T(8,128)(2,1)S(1)} %copy-done.6, bf16[192,768]{1,0:T(8,128)(2,1)S(1)} %collective-permute-done.13.refs_1_, bf16[192,768]{1,0:T(8,128)(2,1)S(1)} %collective-permute-done.14.refs_2_, ...), custom_call_target="tpu_custom_call" | custom-call | flops 905969664 | bytes 5242880 | tf_op jit(solution)/shard_map/pallas_call | solution.py:67
  40.6 1.8 %collective-permute-start.11 = (bf16[64,128]{1,0:T(8,128)(2,1)S(1)}, bf16[64,128]{1,0:T(8,128)(2,1)S(1)}, u32[]{:S(2)}, u32[]{:S(2)}) collective-permute-start(bf16[64,128]{1,0:T(8,128)(2,1)S(1)} %get-tuple-element.39.refs_4_), channel_id=1, source_target_pairs={{0,2},{1,3},{2,0},{3,1},{4,6},{5,7},{6,4},{7,5},{8,10},{9,11},{10,... | collective-permute-start | bytes 49160 | tf_op jit(solution)/shard_map/ppermute | solution.py:32
  42.4 2.1 %shard_map.158 = (bf16[256,768]{1,0:T(8,128)(2,1)S(1)}, f32[128,256]{1,0:T(8,128)S(1)}) custom-call(s32[1]{0:T(128)} %bitcast.id_ref, bf16[1536,256]{1,0:T(8,128)(2,1)S(1)} %copy-done.2, bf16[128,1536]{1,0:T(8,128)(2,1)S(1)} %get-tuple-element.35.own_ref.refs_0_, bf16[192,768]{1,0:T(8,128)(2,1)S(1)} %copy-done.7, ...), custom_call_target="tpu_custom_call" | custom-call | flops 603979776 | bytes 3145728 | tf_op jit(solution)/shard_map/pallas_call | solution.py:67
  44.5 10.1 %collective-permute-done.11.refs_6_ = bf16[64,128]{1,0:T(8,128)(2,1)S(1)} collective-permute-done((bf16[64,128]{1,0:T(8,128)(2,1)S(1)}, bf16[64,128]{1,0:T(8,128)(2,1)S(1)}, u32[]{:S(2)}, u32[]{:S(2)}) %collective-permute-start.11) | collective-permute-done | bytes 16416 | tf_op jit(solution)/shard_map/ppermute | solution.py:32
  54.6 3.2 %shard_map.161 = (bf16[512,768]{1,0:T(8,128)(2,1)S(1)}, bf16[272,256]{1,0:T(8,128)(2,1)S(1)}, bf16[272,256]{1,0:T(8,128)(2,1)S(1)}, bf16[272,256]{1,0:T(8,128)(2,1)S(1)}, bf16[272,256]{1,0:T(8,128)(2,1)S(1)}) custom-call(s32[1]{0:T(128)} %bitcast.id_ref, bf16[512,1536]{1,0:T(8,128)(2,1)S(1)} %get-tuple-element.36.x_ref, ...), custom_call_target="tpu_custom_call" | custom-call | flops 503316480 | bytes 5242880 | tf_op jit(solution)/shard_map/pallas_call | solution.py:67
  58.0 1.7 %collective-permute-start.24 = (bf16[272,256]{1,0:T(8,128)(2,1)S(1)}, bf16[272,256]{1,0:T(8,128)(2,1)S(1)}, u32[]{:S(2)}, u32[]{:S(2)}) collective-permute-start(bf16[272,256]{1,0:T(8,128)(2,1)S(1)} %get-tuple-element.48), channel_id=1, source_target_pairs={{0,2},{1,3},{2,0},{3,1},{4,6},{5,7},{6,4},{7,5},{8,10},{9,11},{10,... | collective-permute-start | bytes 417800 | tf_op jit(solution)/shard_map/ppermute | solution.py:32
  60.0 2.7 %shard_map.162 = (bf16[128,1536]{1,0:T(8,128)(2,1)S(1)}, bf16[128,1536]{1,0:T(8,128)(2,1)S(1)}, bf16[128,1536]{1,0:T(8,128)(2,1)S(1)}, bf16[128,1536]{1,0:T(8,128)(2,1)S(1)}) custom-call(s32[1]{0:T(128)} %bitcast.id_ref, bf16[512,768]{1,0:T(8,128)(2,1)S(1)} %get-tuple-element.40.hid_ref, bf16[192,768]{1,0:T(8,128)(2,1)S(1)} %copy-done.7, ...), custom_call_target="tpu_custom_call" | custom-call | flops 1207959552 | bytes 6291456 | tf_op jit(solution)/shard_map/pallas_call | solution.py:67
  62.7 1.6 %collective-permute-start.21 = (bf16[128,1536]{1,0:T(8,128)(2,1)S(1)}, bf16[128,1536]{1,0:T(8,128)(2,1)S(1)}, u32[]{:S(2)}, u32[]{:S(2)}) collective-permute-start(bf16[128,1536]{1,0:T(8,128)(2,1)S(1)} %get-tuple-element.44), channel_id=1, source_target_pairs={{0,1},{1,0},{2,3},{3,2},{4,5},{5,4},{6,7},{7,6},{8,9},{9,8},{10,11... | collective-permute-start | bytes 1179656 | tf_op jit(solution)/shard_map/ppermute | solution.py:32
  64.3 7.9 %collective-permute-done.24.refs_2_ = bf16[272,256]{1,0:T(8,128)(2,1)S(1)} collective-permute-done((bf16[272,256]{1,0:T(8,128)(2,1)S(1)}, bf16[272,256]{1,0:T(8,128)(2,1)S(1)}, u32[]{:S(2)}, u32[]{:S(2)}) %collective-permute-start.24) | collective-permute-done | bytes 139296 | tf_op jit(solution)/shard_map/ppermute | solution.py:32
  75.4 3.1 %collective-permute-done.27.low_ref = bf16[48,256]{1,0:T(8,128)(2,1)S(1)} collective-permute-done((bf16[48,256]{1,0:T(8,128)(2,1)S(1)}, bf16[48,256]{1,0:T(8,128)(2,1)S(1)}, u32[]{:S(2)}, u32[]{:S(2)}) %collective-permute-start.27) | collective-permute-done | bytes 24608 | tf_op jit(solution)/shard_map/ppermute | solution.py:32
  78.5 3.7 %shard_map.167 = (bf16[256,256]{1,0:T(8,128)(2,1)}, f32[4,256,256]{2,1,0:T(8,128)S(1)}, bf16[4,256,256]{2,1,0:T(8,128)(2,1)S(1)}) custom-call(s32[1]{0:T(128)} %bitcast.id_ref, bf16[256,256]{1,0:T(8,128)(2,1)S(1)} %get-tuple-element.50.field_ref, bf16[16,256]{1,0:T(8,128)(2,1)S(1)} %get-tuple-element.51.side_ref, ...), custom_call_target="tpu_custom_call" | custom-call | flops 536870912 | bytes 5242880 | tf_op jit(solution)/shard_map/pallas_call | solution.py:67
  82.2 2.6 %collective-permute-start.28 = (bf16[4,256,256]{2,1,0:T(8,128)(2,1)S(1)}, bf16[4,256,256]{2,1,0:T(8,128)(2,1)S(1)}, u32[]{:S(2)}, u32[]{:S(2)}) collective-permute-start(bf16[4,256,256]{2,1,0:T(8,128)(2,1)S(1)} %get-tuple-element.58), channel_id=1, source_target_pairs={{0,4},{1,5},{2,6},{3,7},{4,0},{5,1},{6,2},{7,3},{8,12},{9,13},{10,... | collective-permute-start | bytes 1572872 | tf_op jit(solution)/shard_map/ppermute | solution.py:32
  84.8 1.6 %collective-permute-start.22 = (bf16[128,1536]{1,0:T(8,128)(2,1)S(1)}, bf16[128,1536]{1,0:T(8,128)(2,1)S(1)}, u32[]{:S(2)}, u32[]{:S(2)}) collective-permute-start(bf16[128,1536]{1,0:T(8,128)(2,1)S(1)} %shard_map.163), channel_id=1, source_target_pairs={{0,2},{1,3},{2,0},{3,1},{4,6},{5,7},{6,4},{7,5},{8,10},{9,11},{10,... | collective-permute-start | bytes 1179656 | tf_op jit(solution)/shard_map/ppermute | solution.py:32
  86.5 1.4 %collective-permute-start.29 = (bf16[256,256]{1,0:T(8,128)(2,1)S(1)}, bf16[256,256]{1,0:T(8,128)(2,1)S(1)}, u32[]{:S(2)}, u32[]{:S(2)}) collective-permute-start(bf16[256,256]{1,0:T(8,128)(2,1)S(1)} %get-tuple-element.60), channel_id=1, source_target_pairs={{0,8},{1,9},{2,10},{3,11},{4,12},{5,13},{6,14},{7,15},{8,0},{9,1},... | collective-permute-start | bytes 393224 | tf_op jit(solution)/shard_map/ppermute | solution.py:32
  87.9 2.1 %collective-permute-start.31 = (bf16[256,256]{1,0:T(8,128)(2,1)S(1)}, bf16[256,256]{1,0:T(8,128)(2,1)S(1)}, u32[]{:S(2)}, u32[]{:S(2)}) collective-permute-start(bf16[256,256]{1,0:T(8,128)(2,1)S(1)} %get-tuple-element.62), channel_id=1, source_target_pairs={{0,24},{1,25},{2,26},{3,27},{4,28},{5,29},{6,30},{7,31},{8,16},{9,... | collective-permute-start | bytes 393224 | tf_op jit(solution)/shard_map/ppermute | solution.py:32
  90.0 2.7 %collective-permute-done.29.a_ref = bf16[256,256]{1,0:T(8,128)(2,1)S(1)} collective-permute-done((bf16[256,256]{1,0:T(8,128)(2,1)S(1)}, bf16[256,256]{1,0:T(8,128)(2,1)S(1)}, u32[]{:S(2)}, u32[]{:S(2)}) %collective-permute-start.29) | collective-permute-done | bytes 131104 | tf_op jit(solution)/shard_map/ppermute | solution.py:32
  92.7 3.4 %collective-permute-done.30.b_ref = bf16[256,256]{1,0:T(8,128)(2,1)S(1)} collective-permute-done((bf16[256,256]{1,0:T(8,128)(2,1)S(1)}, bf16[256,256]{1,0:T(8,128)(2,1)S(1)}, u32[]{:S(2)}, u32[]{:S(2)}) %collective-permute-start.30) | collective-permute-done | bytes 131104 | tf_op jit(solution)/shard_map/ppermute | solution.py:32
  96.2 2.1 %collective-permute-start.32 = (bf16[64,256]{1,0:T(8,128)(2,1)S(1)}, bf16[64,256]{1,0:T(8,128)(2,1)S(1)}, u32[]{:S(2)}, u32[]{:S(2)}) collective-permute-start(bf16[64,256]{1,0:T(8,128)(2,1)S(1)} %get-tuple-element.64), channel_id=1, source_target_pairs={{0,3},{1,0},{2,1},{3,2},{4,7},{5,4},{6,5},{7,6},{8,11},{9,8},{10,9... | collective-permute-start | bytes 98312 | tf_op jit(solution)/shard_map/ppermute | solution.py:32
  99.8 4.7 %collective-permute-done.20.refs_2_ = bf16[128,1536]{1,0:T(8,128)(2,1)S(1)} collective-permute-done((bf16[128,1536]{1,0:T(8,128)(2,1)S(1)}, bf16[128,1536]{1,0:T(8,128)(2,1)S(1)}, u32[]{:S(2)}, u32[]{:S(2)}) %collective-permute-start.20) | collective-permute-done | bytes 393248 | tf_op jit(solution)/shard_map/ppermute | solution.py:32
  105.6 2.5 %collective-permute-done.33.refs_2_ = bf16[64,256]{1,0:T(8,128)(2,1)S(1)} collective-permute-done((bf16[64,256]{1,0:T(8,128)(2,1)S(1)}, bf16[64,256]{1,0:T(8,128)(2,1)S(1)}, u32[]{:S(2)}, u32[]{:S(2)}) %collective-permute-start.33) | collective-permute-done | bytes 32800 | tf_op jit(solution)/shard_map/ppermute | solution.py:32
  (82 shorter events, 13.6 us)
Async XLA Ops:
  0.6 17.7 %collective-permute-start.3 = (bf16[192,768]{1,0:T(8,128)(2,1)}, bf16[192,768]{1,0:T(8,128)(2,1)S(1)}, u32[]{:S(2)}, u32[]{:S(2)}) collective-permute-start(bf16[192,768]{1,0:T(8,128)(2,1)} %refs_0_.5), channel_id=1, source_target_pairs={{0,16},{1,17},{2,18},{3,19},{4,20},{5,21},{6,22},{7,23},{8,24},{9,... | collective-permute-start | bytes 884744 | tf_op jit(solution)/shard_map/ppermute | solution.py:32
  3.7 14.7 %collective-permute-start.1 = (bf16[192,768]{1,0:T(8,128)(2,1)}, bf16[192,768]{1,0:T(8,128)(2,1)S(1)}, u32[]{:S(2)}, u32[]{:S(2)}) collective-permute-start(bf16[192,768]{1,0:T(8,128)(2,1)} %refs_0_.5), channel_id=1, source_target_pairs={{0,8},{1,9},{2,10},{3,11},{4,12},{5,13},{6,14},{7,15},{8,0},{9,1},... | collective-permute-start | bytes 884744 | tf_op jit(solution)/shard_map/ppermute | solution.py:32
  5.2 14.9 %collective-permute-start = (bf16[192,768]{1,0:T(8,128)(2,1)}, bf16[192,768]{1,0:T(8,128)(2,1)S(1)}, u32[]{:S(2)}, u32[]{:S(2)}) collective-permute-start(bf16[192,768]{1,0:T(8,128)(2,1)} %refs_0_.5), channel_id=1, source_target_pairs={{0,4},{1,5},{2,6},{3,7},{4,0},{5,1},{6,2},{7,3},{8,12},{9,13},{10,... | collective-permute-start | bytes 884744 | tf_op jit(solution)/shard_map/ppermute | solution.py:32
  5.2 15.1 %collective-permute-start.14 = (bf16[192,768]{1,0:T(8,128)(2,1)}, bf16[192,768]{1,0:T(8,128)(2,1)S(1)}, u32[]{:S(2)}, u32[]{:S(2)}) collective-permute-start(bf16[192,768]{1,0:T(8,128)(2,1)} %refs_0_.4), channel_id=1, source_target_pairs={{0,8},{1,9},{2,10},{3,11},{4,12},{5,13},{6,14},{7,15},{8,0},{9,1},... | collective-permute-start | bytes 884744 | tf_op jit(solution)/shard_map/ppermute | solution.py:32
  8.7 5.6 %collective-permute-start.10 = (bf16[64,128]{1,0:T(8,128)(2,1)S(1)}, bf16[64,128]{1,0:T(8,128)(2,1)S(1)}, u32[]{:S(2)}, u32[]{:S(2)}) collective-permute-start(bf16[64,128]{1,0:T(8,128)(2,1)S(1)} %get-tuple-element.39.refs_4_), channel_id=1, source_target_pairs={{0,1},{1,2},{2,3},{3,0},{4,5},{5,6},{6,7},{7,4},{8,9},{9,10},{10,1... | collective-permute-start | bytes 49160 | tf_op jit(solution)/shard_map/ppermute | solution.py:32
  18.1 9.6 %collective-permute-start.16 = (bf16[192,768]{1,0:T(8,128)(2,1)}, bf16[192,768]{1,0:T(8,128)(2,1)S(1)}, u32[]{:S(2)}, u32[]{:S(2)}) collective-permute-start(bf16[192,768]{1,0:T(8,128)(2,1)} %refs_0_.4), channel_id=1, source_target_pairs={{0,16},{1,17},{2,18},{3,19},{4,20},{5,21},{6,22},{7,23},{8,24},{9,... | collective-permute-start | bytes 884744 | tf_op jit(solution)/shard_map/ppermute | solution.py:32
  18.3 9.3 %collective-permute-start.13 = (bf16[192,768]{1,0:T(8,128)(2,1)}, bf16[192,768]{1,0:T(8,128)(2,1)S(1)}, u32[]{:S(2)}, u32[]{:S(2)}) collective-permute-start(bf16[192,768]{1,0:T(8,128)(2,1)} %refs_0_.4), channel_id=1, source_target_pairs={{0,4},{1,5},{2,6},{3,7},{4,0},{5,1},{6,2},{7,3},{8,12},{9,13},{10,... | collective-permute-start | bytes 884744 | tf_op jit(solution)/shard_map/ppermute | solution.py:32
  18.4 9.8 %collective-permute-start.5 = (bf16[192,768]{1,0:T(8,128)(2,1)S(1)}, bf16[192,768]{1,0:T(8,128)(2,1)S(1)}, u32[]{:S(2)}, u32[]{:S(2)}) collective-permute-start(bf16[192,768]{1,0:T(8,128)(2,1)S(1)} %collective-permute-done.3.refs_4_), channel_id=1, source_target_pairs={{0,8},{1,9},{2,10},{3,11},{4,12},{5,13},{6,14},{7,15},{8,0},{9,1},... | collective-permute-start | bytes 884744 | tf_op jit(solution)/shard_map/ppermute | solution.py:32
  20.1 8.1 %collective-permute-start.4 = (bf16[192,768]{1,0:T(8,128)(2,1)S(1)}, bf16[192,768]{1,0:T(8,128)(2,1)S(1)}, u32[]{:S(2)}, u32[]{:S(2)}) collective-permute-start(bf16[192,768]{1,0:T(8,128)(2,1)S(1)} %collective-permute-done.3.refs_4_), channel_id=1, source_target_pairs={{0,4},{1,5},{2,6},{3,7},{4,0},{5,1},{6,2},{7,3},{8,12},{9,13},{10,... | collective-permute-start | bytes 884744 | tf_op jit(solution)/shard_map/ppermute | solution.py:32
  20.3 11.6 %collective-permute-start.18 = (bf16[192,768]{1,0:T(8,128)(2,1)S(1)}, bf16[192,768]{1,0:T(8,128)(2,1)}, u32[]{:S(2)}, u32[]{:S(2)}) collective-permute-start(bf16[192,768]{1,0:T(8,128)(2,1)S(1)} %collective-permute-done.14.refs_2_), channel_id=1, source_target_pairs={{0,16},{1,17},{2,18},{3,19},{4,20},{5,21},{6,22},{7,23},{8,24},{9,... | collective-permute-start | bytes 884744 | tf_op jit(solution)/shard_map/ppermute | solution.py:32
  27.7 4.2 %collective-permute-start.15 = (bf16[192,768]{1,0:T(8,128)(2,1)S(1)}, bf16[192,768]{1,0:T(8,128)(2,1)S(1)}, u32[]{:S(2)}, u32[]{:S(2)}) collective-permute-start(bf16[192,768]{1,0:T(8,128)(2,1)S(1)} %collective-permute-done.14.refs_2_), channel_id=1, source_target_pairs={{0,4},{1,5},{2,6},{3,7},{4,0},{5,1},{6,2},{7,3},{8,12},{9,13},{10,... | collective-permute-start | bytes 884744 | tf_op jit(solution)/shard_map/ppermute | solution.py:32
  28.2 7.8 %collective-permute-start.17 = (bf16[192,768]{1,0:T(8,128)(2,1)S(1)}, bf16[192,768]{1,0:T(8,128)(2,1)S(1)}, u32[]{:S(2)}, u32[]{:S(2)}) collective-permute-start(bf16[192,768]{1,0:T(8,128)(2,1)S(1)} %collective-permute-done.16.refs_4_), channel_id=1, source_target_pairs={{0,4},{1,5},{2,6},{3,7},{4,0},{5,1},{6,2},{7,3},{8,12},{9,13},{10,... | collective-permute-start | bytes 884744 | tf_op jit(solution)/shard_map/ppermute | solution.py:32
  28.3 12.3 %collective-permute-start.6 = (bf16[192,768]{1,0:T(8,128)(2,1)S(1)}, bf16[192,768]{1,0:T(8,128)(2,1)}, u32[]{:S(2)}, u32[]{:S(2)}) collective-permute-start(bf16[192,768]{1,0:T(8,128)(2,1)S(1)} %collective-permute-done.5.refs_6_), channel_id=1, source_target_pairs={{0,4},{1,5},{2,6},{3,7},{4,0},{5,1},{6,2},{7,3},{8,12},{9,13},{10,... | collective-permute-start | bytes 884744 | tf_op jit(solution)/shard_map/ppermute | solution.py:32
  31.9 22.7 %collective-permute-start.19 = (bf16[192,768]{1,0:T(8,128)(2,1)}, bf16[192,768]{1,0:T(8,128)(2,1)}, u32[]{:S(2)}, u32[]{:S(2)}) collective-permute-start(bf16[192,768]{1,0:T(8,128)(2,1)} %collective-permute-done.18.refs_9_), channel_id=1, source_target_pairs={{0,4},{1,5},{2,6},{3,7},{4,0},{5,1},{6,2},{7,3},{8,12},{9,13},{10,... | collective-permute-start | bytes 884744 | tf_op jit(solution)/shard_map/ppermute | solution.py:32
  31.9 22.7 %collective-permute-start.7 = (bf16[6,128,128]{2,1,0:T(8,128)(2,1)}, bf16[6,128,128]{2,1,0:T(8,128)(2,1)}, u32[]{:S(2)}, u32[]{:S(2)}) collective-permute-start(bf16[6,128,128]{2,1,0:T(8,128)(2,1)} %bitcast.7), channel_id=1, source_target_pairs={{0,1},{1,2},{2,3},{3,0},{4,5},{5,6},{6,7},{7,4},{8,9},{9,10},{10,1... | collective-permute-start | bytes 589832 | tf_op jit(solution)/shard_map/ppermute | solution.py:32
  31.9 22.7 %collective-permute-start.8 = (bf16[6,128,128]{2,1,0:T(8,128)(2,1)}, bf16[6,128,128]{2,1,0:T(8,128)(2,1)}, u32[]{:S(2)}, u32[]{:S(2)}) collective-permute-start(bf16[6,128,128]{2,1,0:T(8,128)(2,1)} %bitcast.8), channel_id=1, source_target_pairs={{0,2},{1,3},{2,0},{3,1},{4,6},{5,7},{6,4},{7,5},{8,10},{9,11},{10,... | collective-permute-start | bytes 589832 | tf_op jit(solution)/shard_map/ppermute | solution.py:32
  36.0 18.6 %collective-permute-start.9 = (bf16[6,128,128]{2,1,0:T(8,128)(2,1)}, bf16[6,128,128]{2,1,0:T(8,128)(2,1)}, u32[]{:S(2)}, u32[]{:S(2)}) collective-permute-start(bf16[6,128,128]{2,1,0:T(8,128)(2,1)} %bitcast.9), channel_id=1, source_target_pairs={{0,3},{1,0},{2,1},{3,2},{4,7},{5,4},{6,5},{7,6},{8,11},{9,8},{10,9... | collective-permute-start | bytes 589832 | tf_op jit(solution)/shard_map/ppermute | solution.py:32
  40.6 14.0 %collective-permute-start.11 = (bf16[64,128]{1,0:T(8,128)(2,1)S(1)}, bf16[64,128]{1,0:T(8,128)(2,1)S(1)}, u32[]{:S(2)}, u32[]{:S(2)}) collective-permute-start(bf16[64,128]{1,0:T(8,128)(2,1)S(1)} %get-tuple-element.39.refs_4_), channel_id=1, source_target_pairs={{0,2},{1,3},{2,0},{3,1},{4,6},{5,7},{6,4},{7,5},{8,10},{9,11},{10,... | collective-permute-start | bytes 49160 | tf_op jit(solution)/shard_map/ppermute | solution.py:32
  57.9 6.5 %collective-permute-start.23 = (bf16[272,256]{1,0:T(8,128)(2,1)S(1)}, bf16[272,256]{1,0:T(8,128)(2,1)S(1)}, u32[]{:S(2)}, u32[]{:S(2)}) collective-permute-start(bf16[272,256]{1,0:T(8,128)(2,1)S(1)} %get-tuple-element.47), channel_id=1, source_target_pairs={{0,3},{1,0},{2,1},{3,2},{4,7},{5,4},{6,5},{7,6},{8,11},{9,8},{10,9... | collective-permute-start | bytes 417800 | tf_op jit(solution)/shard_map/ppermute | solution.py:32
  58.0 14.2 %collective-permute-start.24 = (bf16[272,256]{1,0:T(8,128)(2,1)S(1)}, bf16[272,256]{1,0:T(8,128)(2,1)S(1)}, u32[]{:S(2)}, u32[]{:S(2)}) collective-permute-start(bf16[272,256]{1,0:T(8,128)(2,1)S(1)} %get-tuple-element.48), channel_id=1, source_target_pairs={{0,2},{1,3},{2,0},{3,1},{4,6},{5,7},{6,4},{7,5},{8,10},{9,11},{10,... | collective-permute-start | bytes 417800 | tf_op jit(solution)/shard_map/ppermute | solution.py:32
  59.7 12.5 %collective-permute-start.25 = (bf16[272,256]{1,0:T(8,128)(2,1)S(1)}, bf16[272,256]{1,0:T(8,128)(2,1)S(1)}, u32[]{:S(2)}, u32[]{:S(2)}) collective-permute-start(bf16[272,256]{1,0:T(8,128)(2,1)S(1)} %get-tuple-element.49), channel_id=1, source_target_pairs={{0,1},{1,2},{2,3},{3,0},{4,5},{5,6},{6,7},{7,4},{8,9},{9,10},{10,1... | collective-permute-start | bytes 417800 | tf_op jit(solution)/shard_map/ppermute | solution.py:32
  62.7 22.0 %collective-permute-start.21 = (bf16[128,1536]{1,0:T(8,128)(2,1)S(1)}, bf16[128,1536]{1,0:T(8,128)(2,1)S(1)}, u32[]{:S(2)}, u32[]{:S(2)}) collective-permute-start(bf16[128,1536]{1,0:T(8,128)(2,1)S(1)} %get-tuple-element.44), channel_id=1, source_target_pairs={{0,1},{1,0},{2,3},{3,2},{4,5},{5,4},{6,7},{7,6},{8,9},{9,8},{10,11... | collective-permute-start | bytes 1179656 | tf_op jit(solution)/shard_map/ppermute | solution.py:32
  73.7 4.8 %collective-permute-start.27 = (bf16[48,256]{1,0:T(8,128)(2,1)S(1)}, bf16[48,256]{1,0:T(8,128)(2,1)S(1)}, u32[]{:S(2)}, u32[]{:S(2)}) collective-permute-start(bf16[48,256]{1,0:T(8,128)(2,1)S(1)} %get-tuple-element.53), channel_id=1, source_target_pairs={{4,0},{5,1},{6,2},{7,3},{8,4},{9,5},{10,6},{11,7},{12,8},{13,9},{1... | collective-permute-start | bytes 73736 | tf_op jit(solution)/shard_map/ppermute | solution.py:32
  82.2 4.2 %collective-permute-start.28 = (bf16[4,256,256]{2,1,0:T(8,128)(2,1)S(1)}, bf16[4,256,256]{2,1,0:T(8,128)(2,1)S(1)}, u32[]{:S(2)}, u32[]{:S(2)}) collective-permute-start(bf16[4,256,256]{2,1,0:T(8,128)(2,1)S(1)} %get-tuple-element.58), channel_id=1, source_target_pairs={{0,4},{1,5},{2,6},{3,7},{4,0},{5,1},{6,2},{7,3},{8,12},{9,13},{10,... | collective-permute-start | bytes 1572872 | tf_op jit(solution)/shard_map/ppermute | solution.py:32
  84.7 19.8 %collective-permute-start.20 = (bf16[128,1536]{1,0:T(8,128)(2,1)S(1)}, bf16[128,1536]{1,0:T(8,128)(2,1)S(1)}, u32[]{:S(2)}, u32[]{:S(2)}) collective-permute-start(bf16[128,1536]{1,0:T(8,128)(2,1)S(1)} %get-tuple-element.42), channel_id=1, source_target_pairs={{0,1},{1,0},{2,3},{3,2},{4,5},{5,4},{6,7},{7,6},{8,9},{9,8},{10,11... | collective-permute-start | bytes 1179656 | tf_op jit(solution)/shard_map/ppermute | solution.py:32
  84.8 19.8 %collective-permute-start.22 = (bf16[128,1536]{1,0:T(8,128)(2,1)S(1)}, bf16[128,1536]{1,0:T(8,128)(2,1)S(1)}, u32[]{:S(2)}, u32[]{:S(2)}) collective-permute-start(bf16[128,1536]{1,0:T(8,128)(2,1)S(1)} %shard_map.163), channel_id=1, source_target_pairs={{0,2},{1,3},{2,0},{3,1},{4,6},{5,7},{6,4},{7,5},{8,10},{9,11},{10,... | collective-permute-start | bytes 1179656 | tf_op jit(solution)/shard_map/ppermute | solution.py:32
  86.5 6.2 %collective-permute-start.29 = (bf16[256,256]{1,0:T(8,128)(2,1)S(1)}, bf16[256,256]{1,0:T(8,128)(2,1)S(1)}, u32[]{:S(2)}, u32[]{:S(2)}) collective-permute-start(bf16[256,256]{1,0:T(8,128)(2,1)S(1)} %get-tuple-element.60), channel_id=1, source_target_pairs={{0,8},{1,9},{2,10},{3,11},{4,12},{5,13},{6,14},{7,15},{8,0},{9,1},... | collective-permute-start | bytes 393224 | tf_op jit(solution)/shard_map/ppermute | solution.py:32
  87.9 8.2 %collective-permute-start.30 = (bf16[256,256]{1,0:T(8,128)(2,1)S(1)}, bf16[256,256]{1,0:T(8,128)(2,1)S(1)}, u32[]{:S(2)}, u32[]{:S(2)}) collective-permute-start(bf16[256,256]{1,0:T(8,128)(2,1)S(1)} %get-tuple-element.61), channel_id=1, source_target_pairs={{0,16},{1,17},{2,18},{3,19},{4,20},{5,21},{6,22},{7,23},{8,24},{9,... | collective-permute-start | bytes 393224 | tf_op jit(solution)/shard_map/ppermute | solution.py:32
  87.9 8.2 %collective-permute-start.31 = (bf16[256,256]{1,0:T(8,128)(2,1)S(1)}, bf16[256,256]{1,0:T(8,128)(2,1)S(1)}, u32[]{:S(2)}, u32[]{:S(2)}) collective-permute-start(bf16[256,256]{1,0:T(8,128)(2,1)S(1)} %get-tuple-element.62), channel_id=1, source_target_pairs={{0,24},{1,25},{2,26},{3,27},{4,28},{5,29},{6,30},{7,31},{8,16},{9,... | collective-permute-start | bytes 393224 | tf_op jit(solution)/shard_map/ppermute | solution.py:32
  96.2 9.3 %collective-permute-start.32 = (bf16[64,256]{1,0:T(8,128)(2,1)S(1)}, bf16[64,256]{1,0:T(8,128)(2,1)S(1)}, u32[]{:S(2)}, u32[]{:S(2)}) collective-permute-start(bf16[64,256]{1,0:T(8,128)(2,1)S(1)} %get-tuple-element.64), channel_id=1, source_target_pairs={{0,3},{1,0},{2,1},{3,2},{4,7},{5,4},{6,5},{7,6},{8,11},{9,8},{10,9... | collective-permute-start | bytes 98312 | tf_op jit(solution)/shard_map/ppermute | solution.py:32
  98.4 9.7 %collective-permute-start.33 = (bf16[64,256]{1,0:T(8,128)(2,1)S(1)}, bf16[64,256]{1,0:T(8,128)(2,1)S(1)}, u32[]{:S(2)}, u32[]{:S(2)}) collective-permute-start(bf16[64,256]{1,0:T(8,128)(2,1)S(1)} %get-tuple-element.65), channel_id=1, source_target_pairs={{0,2},{1,3},{2,0},{3,1},{4,6},{5,7},{6,4},{7,5},{8,10},{9,11},{10,... | collective-permute-start | bytes 98312 | tf_op jit(solution)/shard_map/ppermute | solution.py:32
  99.0 9.1 %collective-permute-start.34 = (bf16[64,256]{1,0:T(8,128)(2,1)S(1)}, bf16[64,256]{1,0:T(8,128)(2,1)S(1)}, u32[]{:S(2)}, u32[]{:S(2)}) collective-permute-start(bf16[64,256]{1,0:T(8,128)(2,1)S(1)} %get-tuple-element.66), channel_id=1, source_target_pairs={{0,1},{1,2},{2,3},{3,0},{4,5},{5,6},{6,7},{7,4},{8,9},{9,10},{10,1... | collective-permute-start | bytes 98312 | tf_op jit(solution)/shard_map/ppermute | solution.py:32
  (18 other events, 124.9 us)

commit v3 on v2

--- a/solution.py
+++ b/solution.py
@@ -63,7 +63,7 @@
     return sorted(held.items())
 
 
-def call(body, outs, args, specs=None, scratch=(), flops=0, moved=0, tanhs=0, grant=20):
+def call(body, outs, args, specs=None, scratch=(), flops=0, moved=0, tanhs=0, grant=10):
     return pl.pallas_call(
         body,
         out_shape=[jax.ShapeDtypeStruct(*o) for o in outs],
@@ -314,7 +314,7 @@
     kern_ref, gain_ref, win_ref, wout_ref, *refs
 ):
     out_ref, refs = refs[0], refs[1:]
-    pad = refs[-1]
+    pad, sums = refs[-2:]
     cells, channels = field_ref.shape
     core = (id_ref[0] // depth) % 2
     at = 8
@@ -355,19 +355,12 @@
             lax.dot_general(act, dout, TN, preferred_element_type=f32),
         )
         for which, grad in enumerate(grads):
-            if not split:
-                refs[0][which * hid + c * step : which * hid + (c + 1) * step, :] = grad
-                continue
-            spot = 2 * which + c // 2
-
-            @pl.when(core == c % 2)
-            def _():
-                refs[0][spot] = grad
-
-            @pl.when(core != c % 2)
-            def _():
-                refs[1][spot] = grad.astype(bf16)
-
+            (sums if split else refs[0])[which * hid + c * step : which * hid + (c + 1) * step, :] = grad
+    if split:
+        for spot in range(4):
+            for ref, which in ((refs[0], core), (refs[1], 1 - core)):
+                start = pl.multiple_of((2 * spot + which) * step, step)
+                ref[spot] = sums[pl.ds(start, step), :].astype(ref.dtype)
     out_ref[...] = ((field_ref[...].astype(f32) + total) * wet).astype(bf16)
 
 
@@ -578,7 +571,10 @@
             ocean_w_out,
         ),
         specs=[SMEM] + [VMEM] * 11,
-        scratch=[pltpu.VMEM((tile_x + 2, tile_y + 16, channels), f32)],
+        scratch=[
+            pltpu.VMEM((tile_x + 2, tile_y + 16, channels), f32),
+            pltpu.VMEM((2 * hid, channels), f32),
+        ],
         flops=8 * cells * channels * hid,
         moved=5 * mb,
         tanhs=cells * hid,

time: 109 us -> 108 us (level)
  transfers between devices with their start and end apart: 35 -> 35, of which waited for: 12 -> 12; matrix products, arithmetic and copies ran while one was open for 0% -> 0% of each run, Pallas kernels for 12% -> 11%
where the time goes in v3:
time: 108 us
  waiting for transfers between devices  49.6 us (46%)
  starting transfers between devices  36.7 us (34%)
  Pallas kernels  16 us (15%)
  local copies, waits for them, and re-layouts  4.75 us (4%)
    ppermute x35, waiting for transfers between devices, send(): return lax.ppermute(value, ALL, pairs)  49.6 us
    ppermute x35, starting transfers between devices, send(): return lax.ppermute(value, ALL, pairs)  36.7 us
    pallas_call x14, Pallas kernels, call(): pl.pallas_call(body, out_shape=[jax.ShapeDtypeStruct(*o) for o in outs],...  16 us
    unnamed x30, local copies, waits for them, and re-layouts  4.75 us
  transfers between devices with their start and end apart: 35, of which 12 were waited for; matrix products, arithmetic and copies ran while one was open for 0% of the time, Pallas kernels for 11%

profile of v3, /device:TPU:0, one launch (start us, length us, event | category | flops | bytes accessed | tf_op | source)
XLA Modules:
  0.0 107.9 jit_solution(17315786253049567682)
XLA Ops:
  0.6 3.1 %collective-permute-start.3 = (bf16[192,768]{1,0:T(8,128)(2,1)}, bf16[192,768]{1,0:T(8,128)(2,1)S(1)}, u32[]{:S(2)}, u32[]{:S(2)}) collective-permute-start(bf16[192,768]{1,0:T(8,128)(2,1)} %refs_0_.5), channel_id=1, source_target_pairs={{0,16},{1,17},{2,18},{3,19},{4,20},{5,21},{6,22},{7,23},{8,24},{9,... | collective-permute-start | bytes 884744 | tf_op jit(solution)/shard_map/ppermute | solution.py:32
  3.7 1.5 %collective-permute-start.1 = (bf16[192,768]{1,0:T(8,128)(2,1)}, bf16[192,768]{1,0:T(8,128)(2,1)S(1)}, u32[]{:S(2)}, u32[]{:S(2)}) collective-permute-start(bf16[192,768]{1,0:T(8,128)(2,1)} %refs_0_.5), channel_id=1, source_target_pairs={{0,8},{1,9},{2,10},{3,11},{4,12},{5,13},{6,14},{7,15},{8,0},{9,1},... | collective-permute-start | bytes 884744 | tf_op jit(solution)/shard_map/ppermute | solution.py:32
  8.7 1.6 %collective-permute-start.10 = (bf16[64,128]{1,0:T(8,128)(2,1)S(1)}, bf16[64,128]{1,0:T(8,128)(2,1)S(1)}, u32[]{:S(2)}, u32[]{:S(2)}) collective-permute-start(bf16[64,128]{1,0:T(8,128)(2,1)S(1)} %get-tuple-element.39.refs_4_), channel_id=1, source_target_pairs={{0,1},{1,2},{2,3},{3,0},{4,5},{5,6},{6,7},{7,4},{8,9},{9,10},{10,1... | collective-permute-start | bytes 49160 | tf_op jit(solution)/shard_map/ppermute | solution.py:32
  10.4 4.0 %collective-permute-done.10.refs_5_.west_ref = bf16[64,128]{1,0:T(8,128)(2,1)S(1)} collective-permute-done((bf16[64,128]{1,0:T(8,128)(2,1)S(1)}, bf16[64,128]{1,0:T(8,128)(2,1)S(1)}, u32[]{:S(2)}, u32[]{:S(2)}) %collective-permute-start.10) | collective-permute-done | bytes 16416 | tf_op jit(solution)/shard_map/ppermute | solution.py:32
  14.3 1.8 %collective-permute-start.12 = (bf16[64,128]{1,0:T(8,128)(2,1)S(1)}, bf16[64,128]{1,0:T(8,128)(2,1)S(1)}, u32[]{:S(2)}, u32[]{:S(2)}) collective-permute-start(bf16[64,128]{1,0:T(8,128)(2,1)S(1)} %get-tuple-element.39.refs_4_), channel_id=1, source_target_pairs={{0,3},{1,0},{2,1},{3,2},{4,7},{5,4},{6,5},{7,6},{8,11},{9,8},{10,9... | collective-permute-start | bytes 49160 | tf_op jit(solution)/shard_map/ppermute | solution.py:32
  16.1 1.9 %collective-permute-done.12.refs_7_.east_ref = bf16[64,128]{1,0:T(8,128)(2,1)S(1)} collective-permute-done((bf16[64,128]{1,0:T(8,128)(2,1)S(1)}, bf16[64,128]{1,0:T(8,128)(2,1)S(1)}, u32[]{:S(2)}, u32[]{:S(2)}) %collective-permute-start.12) | collective-permute-done | bytes 16416 | tf_op jit(solution)/shard_map/ppermute | solution.py:32
  18.4 1.8 %collective-permute-start.5 = (bf16[192,768]{1,0:T(8,128)(2,1)S(1)}, bf16[192,768]{1,0:T(8,128)(2,1)S(1)}, u32[]{:S(2)}, u32[]{:S(2)}) collective-permute-start(bf16[192,768]{1,0:T(8,128)(2,1)S(1)} %collective-permute-done.3.refs_4_), channel_id=1, source_target_pairs={{0,8},{1,9},{2,10},{3,11},{4,12},{5,13},{6,14},{7,15},{8,0},{9,1},... | collective-permute-start | bytes 884744 | tf_op jit(solution)/shard_map/ppermute | solution.py:32
  20.3 1.5 %collective-permute-start.18 = (bf16[192,768]{1,0:T(8,128)(2,1)S(1)}, bf16[192,768]{1,0:T(8,128)(2,1)}, u32[]{:S(2)}, u32[]{:S(2)}) collective-permute-start(bf16[192,768]{1,0:T(8,128)(2,1)S(1)} %collective-permute-done.14.refs_2_), channel_id=1, source_target_pairs={{0,16},{1,17},{2,18},{3,19},{4,20},{5,21},{6,22},{7,23},{8,24},{9,... | collective-permute-start | bytes 884744 | tf_op jit(solution)/shard_map/ppermute | solution.py:32
  21.8 5.9 %collective-permute-done.16.refs_4_ = bf16[192,768]{1,0:T(8,128)(2,1)S(1)} collective-permute-done((bf16[192,768]{1,0:T(8,128)(2,1)}, bf16[192,768]{1,0:T(8,128)(2,1)S(1)}, u32[]{:S(2)}, u32[]{:S(2)}) %collective-permute-start.16) | collective-permute-done | bytes 294944 | tf_op jit(solution)/shard_map/ppermute | solution.py:32
  28.7 3.2 %collective-permute-done.18.refs_9_ = bf16[192,768]{1,0:T(8,128)(2,1)} collective-permute-done((bf16[192,768]{1,0:T(8,128)(2,1)S(1)}, bf16[192,768]{1,0:T(8,128)(2,1)}, u32[]{:S(2)}, u32[]{:S(2)}) %collective-permute-start.18) | collective-permute-done | bytes 294944 | tf_op jit(solution)/shard_map/ppermute | solution.py:32
  31.9 4.1 %collective-permute-start.8 = (bf16[6,128,128]{2,1,0:T(8,128)(2,1)}, bf16[6,128,128]{2,1,0:T(8,128)(2,1)}, u32[]{:S(2)}, u32[]{:S(2)}) collective-permute-start(bf16[6,128,128]{2,1,0:T(8,128)(2,1)} %bitcast.8), channel_id=1, source_target_pairs={{0,2},{1,3},{2,0},{3,1},{4,6},{5,7},{6,4},{7,5},{8,10},{9,11},{10,... | collective-permute-start | bytes 589832 | tf_op jit(solution)/shard_map/ppermute | solution.py:32
  36.0 1.4 %copy-done.1 = bf16[512,1536]{1,0:T(8,128)(2,1)S(1)} copy-done((bf16[512,1536]{1,0:T(8,128)(2,1)S(1)}, bf16[512,1536]{1,0:T(8,128)(2,1)}, u32[]{:S(2)}) %copy-start.1) | copy-done | bytes 1572888
  39.1 1.5 %shard_map.160.refs_8_ = f32[512,768]{1,0:T(8,128)S(1)} custom-call(s32[1]{0:T(128)} %bitcast.id_ref, bf16[512,1536]{1,0:T(8,128)(2,1)S(1)} %get-tuple-element.36.x_ref, bf16[192,768]{1,0:T(8,128)(2,1)S(1)} %copy-done.6, bf16[192,768]{1,0:T(8,128)(2,1)S(1)} %collective-permute-done.13.refs_1_, bf16[192,768]{1,0:T(8,128)(2,1)S(1)} %collective-permute-done.14.refs_2_, ...), custom_call_target="tpu_custom_call" | custom-call | flops 905969664 | bytes 5242880 | tf_op jit(solution)/shard_map/pallas_call | solution.py:67
  40.6 1.8 %collective-permute-start.11 = (bf16[64,128]{1,0:T(8,128)(2,1)S(1)}, bf16[64,128]{1,0:T(8,128)(2,1)S(1)}, u32[]{:S(2)}, u32[]{:S(2)}) collective-permute-start(bf16[64,128]{1,0:T(8,128)(2,1)S(1)} %get-tuple-element.39.refs_4_), channel_id=1, source_target_pairs={{0,2},{1,3},{2,0},{3,1},{4,6},{5,7},{6,4},{7,5},{8,10},{9,11},{10,... | collective-permute-start | bytes 49160 | tf_op jit(solution)/shard_map/ppermute | solution.py:32
  42.4 2.1 %shard_map.158 = (bf16[256,768]{1,0:T(8,128)(2,1)S(1)}, f32[128,256]{1,0:T(8,128)S(1)}) custom-call(s32[1]{0:T(128)} %bitcast.id_ref, bf16[1536,256]{1,0:T(8,128)(2,1)S(1)} %copy-done.2, bf16[128,1536]{1,0:T(8,128)(2,1)S(1)} %get-tuple-element.35.own_ref.refs_0_, bf16[192,768]{1,0:T(8,128)(2,1)S(1)} %copy-done.7, ...), custom_call_target="tpu_custom_call" | custom-call | flops 603979776 | bytes 3145728 | tf_op jit(solution)/shard_map/pallas_call | solution.py:67
  44.5 10.1 %collective-permute-done.11.refs_6_ = bf16[64,128]{1,0:T(8,128)(2,1)S(1)} collective-permute-done((bf16[64,128]{1,0:T(8,128)(2,1)S(1)}, bf16[64,128]{1,0:T(8,128)(2,1)S(1)}, u32[]{:S(2)}, u32[]{:S(2)}) %collective-permute-start.11) | collective-permute-done | bytes 16416 | tf_op jit(solution)/shard_map/ppermute | solution.py:32
  54.6 3.2 %shard_map.161 = (bf16[512,768]{1,0:T(8,128)(2,1)S(1)}, bf16[272,256]{1,0:T(8,128)(2,1)S(1)}, bf16[272,256]{1,0:T(8,128)(2,1)S(1)}, bf16[272,256]{1,0:T(8,128)(2,1)S(1)}, bf16[272,256]{1,0:T(8,128)(2,1)S(1)}) custom-call(s32[1]{0:T(128)} %bitcast.id_ref, bf16[512,1536]{1,0:T(8,128)(2,1)S(1)} %get-tuple-element.36.x_ref, ...), custom_call_target="tpu_custom_call" | custom-call | flops 503316480 | bytes 5242880 | tf_op jit(solution)/shard_map/pallas_call | solution.py:67
  58.0 1.7 %collective-permute-start.24 = (bf16[272,256]{1,0:T(8,128)(2,1)S(1)}, bf16[272,256]{1,0:T(8,128)(2,1)S(1)}, u32[]{:S(2)}, u32[]{:S(2)}) collective-permute-start(bf16[272,256]{1,0:T(8,128)(2,1)S(1)} %get-tuple-element.48), channel_id=1, source_target_pairs={{0,2},{1,3},{2,0},{3,1},{4,6},{5,7},{6,4},{7,5},{8,10},{9,11},{10,... | collective-permute-start | bytes 417800 | tf_op jit(solution)/shard_map/ppermute | solution.py:32
  60.0 2.7 %shard_map.162 = (bf16[128,1536]{1,0:T(8,128)(2,1)S(1)}, bf16[128,1536]{1,0:T(8,128)(2,1)S(1)}, bf16[128,1536]{1,0:T(8,128)(2,1)S(1)}, bf16[128,1536]{1,0:T(8,128)(2,1)S(1)}) custom-call(s32[1]{0:T(128)} %bitcast.id_ref, bf16[512,768]{1,0:T(8,128)(2,1)S(1)} %get-tuple-element.40.hid_ref, bf16[192,768]{1,0:T(8,128)(2,1)S(1)} %copy-done.7, ...), custom_call_target="tpu_custom_call" | custom-call | flops 1207959552 | bytes 6291456 | tf_op jit(solution)/shard_map/pallas_call | solution.py:67
  62.7 1.6 %collective-permute-start.21 = (bf16[128,1536]{1,0:T(8,128)(2,1)S(1)}, bf16[128,1536]{1,0:T(8,128)(2,1)S(1)}, u32[]{:S(2)}, u32[]{:S(2)}) collective-permute-start(bf16[128,1536]{1,0:T(8,128)(2,1)S(1)} %get-tuple-element.44), channel_id=1, source_target_pairs={{0,1},{1,0},{2,3},{3,2},{4,5},{5,4},{6,7},{7,6},{8,9},{9,8},{10,11... | collective-permute-start | bytes 1179656 | tf_op jit(solution)/shard_map/ppermute | solution.py:32
  64.3 7.9 %collective-permute-done.24.refs_2_ = bf16[272,256]{1,0:T(8,128)(2,1)S(1)} collective-permute-done((bf16[272,256]{1,0:T(8,128)(2,1)S(1)}, bf16[272,256]{1,0:T(8,128)(2,1)S(1)}, u32[]{:S(2)}, u32[]{:S(2)}) %collective-permute-start.24) | collective-permute-done | bytes 139296 | tf_op jit(solution)/shard_map/ppermute | solution.py:32
  75.4 3.1 %collective-permute-done.27.low_ref = bf16[48,256]{1,0:T(8,128)(2,1)S(1)} collective-permute-done((bf16[48,256]{1,0:T(8,128)(2,1)S(1)}, bf16[48,256]{1,0:T(8,128)(2,1)S(1)}, u32[]{:S(2)}, u32[]{:S(2)}) %collective-permute-start.27) | collective-permute-done | bytes 24608 | tf_op jit(solution)/shard_map/ppermute | solution.py:32
  78.5 2.8 %shard_map.167 = (bf16[256,256]{1,0:T(8,128)(2,1)}, f32[4,256,256]{2,1,0:T(8,128)S(1)}, bf16[4,256,256]{2,1,0:T(8,128)(2,1)S(1)}) custom-call(s32[1]{0:T(128)} %bitcast.id_ref, bf16[256,256]{1,0:T(8,128)(2,1)S(1)} %get-tuple-element.50.field_ref, bf16[16,256]{1,0:T(8,128)(2,1)S(1)} %get-tuple-element.51.side_ref, ...), custom_call_target="tpu_custom_call" | custom-call | flops 536870912 | bytes 5242880 | tf_op jit(solution)/shard_map/pallas_call | solution.py:67
  81.3 2.6 %collective-permute-start.28 = (bf16[4,256,256]{2,1,0:T(8,128)(2,1)S(1)}, bf16[4,256,256]{2,1,0:T(8,128)(2,1)S(1)}, u32[]{:S(2)}, u32[]{:S(2)}) collective-permute-start(bf16[4,256,256]{2,1,0:T(8,128)(2,1)S(1)} %get-tuple-element.58), channel_id=1, source_target_pairs={{0,4},{1,5},{2,6},{3,7},{4,0},{5,1},{6,2},{7,3},{8,12},{9,13},{10,... | collective-permute-start | bytes 1572872 | tf_op jit(solution)/shard_map/ppermute | solution.py:32
  84.0 1.6 %collective-permute-start.22 = (bf16[128,1536]{1,0:T(8,128)(2,1)S(1)}, bf16[128,1536]{1,0:T(8,128)(2,1)S(1)}, u32[]{:S(2)}, u32[]{:S(2)}) collective-permute-start(bf16[128,1536]{1,0:T(8,128)(2,1)S(1)} %shard_map.163), channel_id=1, source_target_pairs={{0,2},{1,3},{2,0},{3,1},{4,6},{5,7},{6,4},{7,5},{8,10},{9,11},{10,... | collective-permute-start | bytes 1179656 | tf_op jit(solution)/shard_map/ppermute | solution.py:32
  85.6 1.4 %collective-permute-start.29 = (bf16[256,256]{1,0:T(8,128)(2,1)S(1)}, bf16[256,256]{1,0:T(8,128)(2,1)S(1)}, u32[]{:S(2)}, u32[]{:S(2)}) collective-permute-start(bf16[256,256]{1,0:T(8,128)(2,1)S(1)} %get-tuple-element.60), channel_id=1, source_target_pairs={{0,8},{1,9},{2,10},{3,11},{4,12},{5,13},{6,14},{7,15},{8,0},{9,1},... | collective-permute-start | bytes 393224 | tf_op jit(solution)/shard_map/ppermute | solution.py:32
  87.1 2.1 %collective-permute-start.31 = (bf16[256,256]{1,0:T(8,128)(2,1)S(1)}, bf16[256,256]{1,0:T(8,128)(2,1)S(1)}, u32[]{:S(2)}, u32[]{:S(2)}) collective-permute-start(bf16[256,256]{1,0:T(8,128)(2,1)S(1)} %get-tuple-element.62), channel_id=1, source_target_pairs={{0,24},{1,25},{2,26},{3,27},{4,28},{5,29},{6,30},{7,31},{8,16},{9,... | collective-permute-start | bytes 393224 | tf_op jit(solution)/shard_map/ppermute | solution.py:32
  89.2 2.7 %collective-permute-done.29.a_ref = bf16[256,256]{1,0:T(8,128)(2,1)S(1)} collective-permute-done((bf16[256,256]{1,0:T(8,128)(2,1)S(1)}, bf16[256,256]{1,0:T(8,128)(2,1)S(1)}, u32[]{:S(2)}, u32[]{:S(2)}) %collective-permute-start.29) | collective-permute-done | bytes 131104 | tf_op jit(solution)/shard_map/ppermute | solution.py:32
  91.9 3.4 %collective-permute-done.30.b_ref = bf16[256,256]{1,0:T(8,128)(2,1)S(1)} collective-permute-done((bf16[256,256]{1,0:T(8,128)(2,1)S(1)}, bf16[256,256]{1,0:T(8,128)(2,1)S(1)}, u32[]{:S(2)}, u32[]{:S(2)}) %collective-permute-start.30) | collective-permute-done | bytes 131104 | tf_op jit(solution)/shard_map/ppermute | solution.py:32
  95.3 2.1 %collective-permute-start.32 = (bf16[64,256]{1,0:T(8,128)(2,1)S(1)}, bf16[64,256]{1,0:T(8,128)(2,1)S(1)}, u32[]{:S(2)}, u32[]{:S(2)}) collective-permute-start(bf16[64,256]{1,0:T(8,128)(2,1)S(1)} %get-tuple-element.64), channel_id=1, source_target_pairs={{0,3},{1,0},{2,1},{3,2},{4,7},{5,4},{6,5},{7,6},{8,11},{9,8},{10,9... | collective-permute-start | bytes 98312 | tf_op jit(solution)/shard_map/ppermute | solution.py:32
  98.9 4.7 %collective-permute-done.20.refs_2_ = bf16[128,1536]{1,0:T(8,128)(2,1)S(1)} collective-permute-done((bf16[128,1536]{1,0:T(8,128)(2,1)S(1)}, bf16[128,1536]{1,0:T(8,128)(2,1)S(1)}, u32[]{:S(2)}, u32[]{:S(2)}) %collective-permute-start.20) | collective-permute-done | bytes 393248 | tf_op jit(solution)/shard_map/ppermute | solution.py:32
  104.7 2.5 %collective-permute-done.33.refs_2_ = bf16[64,256]{1,0:T(8,128)(2,1)S(1)} collective-permute-done((bf16[64,256]{1,0:T(8,128)(2,1)S(1)}, bf16[64,256]{1,0:T(8,128)(2,1)S(1)}, u32[]{:S(2)}, u32[]{:S(2)}) %collective-permute-start.33) | collective-permute-done | bytes 32800 | tf_op jit(solution)/shard_map/ppermute | solution.py:32
  (82 shorter events, 13.6 us)
Async XLA Ops:
  0.6 17.7 %collective-permute-start.3 = (bf16[192,768]{1,0:T(8,128)(2,1)}, bf16[192,768]{1,0:T(8,128)(2,1)S(1)}, u32[]{:S(2)}, u32[]{:S(2)}) collective-permute-start(bf16[192,768]{1,0:T(8,128)(2,1)} %refs_0_.5), channel_id=1, source_target_pairs={{0,16},{1,17},{2,18},{3,19},{4,20},{5,21},{6,22},{7,23},{8,24},{9,... | collective-permute-start | bytes 884744 | tf_op jit(solution)/shard_map/ppermute | solution.py:32
  3.7 14.7 %collective-permute-start.1 = (bf16[192,768]{1,0:T(8,128)(2,1)}, bf16[192,768]{1,0:T(8,128)(2,1)S(1)}, u32[]{:S(2)}, u32[]{:S(2)}) collective-permute-start(bf16[192,768]{1,0:T(8,128)(2,1)} %refs_0_.5), channel_id=1, source_target_pairs={{0,8},{1,9},{2,10},{3,11},{4,12},{5,13},{6,14},{7,15},{8,0},{9,1},... | collective-permute-start | bytes 884744 | tf_op jit(solution)/shard_map/ppermute | solution.py:32
  5.2 14.9 %collective-permute-start = (bf16[192,768]{1,0:T(8,128)(2,1)}, bf16[192,768]{1,0:T(8,128)(2,1)S(1)}, u32[]{:S(2)}, u32[]{:S(2)}) collective-permute-start(bf16[192,768]{1,0:T(8,128)(2,1)} %refs_0_.5), channel_id=1, source_target_pairs={{0,4},{1,5},{2,6},{3,7},{4,0},{5,1},{6,2},{7,3},{8,12},{9,13},{10,... | collective-permute-start | bytes 884744 | tf_op jit(solution)/shard_map/ppermute | solution.py:32
  5.2 15.1 %collective-permute-start.14 = (bf16[192,768]{1,0:T(8,128)(2,1)}, bf16[192,768]{1,0:T(8,128)(2,1)S(1)}, u32[]{:S(2)}, u32[]{:S(2)}) collective-permute-start(bf16[192,768]{1,0:T(8,128)(2,1)} %refs_0_.4), channel_id=1, source_target_pairs={{0,8},{1,9},{2,10},{3,11},{4,12},{5,13},{6,14},{7,15},{8,0},{9,1},... | collective-permute-start | bytes 884744 | tf_op jit(solution)/shard_map/ppermute | solution.py:32
  8.7 5.6 %collective-permute-start.10 = (bf16[64,128]{1,0:T(8,128)(2,1)S(1)}, bf16[64,128]{1,0:T(8,128)(2,1)S(1)}, u32[]{:S(2)}, u32[]{:S(2)}) collective-permute-start(bf16[64,128]{1,0:T(8,128)(2,1)S(1)} %get-tuple-element.39.refs_4_), channel_id=1, source_target_pairs={{0,1},{1,2},{2,3},{3,0},{4,5},{5,6},{6,7},{7,4},{8,9},{9,10},{10,1... | collective-permute-start | bytes 49160 | tf_op jit(solution)/shard_map/ppermute | solution.py:32
  18.1 9.6 %collective-permute-start.16 = (bf16[192,768]{1,0:T(8,128)(2,1)}, bf16[192,768]{1,0:T(8,128)(2,1)S(1)}, u32[]{:S(2)}, u32[]{:S(2)}) collective-permute-start(bf16[192,768]{1,0:T(8,128)(2,1)} %refs_0_.4), channel_id=1, source_target_pairs={{0,16},{1,17},{2,18},{3,19},{4,20},{5,21},{6,22},{7,23},{8,24},{9,... | collective-permute-start | bytes 884744 | tf_op jit(solution)/shard_map/ppermute | solution.py:32
  18.3 9.3 %collective-permute-start.13 = (bf16[192,768]{1,0:T(8,128)(2,1)}, bf16[192,768]{1,0:T(8,128)(2,1)S(1)}, u32[]{:S(2)}, u32[]{:S(2)}) collective-permute-start(bf16[192,768]{1,0:T(8,128)(2,1)} %refs_0_.4), channel_id=1, source_target_pairs={{0,4},{1,5},{2,6},{3,7},{4,0},{5,1},{6,2},{7,3},{8,12},{9,13},{10,... | collective-permute-start | bytes 884744 | tf_op jit(solution)/shard_map/ppermute | solution.py:32
  18.4 9.8 %collective-permute-start.5 = (bf16[192,768]{1,0:T(8,128)(2,1)S(1)}, bf16[192,768]{1,0:T(8,128)(2,1)S(1)}, u32[]{:S(2)}, u32[]{:S(2)}) collective-permute-start(bf16[192,768]{1,0:T(8,128)(2,1)S(1)} %collective-permute-done.3.refs_4_), channel_id=1, source_target_pairs={{0,8},{1,9},{2,10},{3,11},{4,12},{5,13},{6,14},{7,15},{8,0},{9,1},... | collective-permute-start | bytes 884744 | tf_op jit(solution)/shard_map/ppermute | solution.py:32
  20.1 8.1 %collective-permute-start.4 = (bf16[192,768]{1,0:T(8,128)(2,1)S(1)}, bf16[192,768]{1,0:T(8,128)(2,1)S(1)}, u32[]{:S(2)}, u32[]{:S(2)}) collective-permute-start(bf16[192,768]{1,0:T(8,128)(2,1)S(1)} %collective-permute-done.3.refs_4_), channel_id=1, source_target_pairs={{0,4},{1,5},{2,6},{3,7},{4,0},{5,1},{6,2},{7,3},{8,12},{9,13},{10,... | collective-permute-start | bytes 884744 | tf_op jit(solution)/shard_map/ppermute | solution.py:32
  20.3 11.6 %collective-permute-start.18 = (bf16[192,768]{1,0:T(8,128)(2,1)S(1)}, bf16[192,768]{1,0:T(8,128)(2,1)}, u32[]{:S(2)}, u32[]{:S(2)}) collective-permute-start(bf16[192,768]{1,0:T(8,128)(2,1)S(1)} %collective-permute-done.14.refs_2_), channel_id=1, source_target_pairs={{0,16},{1,17},{2,18},{3,19},{4,20},{5,21},{6,22},{7,23},{8,24},{9,... | collective-permute-start | bytes 884744 | tf_op jit(solution)/shard_map/ppermute | solution.py:32
  27.7 4.2 %collective-permute-start.15 = (bf16[192,768]{1,0:T(8,128)(2,1)S(1)}, bf16[192,768]{1,0:T(8,128)(2,1)S(1)}, u32[]{:S(2)}, u32[]{:S(2)}) collective-permute-start(bf16[192,768]{1,0:T(8,128)(2,1)S(1)} %collective-permute-done.14.refs_2_), channel_id=1, source_target_pairs={{0,4},{1,5},{2,6},{3,7},{4,0},{5,1},{6,2},{7,3},{8,12},{9,13},{10,... | collective-permute-start | bytes 884744 | tf_op jit(solution)/shard_map/ppermute | solution.py:32
  28.2 7.8 %collective-permute-start.17 = (bf16[192,768]{1,0:T(8,128)(2,1)S(1)}, bf16[192,768]{1,0:T(8,128)(2,1)S(1)}, u32[]{:S(2)}, u32[]{:S(2)}) collective-permute-start(bf16[192,768]{1,0:T(8,128)(2,1)S(1)} %collective-permute-done.16.refs_4_), channel_id=1, source_target_pairs={{0,4},{1,5},{2,6},{3,7},{4,0},{5,1},{6,2},{7,3},{8,12},{9,13},{10,... | collective-permute-start | bytes 884744 | tf_op jit(solution)/shard_map/ppermute | solution.py:32
  28.3 12.3 %collective-permute-start.6 = (bf16[192,768]{1,0:T(8,128)(2,1)S(1)}, bf16[192,768]{1,0:T(8,128)(2,1)}, u32[]{:S(2)}, u32[]{:S(2)}) collective-permute-start(bf16[192,768]{1,0:T(8,128)(2,1)S(1)} %collective-permute-done.5.refs_6_), channel_id=1, source_target_pairs={{0,4},{1,5},{2,6},{3,7},{4,0},{5,1},{6,2},{7,3},{8,12},{9,13},{10,... | collective-permute-start | bytes 884744 | tf_op jit(solution)/shard_map/ppermute | solution.py:32
  31.9 22.7 %collective-permute-start.19 = (bf16[192,768]{1,0:T(8,128)(2,1)}, bf16[192,768]{1,0:T(8,128)(2,1)}, u32[]{:S(2)}, u32[]{:S(2)}) collective-permute-start(bf16[192,768]{1,0:T(8,128)(2,1)} %collective-permute-done.18.refs_9_), channel_id=1, source_target_pairs={{0,4},{1,5},{2,6},{3,7},{4,0},{5,1},{6,2},{7,3},{8,12},{9,13},{10,... | collective-permute-start | bytes 884744 | tf_op jit(solution)/shard_map/ppermute | solution.py:32
  31.9 22.7 %collective-permute-start.7 = (bf16[6,128,128]{2,1,0:T(8,128)(2,1)}, bf16[6,128,128]{2,1,0:T(8,128)(2,1)}, u32[]{:S(2)}, u32[]{:S(2)}) collective-permute-start(bf16[6,128,128]{2,1,0:T(8,128)(2,1)} %bitcast.7), channel_id=1, source_target_pairs={{0,1},{1,2},{2,3},{3,0},{4,5},{5,6},{6,7},{7,4},{8,9},{9,10},{10,1... | collective-permute-start | bytes 589832 | tf_op jit(solution)/shard_map/ppermute | solution.py:32
  31.9 22.7 %collective-permute-start.8 = (bf16[6,128,128]{2,1,0:T(8,128)(2,1)}, bf16[6,128,128]{2,1,0:T(8,128)(2,1)}, u32[]{:S(2)}, u32[]{:S(2)}) collective-permute-start(bf16[6,128,128]{2,1,0:T(8,128)(2,1)} %bitcast.8), channel_id=1, source_target_pairs={{0,2},{1,3},{2,0},{3,1},{4,6},{5,7},{6,4},{7,5},{8,10},{9,11},{10,... | collective-permute-start | bytes 589832 | tf_op jit(solution)/shard_map/ppermute | solution.py:32
  36.0 18.6 %collective-permute-start.9 = (bf16[6,128,128]{2,1,0:T(8,128)(2,1)}, bf16[6,128,128]{2,1,0:T(8,128)(2,1)}, u32[]{:S(2)}, u32[]{:S(2)}) collective-permute-start(bf16[6,128,128]{2,1,0:T(8,128)(2,1)} %bitcast.9), channel_id=1, source_target_pairs={{0,3},{1,0},{2,1},{3,2},{4,7},{5,4},{6,5},{7,6},{8,11},{9,8},{10,9... | collective-permute-start | bytes 589832 | tf_op jit(solution)/shard_map/ppermute | solution.py:32
  40.6 14.0 %collective-permute-start.11 = (bf16[64,128]{1,0:T(8,128)(2,1)S(1)}, bf16[64,128]{1,0:T(8,128)(2,1)S(1)}, u32[]{:S(2)}, u32[]{:S(2)}) collective-permute-start(bf16[64,128]{1,0:T(8,128)(2,1)S(1)} %get-tuple-element.39.refs_4_), channel_id=1, source_target_pairs={{0,2},{1,3},{2,0},{3,1},{4,6},{5,7},{6,4},{7,5},{8,10},{9,11},{10,... | collective-permute-start | bytes 49160 | tf_op jit(solution)/shard_map/ppermute | solution.py:32
  57.9 6.5 %collective-permute-start.23 = (bf16[272,256]{1,0:T(8,128)(2,1)S(1)}, bf16[272,256]{1,0:T(8,128)(2,1)S(1)}, u32[]{:S(2)}, u32[]{:S(2)}) collective-permute-start(bf16[272,256]{1,0:T(8,128)(2,1)S(1)} %get-tuple-element.47), channel_id=1, source_target_pairs={{0,3},{1,0},{2,1},{3,2},{4,7},{5,4},{6,5},{7,6},{8,11},{9,8},{10,9... | collective-permute-start | bytes 417800 | tf_op jit(solution)/shard_map/ppermute | solution.py:32
  58.0 14.2 %collective-permute-start.24 = (bf16[272,256]{1,0:T(8,128)(2,1)S(1)}, bf16[272,256]{1,0:T(8,128)(2,1)S(1)}, u32[]{:S(2)}, u32[]{:S(2)}) collective-permute-start(bf16[272,256]{1,0:T(8,128)(2,1)S(1)} %get-tuple-element.48), channel_id=1, source_target_pairs={{0,2},{1,3},{2,0},{3,1},{4,6},{5,7},{6,4},{7,5},{8,10},{9,11},{10,... | collective-permute-start | bytes 417800 | tf_op jit(solution)/shard_map/ppermute | solution.py:32
  59.7 12.5 %collective-permute-start.25 = (bf16[272,256]{1,0:T(8,128)(2,1)S(1)}, bf16[272,256]{1,0:T(8,128)(2,1)S(1)}, u32[]{:S(2)}, u32[]{:S(2)}) collective-permute-start(bf16[272,256]{1,0:T(8,128)(2,1)S(1)} %get-tuple-element.49), channel_id=1, source_target_pairs={{0,1},{1,2},{2,3},{3,0},{4,5},{5,6},{6,7},{7,4},{8,9},{9,10},{10,1... | collective-permute-start | bytes 417800 | tf_op jit(solution)/shard_map/ppermute | solution.py:32
  62.7 21.1 %collective-permute-start.21 = (bf16[128,1536]{1,0:T(8,128)(2,1)S(1)}, bf16[128,1536]{1,0:T(8,128)(2,1)S(1)}, u32[]{:S(2)}, u32[]{:S(2)}) collective-permute-start(bf16[128,1536]{1,0:T(8,128)(2,1)S(1)} %get-tuple-element.44), channel_id=1, source_target_pairs={{0,1},{1,0},{2,3},{3,2},{4,5},{5,4},{6,7},{7,6},{8,9},{9,8},{10,11... | collective-permute-start | bytes 1179656 | tf_op jit(solution)/shard_map/ppermute | solution.py:32
  73.7 4.8 %collective-permute-start.27 = (bf16[48,256]{1,0:T(8,128)(2,1)S(1)}, bf16[48,256]{1,0:T(8,128)(2,1)S(1)}, u32[]{:S(2)}, u32[]{:S(2)}) collective-permute-start(bf16[48,256]{1,0:T(8,128)(2,1)S(1)} %get-tuple-element.53), channel_id=1, source_target_pairs={{4,0},{5,1},{6,2},{7,3},{8,4},{9,5},{10,6},{11,7},{12,8},{13,9},{1... | collective-permute-start | bytes 73736 | tf_op jit(solution)/shard_map/ppermute | solution.py:32
  81.3 4.2 %collective-permute-start.28 = (bf16[4,256,256]{2,1,0:T(8,128)(2,1)S(1)}, bf16[4,256,256]{2,1,0:T(8,128)(2,1)S(1)}, u32[]{:S(2)}, u32[]{:S(2)}) collective-permute-start(bf16[4,256,256]{2,1,0:T(8,128)(2,1)S(1)} %get-tuple-element.58), channel_id=1, source_target_pairs={{0,4},{1,5},{2,6},{3,7},{4,0},{5,1},{6,2},{7,3},{8,12},{9,13},{10,... | collective-permute-start | bytes 1572872 | tf_op jit(solution)/shard_map/ppermute | solution.py:32
  83.9 19.8 %collective-permute-start.20 = (bf16[128,1536]{1,0:T(8,128)(2,1)S(1)}, bf16[128,1536]{1,0:T(8,128)(2,1)S(1)}, u32[]{:S(2)}, u32[]{:S(2)}) collective-permute-start(bf16[128,1536]{1,0:T(8,128)(2,1)S(1)} %get-tuple-element.42), channel_id=1, source_target_pairs={{0,1},{1,0},{2,3},{3,2},{4,5},{5,4},{6,7},{7,6},{8,9},{9,8},{10,11... | collective-permute-start | bytes 1179656 | tf_op jit(solution)/shard_map/ppermute | solution.py:32
  84.0 19.8 %collective-permute-start.22 = (bf16[128,1536]{1,0:T(8,128)(2,1)S(1)}, bf16[128,1536]{1,0:T(8,128)(2,1)S(1)}, u32[]{:S(2)}, u32[]{:S(2)}) collective-permute-start(bf16[128,1536]{1,0:T(8,128)(2,1)S(1)} %shard_map.163), channel_id=1, source_target_pairs={{0,2},{1,3},{2,0},{3,1},{4,6},{5,7},{6,4},{7,5},{8,10},{9,11},{10,... | collective-permute-start | bytes 1179656 | tf_op jit(solution)/shard_map/ppermute | solution.py:32
  85.6 6.2 %collective-permute-start.29 = (bf16[256,256]{1,0:T(8,128)(2,1)S(1)}, bf16[256,256]{1,0:T(8,128)(2,1)S(1)}, u32[]{:S(2)}, u32[]{:S(2)}) collective-permute-start(bf16[256,256]{1,0:T(8,128)(2,1)S(1)} %get-tuple-element.60), channel_id=1, source_target_pairs={{0,8},{1,9},{2,10},{3,11},{4,12},{5,13},{6,14},{7,15},{8,0},{9,1},... | collective-permute-start | bytes 393224 | tf_op jit(solution)/shard_map/ppermute | solution.py:32
  87.1 8.2 %collective-permute-start.30 = (bf16[256,256]{1,0:T(8,128)(2,1)S(1)}, bf16[256,256]{1,0:T(8,128)(2,1)S(1)}, u32[]{:S(2)}, u32[]{:S(2)}) collective-permute-start(bf16[256,256]{1,0:T(8,128)(2,1)S(1)} %get-tuple-element.61), channel_id=1, source_target_pairs={{0,16},{1,17},{2,18},{3,19},{4,20},{5,21},{6,22},{7,23},{8,24},{9,... | collective-permute-start | bytes 393224 | tf_op jit(solution)/shard_map/ppermute | solution.py:32
  87.1 8.2 %collective-permute-start.31 = (bf16[256,256]{1,0:T(8,128)(2,1)S(1)}, bf16[256,256]{1,0:T(8,128)(2,1)S(1)}, u32[]{:S(2)}, u32[]{:S(2)}) collective-permute-start(bf16[256,256]{1,0:T(8,128)(2,1)S(1)} %get-tuple-element.62), channel_id=1, source_target_pairs={{0,24},{1,25},{2,26},{3,27},{4,28},{5,29},{6,30},{7,31},{8,16},{9,... | collective-permute-start | bytes 393224 | tf_op jit(solution)/shard_map/ppermute | solution.py:32
  95.3 9.3 %collective-permute-start.32 = (bf16[64,256]{1,0:T(8,128)(2,1)S(1)}, bf16[64,256]{1,0:T(8,128)(2,1)S(1)}, u32[]{:S(2)}, u32[]{:S(2)}) collective-permute-start(bf16[64,256]{1,0:T(8,128)(2,1)S(1)} %get-tuple-element.64), channel_id=1, source_target_pairs={{0,3},{1,0},{2,1},{3,2},{4,7},{5,4},{6,5},{7,6},{8,11},{9,8},{10,9... | collective-permute-start | bytes 98312 | tf_op jit(solution)/shard_map/ppermute | solution.py:32
  97.5 9.7 %collective-permute-start.33 = (bf16[64,256]{1,0:T(8,128)(2,1)S(1)}, bf16[64,256]{1,0:T(8,128)(2,1)S(1)}, u32[]{:S(2)}, u32[]{:S(2)}) collective-permute-start(bf16[64,256]{1,0:T(8,128)(2,1)S(1)} %get-tuple-element.65), channel_id=1, source_target_pairs={{0,2},{1,3},{2,0},{3,1},{4,6},{5,7},{6,4},{7,5},{8,10},{9,11},{10,... | collective-permute-start | bytes 98312 | tf_op jit(solution)/shard_map/ppermute | solution.py:32
  98.1 9.1 %collective-permute-start.34 = (bf16[64,256]{1,0:T(8,128)(2,1)S(1)}, bf16[64,256]{1,0:T(8,128)(2,1)S(1)}, u32[]{:S(2)}, u32[]{:S(2)}) collective-permute-start(bf16[64,256]{1,0:T(8,128)(2,1)S(1)} %get-tuple-element.66), channel_id=1, source_target_pairs={{0,1},{1,2},{2,3},{3,0},{4,5},{5,6},{6,7},{7,4},{8,9},{9,10},{10,1... | collective-permute-start | bytes 98312 | tf_op jit(solution)/shard_map/ppermute | solution.py:32
  (18 other events, 124.9 us)
